TPU v7x, 32 devices: a whole 2x2x4 slice. The times are simulated.
32 devices in a mesh: seq: 8 (over z, y), rows: 4 (over x, core).
Axes of the slice: x: 2, y: 2, z: 4, core: 2. Of those that a mesh axis runs over, the one named last changes fastest.
Arguments:
- hidden: bfloat16 [4, 1024, 768], P('rows', 'seq'), may hold values from -6 to 6
- cotangent: bfloat16 [4, 1024, 768], P('rows', 'seq'), may hold values from -6 to 6
- segment_ids: int32 [4, 1024], P('rows', 'seq'), may hold values from 0 to 15, never falling along the last dimension, each value on 1 to 768 neighbouring positions
- timesteps: int32 [4, 16], P('rows'), may hold values from 0 to 4999
- qkv_weight: bfloat16 [768, 2304], replicated, may hold values from -0.21875 to 0.21875
- qv_bias: float32 [1536], replicated, may hold values from -3 to 3
- out_weight: bfloat16 [768, 768], replicated, may hold values from -1.75 to 1.75
- out_bias: float32 [768], replicated, may hold values from -3 to 3
- up_weight: bfloat16 [768, 3072], replicated, may hold values from -0.21875 to 0.21875
- up_bias: float32 [3072], replicated, may hold values from -3 to 3
- down_weight: bfloat16 [3072, 768], replicated, may hold values from -0.109375 to 0.109375
- down_bias: float32 [768], replicated, may hold values from -3 to 3
- norm_gain: float32 [2, 768], replicated, may hold values from 0.1 to 1.9
- norm_bias: float32 [2, 768], replicated, may hold values from -3 to 3
- time_weight: bfloat16 [768, 768], replicated, may hold values from -0.21875 to 0.21875
Outputs:
- result: bfloat16 [4, 1024, 768], P('rows', 'seq')
- input_grad: float32 [4, 1024, 768], P('rows', 'seq')
- grad_qkv_weight: float32 [768, 2304], P('seq')
- grad_qv_bias: float32 [1536], P('seq')
- grad_out_weight: float32 [768, 768], P('seq')
- grad_out_bias: float32 [768], P('seq')
- grad_up_weight: float32 [768, 3072], P('seq')
- grad_up_bias: float32 [3072], P('seq')
- grad_down_weight: float32 [3072, 768], P('seq')
- grad_down_bias: float32 [768], P('seq')
- grad_norm_gain: float32 [2, 768], P(None, 'seq')
- grad_norm_bias: float32 [2, 768], P(None, 'seq')
- grad_time_weight: float32 [768, 768], P('seq')
Inputs may be any that keep to these rules, and one draw needn't show every extreme that they name: `segment_ids`: along each row the ids never fall; each of the 16 documents covers 1 to 768 consecutive tokens, and one of each row covers exactly 768.
All inputs are finite; a program needn't handle non-finite values.
Results may differ from a plain program's by a relative error of at most 0.023.
Values may be sent and summed in bfloat16 or wider, within the bound.
No kernel may reach another device: no remote copies, remote signals or barrier semaphores. Data moves between devices by JAX's collectives and lax.ppermute only.
A program may use at most 192 MiB of HBM per device.

v0:
```python
import functools
import math

import jax
import jax.numpy as jnp
from jax import lax
from jax.experimental import pallas as pl
from jax.experimental.pallas import tpu as pltpu
from jax.sharding import PartitionSpec as P

D = 768
H = 12
HD = 64
FF = 3072
DOCS = 16
PAIR = 2 * HD
PAIRS = D // PAIR
Z_STEPS = 4
SUMS = 16

EPS = 1e-05
MASKED = -1e30
BF = jnp.bfloat16
F32 = jnp.float32
precise = lax.Precision.HIGHEST
VMEM = pl.BlockSpec(memory_space=pltpu.VMEM)


def swap(block, axis, bit):
    return lax.ppermute(block, axis, [(i, i ^ bit) for i in range(lax.axis_size(axis))])


def dot(a, b, dims):
    return lax.dot_general(a, b, (dims, ((), ())), preferred_element_type=F32)


def nn(a, b):
    return dot(a, b, ((1,), (0,)))


def nt(a, b):
    return dot(a, b, ((1,), (1,)))


def tn(a, b):
    return dot(a, b, ((0,), (0,)))


APART = pl.BlockSpec(memory_space=pltpu.HBM)
FAR = "far"
NEAR = "near"


def far(value):
    return FAR, value


def call(kernel, name, ins, outs, scratch=(), vmem=8, copies=0):
    specs = [APART if isinstance(one, tuple) else VMEM for one in ins]
    values = [
        pltpu.with_memory_space_constraint(one[1], pltpu.HBM) if isinstance(one, tuple) else one
        for one in ins
    ]
    held = [pltpu.VMEM(*one) for one in scratch]
    if copies:
        held.append(pltpu.SemaphoreType.DMA((copies,)))
    return pl.pallas_call(
        kernel,
        out_shape=tuple(
            (pltpu.HBM if FAR in one else pltpu.VMEM)(*one[:2])
            if one[2:]
            else jax.ShapeDtypeStruct(*one)
            for one in outs
        ),
        in_specs=specs,
        out_specs=tuple(APART if FAR in one else VMEM for one in outs),
        scratch_shapes=held,
        compiler_params=pltpu.CompilerParams(vmem_limit_bytes=vmem << 20),
        cost_estimate=pl.CostEstimate(flops=int(COSTS[name] * 1e9), transcendentals=0, bytes_accessed=0),
        name=name,
    )(*values)


def copy(source, target, sems, at):
    moved = pltpu.make_async_copy(source, target, sems.at[at])
    moved.start()
    return moved


def copies(pairs, sems, first):
    return [copy(one, to, sems, first + at) for at, (one, to) in enumerate(pairs)]


def wait(moved):
    for one in moved:
        one.wait()


def loop(count, step):
    def body(at, carry):
        step(at)
        return carry

    lax.fori_loop(0, count, body, 0)


def at_rows(index, size):
    return pl.ds(pl.multiple_of(index * size, 8), size)


def at_lanes(index, size):
    return pl.ds(pl.multiple_of(index * size, 128), size)


def time_features(timesteps):
    half_width = D // 2
    frequency = jnp.exp(
        jnp.arange(half_width, dtype=F32) * (-math.log(10000.0) / half_width)
    )
    phases = timesteps.astype(F32)[..., None] * frequency
    return jnp.concatenate([jnp.sin(phases), jnp.cos(phases)], axis=-1)


def gather_seq(block, known, gate):
    size = lax.axis_size("seq")
    inner = size // Z_STEPS
    found = [None] * size
    found[0] = block
    for far in range(1, Z_STEPS):
        name = "Z%d" % far
        found[far * inner] = swap(gate(name, block), "seq", far * inner)
        known[name] = found[far * inner]
    for far in range(Z_STEPS):
        name = "Y%d" % far
        held = gate(name, found[far * inner])
        for near in range(1, inner):
            found[far * inner + near] = swap(held, "seq", near)
        known[name] = found[far * inner + inner - 1]
    return found


ORDER = {
    "fetch": ("Y0", ),
    "part": ("Z1", ),
    "feat": ("Y0", ),
    "Z3": ("Z1", ),
    "backward": ("forward", ),
    "head": ("heads", ),
    "Etwin": ("head", ),
    "headend": ("E", ),
    "half": ("hw", ),
    "all": ("GA2A", "in", ),
    "finh": ("AGF", ),
    "AGF": ("DOCS", ),
    "time": ("AGG", ),
}
COSTS = {
    "fetch": 7, "forward": 12, "backward": 5, "heads": 3, "part_weights": 3, "feed_grad": 8,
    "head_grad": 9, "head_weights": 2, "input_grad": 2, "combine": 1, "combine_half": 1,
    "combine_all": 1, "finish_all": 2, "finish_heads": 1, "time_grad": 1,
}


def split2(value):
    high = value.astype(BF)
    return high, (value - high.astype(F32)).astype(BF)


def split3(value):
    high = value.astype(BF)
    rest = value - high.astype(F32)
    middle = rest.astype(BF)
    low = (rest - middle.astype(F32)).astype(BF)
    return high, middle, low


def head_start(seq, share):
    return jnp.minimum(seq * share // HD, H - 2) * HD


def head_window(share):
    start = head_start(lax.axis_index("seq"), share)
    base = jnp.minimum(start // PAIR, PAIRS - 2) * PAIR
    return base, (2 * PAIR - (start - base)) % (2 * PAIR)


def normalize(value):
    centered = value - jnp.mean(value, axis=-1, keepdims=True)
    inverse = lax.rsqrt(jnp.mean(centered * centered, axis=-1, keepdims=True) + EPS)
    return centered * inverse, inverse


def normalize_back(z, inverse, grad):
    return inverse * (
        grad
        - jnp.mean(grad, axis=-1, keepdims=True)
        - z * jnp.mean(grad * z, axis=-1, keepdims=True)
    )


def total(value):
    return jnp.sum(value, axis=0, keepdims=True)


def gelu_parts(u):
    phi = 0.5 * (1.0 + lax.erf(u * math.sqrt(0.5)))
    return phi, phi + u * (jnp.exp(-0.5 * u * u) * (1.0 / math.sqrt(2.0 * math.pi)))


def fetch_kernel(*refs):
    count = (len(refs) - 1) // 2
    wait(copies(zip(refs[:count], refs[count:-1]), refs[-1], 0))


def forward_kernel(count, *refs):
    shards = refs[:count]
    embed_ref, qkv_ref, bias_ref, wo_ref, bo_ref, gain_ref, off_ref = refs[count : count + 7]
    cot_ref, up_ref, bu_ref, down_ref, bd_ref = refs[count + 7 : count + 12]
    refs = refs[count + 12 :]
    xlow_out, lse_ref, attn_ref, hot_ref, z1_ref, inverse_ref = refs[:6]
    result_ref, ydf_ref, dr2_ref, slope_ref, z2_sum_ref = refs[6:11]
    mask_ref, x_ref, xlow_ref, k_ref, v_ref, q_ref, sems = refs[11:]
    seq = lax.axis_index("seq")
    rows = attn_ref.shape[0]
    width = D
    parts = [slice(at * width, (at + 1) * width) for at in range(FF // width)]
    embed = jnp.concatenate(split3(embed_ref[...]), axis=0)
    places = lax.broadcasted_iota(jnp.int32, (DOCS, rows), 0).astype(F32)
    hot_own = None
    for at in range(count):
        ids = shards[at][rows : rows + 8, :rows].astype(F32)[:1]
        hot = (places == ids).astype(BF)
        hot_ref[:, at_lanes(seq ^ at, rows)] = hot
        x = shards[at][:rows, :].astype(F32) + tn(jnp.concatenate([hot] * 3, axis=0), embed)
        if at == 0:
            hot_own = hot
            x_ref[...] = x
            own = x.astype(BF)
        xlow_ref[at_rows(seq ^ at, rows), :] = x.astype(BF)
    moved = copy(xlow_ref, xlow_out, sems, 0)
    q_ref[...] = (
        (nn(own, qkv_ref[:, :D]) + bias_ref[:, :D]).astype(BF).astype(F32) * (HD**-0.5)
    ).astype(BF)
    step = 2 * rows
    for at in range(count * rows // step):
        piece = slice(at * step, (at + 1) * step)
        every = xlow_ref[piece, :]
        k_ref[piece, :] = nn(every, qkv_ref[:, D : 2 * D]).astype(BF)
        v_ref[piece, :] = (nn(every, qkv_ref[:, 2 * D :]) + bias_ref[:, D:]).astype(BF)
    mask_ref[...] = (tn(hot_own, hot_ref[...]) - 1.0) * -MASKED
    first = lax.broadcasted_iota(jnp.int32, (rows, PAIR), 1) < HD
    lane = lax.broadcasted_iota(jnp.int32, (rows, 128), 1)
    lse = jnp.zeros((rows, 128), F32)
    for pair in range(PAIRS):
        cols = slice(pair * PAIR, (pair + 1) * PAIR)
        q = q_ref[:, cols]
        halves = []
        for half in range(2):
            q_one = jnp.where(first if half == 0 else ~first, q, jnp.zeros_like(q))
            scores = nt(q_one, k_ref[:, cols]) + mask_ref[...]
            top = jnp.max(scores, axis=-1, keepdims=True)
            weights = jnp.exp(scores - top)
            summed = jnp.sum(weights, axis=-1, keepdims=True)
            halves.append(nn(weights.astype(BF), v_ref[:, cols]) / summed)
            lse = jnp.where(lane == 2 * pair + half, top + jnp.log(summed), lse)
        attn_ref[:, cols] = jnp.where(first, halves[0], halves[1])
    lse_ref[...] = lse
    z1, inverse = normalize(x_ref[...] + nn(attn_ref[...].astype(BF), wo_ref[...]) + bo_ref[...])
    z1_ref[...] = z1
    inverse_ref[...] = jnp.broadcast_to(inverse, (rows, 128))
    y1 = z1 * gain_ref[0:1, :] + off_ref[0:1, :]
    y1_low = y1.astype(BF)
    ydf_ref[:, :D] = y1_low
    r2 = y1 + bd_ref[...]
    for cols in parts:
        u = nn(y1_low, up_ref[:, cols]) + bu_ref[:, cols]
        phi, slope = gelu_parts(u)
        slope_ref[:, cols] = slope
        r2 = r2 + nn((u * phi).astype(BF), down_ref[cols, :])
    z2, inverse2 = normalize(r2)
    result_ref[...] = (z2 * gain_ref[1:2, :] + off_ref[1:2, :]).astype(BF)
    cot = cot_ref[...].astype(F32)
    dr2 = normalize_back(z2, inverse2, cot * gain_ref[1:2, :])
    ydf_ref[:, D:] = dr2.astype(BF)
    dr2_ref[...] = dr2
    z2_sum_ref[...] = total(cot * z2)
    moved.wait()


def backward_kernel(
    starts, chips,
    z1_ref, inverse_ref, dr2_ref, slope_ref, z2_sum_ref, attn_ref, cot_ref, hot_ref, lse_ref,
    wo_ref, up_ref, down_ref, gain_ref, ydf_ref,
    packed_ref, dr1_out, docs_out, hot_out, *refs,
):
    ado_outs, ados = refs[:chips], refs[-chips - 1 : -1]
    dr1_ref, docs_ref, sums_ref = refs[chips : chips + 3]
    sems = refs[-1]
    rows = z1_ref.shape[0]
    moved = [copy(hot_ref, hot_out, sems, 0)]
    if chips > 1:
        moved += copies([(ydf_ref, one.at[:, : 2 * D]) for one in ado_outs], sems, 3 + chips)
        ado_outs = [one.at[:, 2 * D :] for one in ado_outs]
    z1 = z1_ref[...]
    dr2 = dr2_ref[...]
    df_low = dr2.astype(BF)
    dy1 = dr2
    width = D
    for at in range(FF // width):
        cols = slice(at * width, (at + 1) * width)
        du_low = (nt(df_low, down_ref[cols, :]) * slope_ref[:, cols]).astype(BF)
        sums_ref[6 + at : 7 + at, :] = total(du_low.astype(F32))
        dy1 = dy1 + nt(du_low, up_ref[:, cols])
    dr1 = normalize_back(z1, inverse_ref[:, 0:1], dy1 * gain_ref[0:1, :])
    dr1_ref[...] = dr1
    moved.append(copy(dr1_ref, dr1_out, sems, 1))
    do_low = dr1.astype(BF)
    da = nt(do_low, wo_ref[...]).astype(BF)
    attn = attn_ref[...]
    to_heads = (
        lax.broadcasted_iota(jnp.int32, (D, 128), 0) // HD
        == lax.broadcasted_iota(jnp.int32, (D, 128), 1)
    ).astype(BF)
    high, middle, low = split3(da.astype(F32) * attn)
    delta = nn(high, to_heads) + nn(middle, to_heads) + nn(low, to_heads)
    lse_first, delta_first = lse_ref[...].T, delta.T
    cot = cot_ref[...].astype(F32)
    sums_ref[0:1, :] = total(dy1 * z1)
    sums_ref[1:2, :] = z2_sum_ref[...]
    sums_ref[2:3, :] = total(dy1)
    sums_ref[3:4, :] = total(cot)
    sums_ref[4:5, :] = total(do_low.astype(F32))
    sums_ref[5:6, :] = total(df_low.astype(F32))
    sums_ref[6 + FF // width :, :] = jnp.zeros((SUMS - 6 - FF // width, D), F32)
    share = D // len(starts)
    for at, start in enumerate(starts):
        packed_ref[at, :rows, :] = da[:, start : start + PAIR]
        head = start // HD
        lines = [lse_first[head : head + 2], delta_first[head : head + 2]]
        if chips > 1:
            mine = sums_ref[:6, at * share : (at + 1) * share]
            lines.append(jnp.concatenate([mine, jnp.zeros((6, 128 - share), F32)], axis=1))
            for part in range(3):
                first = at * 4 * share + part * 128
                lines.append(sums_ref[6 + first // D : 7 + first // D, first % D : first % D + 128])
        used = sum(one.shape[0] for one in lines)
        lines.append(jnp.zeros((SUMS - used, 128), F32))
        lines = jnp.concatenate(lines, axis=0)
        parts = jnp.concatenate([one.astype(F32) for one in split3(lines)], axis=0).astype(BF)
        packed_ref[at, rows:, :] = parts
    hot = hot_ref[:, at_lanes(lax.axis_index("seq"), rows)]
    high, middle, low = split3(dr1)
    docs_ref[...] = nn(hot, high) + nn(hot, middle) + nn(hot, low)
    moved.append(copy(docs_ref, docs_out, sems, 2))
    attn = attn.astype(BF)
    if chips == 1:
        high, low = split2(sums_ref[...])
        ados[0][:rows, :D] = attn
        ados[0][:rows, D:] = do_low
        ados[0][rows:, :D] = high
        ados[0][rows:, D:] = low
    else:
        near, across = lax.axis_index("seq") % 2, lax.axis_index("rows") // 2
        shares = [
            jnp.concatenate(
                [attn[:, (2 * z + y) * 96 : (2 * z + y + 1) * 96] for z in range(4)], axis=1
            )
            for y in range(2)
        ]
        sides = do_low[:, : D // 2], do_low[:, D // 2 :]
        for to, ref in enumerate(ados):
            swapped, over = to // 2, to % 2
            ref[:, : D // 2] = jnp.where(near == swapped, shares[0], shares[1])
            ref[:, D // 2 :] = jnp.where(across == over, sides[0], sides[1])
    moved += copies(zip(ados, ado_outs), sems, 3)
    wait(moved)


def heads_kernel(share, x_in, qkv_in, bias_ref, *refs):
    q_out, k_out, v_out, w_out, x_ref, q_ref, k_ref, v_ref, w_ref, wide_ref, sems = refs
    length = x_ref.shape[0]
    base, back = head_window(share)
    windows = copies(
        [
            (qkv_in.at[:, pl.ds(pl.multiple_of(base + kind * D, PAIR), 2 * PAIR)], wide_ref.at[kind])
            for kind in range(3)
        ],
        sems,
        0,
    )
    step = 256
    pieces = [slice(at * step, (at + 1) * step) for at in range(length // step)]
    loads = copies([(x_in.at[one, :], x_ref.at[one, :]) for one in pieces], sems, 3)
    biases = []
    for kind in range(3):
        windows[kind].wait()
        turned = pltpu.roll(wide_ref[kind].astype(F32), back, 1)[:, :PAIR]
        w_ref[:, kind * PAIR : (kind + 1) * PAIR] = turned.astype(BF)
        if kind == 1:
            biases.append(jnp.zeros((1, PAIR), F32))
        else:
            cols = pl.ds(pl.multiple_of(base + (kind // 2) * D, PAIR), 2 * PAIR)
            bias = jnp.broadcast_to(bias_ref[:, cols], (8, 2 * PAIR))
            biases.append(pltpu.roll(bias, back, 1)[:1, :PAIR])
    first = 3 + len(pieces)
    moved = [copy(w_ref, w_out, sems, first)]
    for at, piece in enumerate(pieces):
        loads[at].wait()
        three = nn(x_ref[piece, :], w_ref[...])
        q_ref[piece, :] = (
            (three[:, :PAIR] + biases[0]).astype(BF).astype(F32) * (HD**-0.5)
        ).astype(BF)
        k_ref[piece, :] = three[:, PAIR : 2 * PAIR].astype(BF)
        v_ref[piece, :] = (three[:, 2 * PAIR :] + biases[2]).astype(BF)
    moved += copies(((q_ref, q_out), (k_ref, k_out), (v_ref, v_out)), sems, first + 1)
    wait(moved)


def head_grad_kernel(step, share, *refs):
    w_in, q_in, k_in, v_in, hot_in, docs_in, da_ref = refs[:7]
    back_ref, heads_out, bias_ref, sums_ref = refs[7:11]
    refs = refs[1:]
    w_ref, q_ref, k_ref, v_ref, hot_ref, docs_ref = refs[10:16]
    dq_ref, dk_ref, dv_ref, heads_ref, sems = refs[16:]
    length = q_ref.shape[0]
    rows = length // (D // share)
    seq = lax.axis_index("seq")
    loads = copies(
        (
            (hot_in, hot_ref), (v_in, v_ref), (k_in, k_ref), (q_in, q_ref),
            (w_in, w_ref), (docs_in, docs_ref),
        ),
        sems,
        0,
    )
    wait(loads[:4])
    first = lax.broadcasted_iota(jnp.int32, (step, PAIR), 1) < HD
    each = step // rows
    sums = jnp.zeros((SUMS, rows), F32)
    for at in range(D // share):
        lines = da_ref[at, rows:, :].astype(F32)
        sums = sums + (lines[:SUMS] + lines[SUMS : 2 * SUMS] + lines[2 * SUMS :])
    sums_ref[...] = sums
    dk_ref[...] = jnp.zeros((length, PAIR), F32)
    dv_ref[...] = jnp.zeros((length, PAIR), F32)

    @functools.partial(loop, length // step)
    def _(at):
        piece = at_rows(at, step)
        blocks = [at * each + one for one in range(each)]
        da_all = jnp.concatenate([da_ref[one, :rows, :] for one in blocks], axis=0)
        stats = jnp.concatenate(
            [da_ref[one, rows:, :].astype(F32) for one in blocks], axis=1
        )
        stats = stats[:SUMS] + stats[SUMS : 2 * SUMS] + stats[2 * SUMS :]
        mask = (tn(hot_ref[...], hot_ref[:, at_lanes(at, step)]) - 1.0) * -MASKED
        halves = []
        for half in range(2):
            here = first if half == 0 else ~first
            q = jnp.where(here, q_ref[piece, :], jnp.zeros((step, PAIR), BF))
            da = jnp.where(here, da_all, jnp.zeros((step, PAIR), BF))
            probs = jnp.exp(nt(k_ref[...], q) + (mask - stats[half : half + 1]))
            ds = (probs * (nt(v_ref[...], da) - stats[2 + half : 3 + half])).astype(BF)
            halves.append(tn(ds, k_ref[...]))
            dk_ref[...] += nn(ds, q)
            dv_ref[...] += nn(probs.astype(BF), da)
        dq_ref[piece, :] = jnp.where(first, halves[0], halves[1]) * (HD**-0.5)

    wait(loads[4:])
    offset = seq * share - head_start(seq, share)
    left = (PAIR - offset) % PAIR
    for at in range(length // step):
        piece = slice(at * step, (at + 1) * step)
        heads_ref[piece, :] = jnp.concatenate(
            [pltpu.roll(ref[piece, :], left, 1)[:, :share] for ref in (dq_ref, dk_ref, dv_ref)],
            axis=1,
        ).astype(BF)
    moved = copy(heads_ref, heads_out, sems, 6)
    doc_sums = nn(hot_ref[...], heads_ref[...])
    bias_ref[...] = total(doc_sums)
    docs = docs_ref[...]
    for kind in range(3):
        piece = doc_sums[:, kind * share : (kind + 1) * share]
        piece = jnp.concatenate([piece, jnp.zeros((DOCS, PAIR - share), F32)], axis=1)
        parts = jnp.concatenate(split3(pltpu.roll(piece, offset, 1)), axis=0)
        product = nt(parts, w_ref[:, kind * PAIR : (kind + 1) * PAIR])
        docs = docs + (product[:DOCS] + product[DOCS : 2 * DOCS] + product[2 * DOCS :])
    docs = docs.astype(BF)
    extra = back_ref.shape[1] - 6 * DOCS
    full = 3 * share // PAIR
    rest = 3 * share % PAIR
    group = rows * rest // PAIR
    for at in range(D // share):
        for part in range(full):
            back_ref[at, part * rows : (part + 1) * rows, :] = heads_ref[
                at * rows : (at + 1) * rows, part * PAIR : (part + 1) * PAIR
            ]
        back_ref[at, full * rows : extra, :] = jnp.concatenate(
            [
                heads_ref[first : first + group, full * PAIR :]
                for first in range(at * rows, (at + 1) * rows, group)
            ],
            axis=1,
        )
        for col in range(PAIRS):
            back_ref[at, extra + col * DOCS : extra + (col + 1) * DOCS, :] = docs[
                :, col * PAIR : (col + 1) * PAIR
            ]
    moved.wait()


def head_weights_kernel(share, split, x_in, heads_in, bias_ref, *refs):
    outs, (x_ref, heads_ref, grad_ref, sems) = refs[:-4], refs[-4:]
    wait(copies(((heads_in, heads_ref), (x_in, x_ref)), sems, 0))
    if not split:
        outs[0][...] = tn(x_ref[...], heads_ref[...])
        return
    *sent, mine_ref = outs
    grad_ref[...] = tn(x_ref[...], heads_ref[...])
    rank = lax.axis_index("rows")
    part = share // split
    high, low = split2(jnp.broadcast_to(bias_ref[...], (8, 3 * share)))
    row = lax.broadcasted_iota(jnp.int32, (8, 3 * share), 0)
    tail = jnp.where(row == 0, high.astype(F32), jnp.where(row == 1, low.astype(F32), 0.0))
    for to, ref in enumerate([mine_ref] + list(sent)):
        for at in range(D // share):
            here = pl.ds(pl.multiple_of(at * share + (rank ^ to) * part, 8), part)
            ref[at, :part, :] = grad_ref[here, :].astype(ref.dtype)
            ref[at, part:, :] = tail.astype(ref.dtype)


def head_grad(apart, da, share):
    length = apart[1].shape[0]
    count = D // share
    rows = length // count
    outs = [((count, rows * 3 * share // PAIR + 6 * DOCS, PAIR), BF)]
    outs += [((length, 3 * share), BF, FAR), ((1, 3 * share), F32), ((SUMS, rows), F32)]
    scratch = [(one.shape, one.dtype) for one in apart] + [((length, PAIR), F32)] * 3
    scratch += [((length, 3 * share), BF)]
    return call(
        functools.partial(head_grad_kernel, 512, share),
        "head_grad",
        (*(far(one) for one in apart), da),
        outs,
        scratch,
        20 if length <= 1024 else 40,
        7,
    )


def head_weights(x_low, heads, bias, share, split):
    block = (D // share, share // split + 8, 3 * share) if split else (D, 3 * share)
    return call(
        functools.partial(head_weights_kernel, share, split),
        "head_weights",
        (far(x_low), far(heads), bias),
        [(block, BF)] * (split - 1) + [(block, F32)] if split else [(block, F32)],
        [(x_low.shape, BF), (heads.shape, BF), ((D, 3 * share), F32)],
        16,
        2,
    )


def input_grad_kernel(
    share, back_ref, dr1_in, qkv_in, sums_ref, grad_ref, docs_ref, dr1_ref, qkv_ref, sems
):
    loads = copies(
        [(qkv_in.at[:, c], qkv_ref.at[:, c]) for c in [slice(i * D, i * D + D) for i in range(3)]],
        sems,
        0,
    )
    loads.append(copy(dr1_in, dr1_ref, sems, 3))
    rows = dr1_ref.shape[0]
    count = D // share
    extra = back_ref.shape[1] - 6 * DOCS
    full = 3 * share // PAIR
    rest = 3 * share % PAIR
    kinds = [[], [], []]
    for at in range(count):
        here = [back_ref[at, part * rows : (part + 1) * rows, :] for part in range(full)]
        last = back_ref[at, full * rows : extra, :]
        here.append(
            jnp.concatenate([last[:, c : c + rest] for c in range(0, PAIR, rest)], axis=0)
        )
        here = jnp.concatenate(here, axis=1)
        for kind in range(3):
            kinds[kind].append(here[:, kind * share : (kind + 1) * share])
    docs = jnp.zeros((6 * DOCS, PAIR), F32)
    for at in range(count):
        docs = docs + back_ref[at, extra:, :].astype(F32)
    docs_ref[:DOCS, :] = jnp.concatenate(
        [docs[at * DOCS : (at + 1) * DOCS] for at in range(PAIRS)], axis=1
    )
    docs_ref[DOCS:, :128] = sums_ref[...]
    docs_ref[DOCS:, 128:] = jnp.zeros((SUMS, D - 128), F32)
    loads[3].wait()
    result = dr1_ref[...]
    for kind in range(3):
        cols = slice(kind * D, (kind + 1) * D)
        loads[kind].wait()
        result = result + nt(jnp.concatenate(kinds[kind], axis=1), qkv_ref[:, cols])
    grad_ref[...] = result


def unit_share(at):
    return 2 * (at % 4) + at // 4


def part_weights_kernel(up_near, bu_ref, up_out, bu_out, up_ref, sems):
    back = (384 - lax.axis_index("rows") * 96) % 384
    ups, biases = [], []
    for at in range(8):
        cols = slice(unit_share(at) * 384, (unit_share(at) + 1) * 384)
        ups.append(pltpu.roll(up_near[:, cols].astype(F32), back, 1)[:, :96].astype(BF))
        bias = jnp.broadcast_to(bu_ref[:, cols], (8, 384))
        biases.append(pltpu.roll(bias, back, 1)[:1, :96])
    up_ref[...] = jnp.concatenate(ups, axis=1)
    moved = copy(up_ref, up_out, sems, 0)
    bu_out[...] = jnp.concatenate(biases, axis=1)
    moved.wait()


def feed_grad_kernel(*refs):
    pieces = refs[:8]
    up_in, bu_ref, down_in, up_own_ref, up_sent_ref, down_own_ref, down_sent_ref = refs[8:15]
    y1_ref, df_ref, up_ref, down_ref, g_ref, du_ref, attn_ref, do_ref = refs[15:23]
    up_grad_ref, down_grad_ref, out_grad_ref, sems = refs[23:]
    seq, rank = lax.axis_index("seq"), lax.axis_index("rows")
    near, z = seq % 2, seq // 2
    rows = pieces[0].shape[0]
    here = [slice(at * rows, (at + 1) * rows) for at in range(8)]
    loads = [copy(up_in, up_ref, sems, 16)]
    loads += copies([(piece.at[:, :D], y1_ref.at[r, :]) for piece, r in zip(pieces, here)], sems, 0)
    first = rank * 96
    downs = copies(
        [
            (
                down_in.at[pl.ds(pl.multiple_of(unit_share(at) * 384 + first, 32), 96), :],
                down_ref.at[at * 96 : (at + 1) * 96, :],
            )
            for at in range(8)
        ],
        sems,
        17,
    )
    grads = copies([(piece.at[:, D : 2 * D], df_ref.at[r, :]) for piece, r in zip(pieces, here)], sems, 8)
    base = pl.multiple_of(2 * D + D // 2 + (rank % 2) * 128, 128)
    attns = slice(2 * D, 2 * D + D // 2)
    outs = copies([(piece.at[:, attns], attn_ref.at[r, :]) for piece, r in zip(pieces, here)], sems, 25)
    outs += copies(
        [(piece.at[:, pl.ds(base, 256)], do_ref.at[r, :]) for piece, r in zip(pieces, here)], sems, 33
    )
    step = 2 * rows
    wait(loads)
    wait(downs)
    wait(grads)

    @functools.partial(loop, 4)
    def _(at):
        piece = at_rows(at, step)
        u = nn(y1_ref[piece, :], up_ref[...]) + bu_ref[...]
        phi, slope = gelu_parts(u)
        g_ref[piece, :] = (u * phi).astype(BF)
        du_ref[piece, :] = (nt(df_ref[piece, :], down_ref[...]) * slope).astype(BF)

    down_grad_ref[...] = tn(g_ref[:, at_lanes(near, 384)], df_ref[...])
    up_grad_ref[...] = tn(y1_ref[...], du_ref[...])
    wait(outs)
    back = (256 - (rank % 2) * 64) % 256
    out_grad_ref[...] = pltpu.roll(tn(attn_ref[...], do_ref[...]), back, 1)
    for to in range(4):
        up_rows = pl.ds(pl.multiple_of((2 * (z ^ to) + near) * 96, 8), 96)
        down_rows = pl.ds(pl.multiple_of((z ^ to) * 96, 8), 96)
        ref = up_own_ref.at[to // 2] if to % 2 == 0 else up_sent_ref.at[to // 2]
        ref[:96, :] = up_grad_ref[up_rows, :].astype(ref.dtype)
        out = out_grad_ref[down_rows, :192]
        ref[96:, :] = jnp.concatenate(
            [out[part * 24 : (part + 1) * 24] for part in range(4)], axis=1
        ).astype(ref.dtype)
        ref = down_own_ref.at[to % 2] if to < 2 else down_sent_ref.at[to % 2]
        ref[...] = down_grad_ref[down_rows, :].astype(ref.dtype)


def feed_grad(pieces, up, bias, down):
    tokens = 8 * pieces[0].shape[0]
    blocks = (2, 120, D), (2, 96, D)
    wide = ((tokens, D), BF)
    return call(
        feed_grad_kernel,
        "feed_grad",
        (*(far(one) for one in pieces), far(up), bias, far(down)),
        [(block, dtype) for block in blocks for dtype in (F32, BF)],
        [
            wide, wide, ((D, D), BF), ((D, D), BF), wide, wide, ((tokens, D // 2), BF),
            ((tokens, 256), BF), ((D, D), F32), ((384, D), F32), ((384, 256), F32),
        ],
        26,
        41,
    )


def combine_half_kernel(*refs):
    for own_ref, got_ref, mine_ref, sent_ref in (refs[0::2], refs[1::2]):
        mine_ref[...] = own_ref[0] + got_ref[0].astype(F32)
        sent_ref[...] = (own_ref[1] + got_ref[1].astype(F32)).astype(BF)


def combine_all_kernel(up_ref, down_ref, up_got_ref, down_got_ref, out_ref):
    out_ref[:120, :] = (up_ref[...] + up_got_ref[...].astype(F32)).astype(BF)
    out_ref[120:, :] = (down_ref[...] + down_got_ref[...].astype(F32)).astype(BF)


def finish_all_kernel(a_ref, b_ref, c_ref, d_ref, up_ref, down_ref, out_ref, held_ref):
    rank = lax.axis_index("rows")
    for at, ref in enumerate((a_ref, b_ref, c_ref, d_ref)):
        held_ref[rank ^ at] = ref[:120, :].astype(F32)
        down_ref[pl.ds(pl.multiple_of((rank ^ at) * 96, 8), 96), :] = ref[120:, :].astype(F32)
    for share in range(8):
        at = (share // 2) + 4 * (share % 2)
        up_ref[:, share * 384 : (share + 1) * 384] = jnp.concatenate(
            [held_ref[r, :96, at * 96 : (at + 1) * 96] for r in range(4)], axis=1
        )
    for at in range(4):
        out_ref[at * 24 : (at + 1) * 24, :] = jnp.concatenate(
            [held_ref[r, 96:, at * 192 : (at + 1) * 192] for r in range(4)], axis=1
        )


def time_grad_kernel(*refs):
    features, docs, (out_ref, norm_ref, bias_ref, up_ref, left_ref, sems) = refs[:4], refs[4:8], refs[8:]
    seq = lax.axis_index("seq")
    wait(
        copies([(ref, left_ref.at[at * DOCS : (at + 1) * DOCS]) for at, ref in enumerate(features)], sems, 0)
    )
    left = left_ref[...].astype(F32)
    left = pltpu.roll(left, (D - seq * 96) % D, 1)[:, :96].astype(BF)
    high, middle, low = split3(jnp.concatenate([ref[:DOCS, :] for ref in docs], axis=0))
    out_ref[...] = tn(left, high) + tn(left, middle) + tn(left, low)
    sums = jnp.zeros((SUMS, 128), F32)
    for ref in docs:
        sums = sums + ref[DOCS:, :128]
    norm_ref[...] = sums[4:8, :96]
    bias_ref[...] = sums[8:10, :96]
    up_ref[...] = jnp.concatenate([sums[at : at + 1] for at in range(10, 13)], axis=1)


def finish_heads_kernel(a_ref, b_ref, c_ref, d_ref, out_ref, bias_ref):
    rank = lax.axis_index("rows")
    order = [(kind, at) for kind in range(3) for at in range(8)]
    for to, ref in enumerate((a_ref, b_ref, c_ref, d_ref)):
        value = jnp.concatenate(
            [ref[at, :24, kind * 96 : (kind + 1) * 96].astype(F32) for kind, at in order], axis=1
        )
        out_ref[pl.ds(pl.multiple_of((rank ^ to) * 24, 8), 24), :] = value
    tail = jnp.concatenate(
        [a_ref[at, 24:, kind * 96 : (kind + 1) * 96].astype(F32) for kind, at in order], axis=1
    )
    sums = tail[0:1] + tail[1:2]
    sums = jnp.concatenate([sums[:, :D], sums[:, 2 * D :]], axis=1)
    back = (2 * D - lax.axis_index("seq") * 192) % (2 * D)
    bias_ref[...] = pltpu.roll(jnp.broadcast_to(sums, (8, 2 * D)), back, 1)[:1, :192]


def combine_kernel(tail, own_ref, a_ref, b_ref, c_ref, out_ref):
    value = own_ref[...]
    for ref in (a_ref, b_ref, c_ref):
        value = value + ref[...].astype(F32)
    if tail:
        count, rows, wide = value.shape
        out_ref[:, : rows - 8, :] = value[:, : rows - 8].astype(out_ref.dtype)
        row = lax.broadcasted_iota(jnp.int32, (8, wide), 0)
        for at in range(count):
            last = value[at, rows - 8 :]
            high, low = split2(jnp.broadcast_to(last[0:1] + last[1:2], (8, wide)))
            out_ref[at, rows - 8 :, :] = jnp.where(
                row == 0, high.astype(F32), jnp.where(row == 1, low.astype(F32), 0.0)
            ).astype(out_ref.dtype)
    else:
        out_ref[...] = value.astype(out_ref.dtype)


def combine(blocks, dtype, tail=False):
    return call(
        functools.partial(combine_kernel, tail), "combine", blocks, [(blocks[0].shape, dtype)]
    )[0]


def after(value, *others):
    return lax.optimization_barrier((value,) + others)[0]


def after_all(values, *others):
    return list(lax.optimization_barrier((tuple(values), others))[0])


def gates(order):
    known = {}

    def gate(name, value):
        held = [known[one] for one in order.get(name, ()) if one in known]
        return lax.optimization_barrier((value, held))[0] if held else value

    return known, gate


def from_chips(own, over, near, both):
    pairs = [((s * 4 + r), ((s ^ 1) * 4 + (r ^ 2))) for s in range(8) for r in range(4)]
    across = lax.ppermute(both, ("seq", "rows"), pairs)
    return [own, swap(over, "rows", 2), swap(near, "seq", 1), across]


def with_twin(blocks):
    return blocks + [swap(one, "rows", 1) for one in blocks]


def spread_rows(block):
    across = swap(block, "rows", 2)
    return block, swap(block, "rows", 1), across, swap(across, "rows", 1)


def pick(blocks, index, axis=0):
    return lax.dynamic_index_in_dim(blocks, index, axis, keepdims=False)


def reduce_rows(blocks, place):
    bit = 1
    while blocks.shape[0] > 1:
        pairs = blocks.reshape((blocks.shape[0] // 2, 2) + blocks.shape[1:])
        mine = (place // bit) % 2
        sent = swap(pick(pairs, 1 - mine, 1).astype(BF), "rows", bit)
        blocks = pick(pairs, mine, 1).astype(F32) + sent.astype(F32)
        bit *= 2
    return blocks[0]


def gather_rows(block, place):
    count = lax.axis_size("rows")
    found = block[None]
    bit = count // 2
    while bit >= 1:
        other = swap(found, "rows", bit)
        mine = (place // bit) % 2
        low, high = jnp.where(mine == 0, found, other), jnp.where(mine == 0, other, found)
        if bit == count // 2:
            found = jnp.concatenate([low, high], axis=0)
        else:
            found = jnp.stack([low, high], axis=1).reshape((-1,) + block.shape)
        bit //= 2
    return found


def general_grads(ydf, ado, grad_heads, head_sums, up_weight, up_bias, down_weight):
    seqs, ranks = lax.axis_size("seq"), lax.axis_size("rows")
    seq, rank = lax.axis_index("seq"), lax.axis_index("rows")
    inner = seqs // Z_STEPS
    near = seq % inner
    share = D // seqs
    ff_share = FF // seqs
    ff_part = ff_share // ranks
    rows = ydf.shape[0]

    part = share // ranks
    grad_heads = grad_heads.reshape(seqs, ranks, part, 3 * share)
    mine = reduce_rows(jnp.moveaxis(grad_heads, 1, 0), rank)
    spread = lax.all_to_all(mine.astype(BF), "seq", 0, 0, tiled=True)
    columns = [
        spread[i, :, kind * share : (kind + 1) * share] for kind in range(3) for i in range(seqs)
    ]
    quarter = jnp.concatenate(columns, axis=1)
    grad_qkv = gather_rows(quarter, rank).reshape(share, 3 * D).astype(F32)

    def gather_near(block):
        found = [block]
        bit = 2
        while bit < ranks:
            found = found + [swap(one, "rows", bit) for one in found]
            bit *= 2
        for step in range(1, inner):
            found = found + [swap(one, "seq", step) for one in found[: len(found) // step]]
        mine = jnp.concatenate(found, axis=0)
        return jnp.concatenate([mine, swap(mine, "rows", 1)], axis=0)

    ydf_all = gather_near(ydf)
    y1_all, df_all = ydf_all[:, :D], ydf_all[:, D:]
    order = [far * inner + i for i in range(inner) for far in range(Z_STEPS)]
    ff_starts = [i * ff_share + rank * ff_part for i in order]
    take = lambda array, axis: jnp.concatenate(
        [lax.dynamic_slice_in_dim(array, a, ff_part, axis) for a in ff_starts], axis=axis
    )
    up_mine, down_mine, bias_mine = take(up_weight, 1), take(down_weight, 0), take(up_bias, 0)
    u = nn(y1_all, up_mine) + bias_mine
    phi, slope = gelu_parts(u)
    du_all = (nt(df_all, down_mine) * slope).astype(BF)
    g_all = (u * phi).astype(BF)
    group = Z_STEPS * ff_part
    g_near = lax.dynamic_slice_in_dim(g_all, near * group, group, 1)
    grad_down = tn(g_near, df_all).reshape(Z_STEPS, ff_part, D)
    grad_up = pick(tn(y1_all, du_all).reshape(Z_STEPS, inner, share, seqs * ff_part), near, 1)
    ado, grad_up, grad_down = lax.optimization_barrier((ado, grad_up, grad_down))
    ado_all = gather_near(ado[:rows])
    attn_all, do_all = ado_all[:, :D], ado_all[:, D:]
    out_part = D // ranks
    do_mine = lax.dynamic_slice_in_dim(do_all, rank * out_part, out_part, 1)
    grad_out = pick(tn(attn_all, do_mine).reshape(Z_STEPS, inner, share, out_part), near, 1)

    def reduce_far(blocks):
        blocks = blocks.astype(BF)
        far = seq // inner
        summed = pick(blocks, far).astype(F32)
        for step in range(1, Z_STEPS):
            summed = summed + swap(pick(blocks, far ^ step), "seq", step * inner).astype(F32)
        return gather_rows(summed.astype(BF), rank)

    grad_down = reduce_far(grad_down).reshape(ff_share, D).astype(F32)
    grad_up = reduce_far(grad_up).reshape(ranks, share, inner, Z_STEPS, ff_part)
    grad_up = jnp.transpose(grad_up, (1, 3, 2, 0, 4)).reshape(share, FF).astype(F32)
    grad_out = jnp.transpose(reduce_far(grad_out), (1, 0, 2)).reshape(share, D).astype(F32)

    sums = ado[rows:, :D].astype(F32) + ado[rows:, D:].astype(F32)
    placed = lambda kind: lax.dynamic_update_slice_in_dim(
        jnp.zeros((D,), F32), head_sums[0, kind * share : (kind + 1) * share], seq * share, 0
    )
    sums = sums.at[10].set(placed(0)).at[11].set(placed(2))
    for axis, count in (("rows", ranks), ("seq", seqs)):
        bit = 1
        while bit < count:
            sums = sums + swap(sums, axis, bit)
            bit *= 2
    return grad_qkv, sums[10:12].reshape(-1), grad_out, grad_up, grad_down, sums


def body(
    hidden, cotangent, segment_ids, timesteps, qkv_weight, qv_bias, out_weight, out_bias,
    up_weight, up_bias, down_weight, down_bias, norm_gain, norm_bias, time_weight,
):
    assert hidden.shape[0] == 1
    rows = hidden.shape[1]
    seqs, ranks = lax.axis_size("seq"), lax.axis_size("rows")
    length = seqs * rows
    seq, rank = lax.axis_index("seq"), lax.axis_index("rows")
    share = D // seqs
    inner = seqs // Z_STEPS
    fast = seqs == 8 and ranks == 4
    starts = [min(i * share // HD, H - 2) * HD for i in range(seqs)]

    ids = jnp.pad(segment_ids.astype(BF), ((0, 7), (0, D - rows)))
    known, gate = gates(ORDER if fast else {})
    shards = gather_seq(jnp.concatenate([hidden[0], ids], axis=0), known, gate)

    features = time_features(timesteps[0]).astype(BF)
    embed = nn(features, time_weight)
    if fast:
        all_features = spread_rows(gate("feat", features))
        known["feat"] = all_features[1:]
    else:
        all_features = gather_rows(features, rank)
        all_features = lax.dynamic_slice_in_dim(all_features, seq * share, share, 2)
    qv_row, up_row = qv_bias.reshape(1, -1), up_bias.reshape(1, -1)
    tile = ((rows, D), BF)
    tile32 = ((rows, D), F32)
    narrow32 = ((rows, 128), F32)
    wide = ((length, D), BF)
    weights = [((D, 3 * D), BF), ((D, D), BF), ((D, FF), BF), ((FF, D), BF)]
    qkv_near, out_near, up_near, down_near = call(
        fetch_kernel,
        "fetch",
        (far(gate("fetch", qkv_weight)), far(out_weight), far(up_weight), far(down_weight)),
        [(*one, NEAR) for one in weights],
        (),
        2,
        4,
    )
    out_row, down_row = out_bias.reshape(1, -1), down_bias.reshape(1, -1)
    known["fetch"] = out_near
    if fast:
        up_part, bias_part = call(
            part_weights_kernel,
            "part_weights",
            (up_near, gate("part", up_row)),
            [((D, D), BF, FAR), ((1, D), F32)],
            [((D, D), BF)],
            14,
            1,
        )
        known["part"] = bias_part
        embed = after(embed, bias_part, all_features)
    x_low, lse, attn, hot, z1, inverse1, result, ydf, dr2, slope, z2_sum = call(
        functools.partial(forward_kernel, seqs),
        "forward",
        (
            *shards, embed, qkv_near, qv_row, out_near, out_row, norm_gain,
            norm_bias, cotangent[0], up_near, up_row, down_near, down_row,
        ),
        [
            (*wide, FAR), narrow32,
            tile32, ((DOCS, length), BF), tile32, narrow32,
            tile, ((rows, 2 * D), BF), tile32, ((rows, FF), F32), ((1, D), F32),
        ],
        [((rows, length), F32), tile32, wide, wide, wide, tile],
        16 if fast else 28,
        1,
    )
    known["forward"] = z1
    if fast:
        ados = [((rows, 3 * D), BF)] * 4
    else:
        ados = [((rows + SUMS, 2 * D), BF)]
    hots = ((DOCS, length), BF)
    docs_shape = ((DOCS, D), F32)
    packed, dr1, docs, hot, *ado = call(
        functools.partial(backward_kernel, starts, len(ados)),
        "backward",
        (
            gate("backward", z1), inverse1, dr2, slope, z2_sum, attn, cotangent[0], hot, lse,
            out_near, up_near, down_near, norm_gain, ydf,
        ),
        [
            ((seqs, rows + 3 * SUMS, PAIR), BF), (*tile32, FAR), (*docs_shape, FAR), (*hots, FAR),
            *((*one, FAR) for one in ados),
        ],
        [tile32, docs_shape, ((SUMS, D), F32), *([tile] * 4 if fast else ados)],
        8,
        3 + 2 * len(ados),
    )
    known["backward"] = packed

    arrived = lax.all_to_all(gate("DA", packed), "seq", 0, 0, tiled=True)
    known["DA"] = arrived
    pair = ((length, PAIR), BF)
    head_shape = ((D, 3 * PAIR), BF)
    q_two, k_two, v_two, head_weight = call(
        functools.partial(heads_kernel, share),
        "heads",
        (far(x_low), far(qkv_weight), gate("heads", qv_row)),
        [(*one, FAR) for one in (pair, pair, pair, head_shape)],
        [wide, pair, pair, pair, head_shape, ((3, D, 2 * PAIR), BF)],
        16,
        7 + length // 256,
    )
    known["heads"] = q_two
    if fast:
        near_all = from_chips(*gate("E", ado))
        known["E"] = near_all[1:]
    back, heads, head_sums, sums = head_grad(
        (head_weight, q_two, k_two, v_two, hot, docs), gate("head", arrived), share
    )
    back, heads, head_sums, sums = gate("headend", (back, heads, head_sums, sums))
    known["head"] = back
    if fast:
        near_all = with_twin(gate("Etwin", near_all))
        known["Etwin"] = near_all[4:]
        up_own, up_sent, down_own, down_sent = feed_grad(
            near_all, up_part, gate("feed", bias_part), down_weight
        )
        known["feed"] = up_own
        up_sent, down_sent = gate("RS1", (up_sent, down_sent))
        up_got, down_got = swap(up_sent, "seq", 2), swap(down_sent, "seq", 4)
        known["RS1"] = (up_got, down_got)
    back = lax.all_to_all(gate("BACK", back), "seq", 0, 0, tiled=True)
    known["BACK"] = back
    if fast:
        up_got, down_got = gate("half", (up_got, down_got))
        up_mine, down_mine, up_sent, down_sent = call(
            combine_half_kernel, "combine_half", (up_own, down_own, up_got, down_got),
            [((120, D), F32), ((96, D), F32), ((120, D), BF), ((96, D), BF)],
        )
        known["half"] = up_mine
        up_sent, down_sent = gate("RS2", (up_sent, down_sent))
        up_got, down_got = swap(up_sent, "seq", 4), swap(down_sent, "seq", 2)
        known["RS2"] = (up_got, down_got)
    grads = head_weights(x_low, heads, gate("hw", head_sums), share, 4 if fast else 0)
    known["hw"] = grads
    if fast:
        *sent, own = gate("GRS", grads)
        sent = [swap(block, "rows", to + 1) for to, block in enumerate(sent)]
        known["GRS"] = sent
        mine = combine((own, *gate("gc", sent)), BF, True)
        known["gc"] = mine
        spread = lax.all_to_all(gate("GA2A", mine), "seq", 0, 0, tiled=True)
        known["GA2A"] = spread
    input_grad, doc_grad = call(
        functools.partial(input_grad_kernel, share),
        "input_grad",
        (gate("in", back), far(dr1), far(qkv_weight), sums),
        [tile32, ((DOCS + SUMS, D), F32)],
        [tile32, ((D, 3 * D), BF)],
        10,
        4,
    )
    known["in"] = input_grad
    if fast:
        docs_all = spread_rows(gate("DOCS", doc_grad))
        known["DOCS"] = docs_all[1:]
        up_got, down_got = gate("all", (up_got, down_got))
        merged = call(
            combine_all_kernel, "combine_all", (up_mine, down_mine, up_got, down_got),
            [((216, D), BF)],
        )[0]
        known["all"] = merged
        feed_all = spread_rows(gate("AGF", merged))
        known["AGF"] = feed_all[1:]
        heads_all = spread_rows(gate("AGG", spread))
        known["AGG"] = heads_all[1:]
        grad_time_weight, norm_sums, bias_sums, grad_up_bias = call(
            time_grad_kernel, "time_grad",
            (*(far(one) for one in all_features), *gate("time", docs_all)),
            [((share, D), F32), ((4, 96), F32), ((2, 96), F32), ((1, 384), F32)],
            [((4 * DOCS, D), BF)],
            8,
            4,
        )
        known["time"] = grad_time_weight
        grad_up_weight, grad_down_weight, grad_out_weight = call(
            finish_all_kernel, "finish_all", gate("finf", feed_all),
            [((share, FF), F32), ((FF // seqs, D), F32), ((share, D), F32)],
            [((4, 120, D), F32)],
        )
        known["finf"] = grad_out_weight
        grad_qkv_weight, grad_qv_bias = call(
            finish_heads_kernel, "finish_heads", gate("finh", heads_all),
            [((share, 3 * D), F32), ((1, 192), F32)],
        )
        grad_qv_bias, grad_up_bias = grad_qv_bias[0], grad_up_bias[0]
        grad_out_bias, grad_down_bias = bias_sums[0], bias_sums[1]
        grad_norm_gain, grad_norm_bias = norm_sums[:2], norm_sums[2:]
    else:
        doc_grad = gather_rows(doc_grad[:DOCS], rank).reshape(ranks * DOCS, D)
        grad_time_weight = lax.dot_general(
            all_features.reshape(ranks * DOCS, share).astype(F32),
            doc_grad,
            (((0,), (0,)), ((), ())),
            precision=precise,
        )
        grad_qkv_weight, qv_sums, grad_out_weight, grad_up_weight, grad_down_weight, totals = (
            general_grads(ydf, ado[0], grads[0], head_sums, up_weight, up_bias, down_weight)
        )

        def part_of(vector, axis=0):
            size = vector.shape[axis] // seqs
            return lax.dynamic_slice_in_dim(vector, seq * size, size, axis)

        grad_qv_bias, grad_out_bias = part_of(qv_sums), part_of(totals[4])
        grad_up_bias = part_of(totals[6 : 6 + FF // D].reshape(-1))
        grad_down_bias = part_of(totals[5])
        grad_norm_gain, grad_norm_bias = part_of(totals[0:2], 1), part_of(totals[2:4], 1)

    return (
        result[None],
        input_grad[None],
        grad_qkv_weight,
        grad_qv_bias,
        grad_out_weight,
        grad_out_bias,
        grad_up_weight,
        grad_up_bias,
        grad_down_weight,
        grad_down_bias,
        grad_norm_gain,
        grad_norm_bias,
        grad_time_weight,
    )


def solution(mesh):
    tokens = P("rows", "seq", None)
    whole = P()
    return jax.shard_map(
        body,
        mesh=mesh,
        in_specs=(tokens, tokens, P("rows", "seq"), P("rows", None)) + (whole,) * 11,
        out_specs=(
            tokens,
            tokens,
            P("seq", None),
            P("seq"),
            P("seq", None),
            P("seq"),
            P("seq", None),
            P("seq"),
            P("seq", None),
            P("seq"),
            P(None, "seq"),
            P(None, "seq"),
            P("seq", None),
        ),
        check_vma=False,
    )
```

profile of v0, /device:TPU:0, one launch (start us, length us, event | category | flops | bytes accessed | tf_op | source)
XLA Modules:
  0.0 167.1 jit_solution(2725130247650669861)
XLA Ops:
  0.7 0.8 convert_element_type.16
  1.4 0.9 fusion.1.refs_0_
  2.4 4.1 %collective-permute-start.3 = (bf16[136,768]{1,0:T(8,128)(2,1)S(1)}, bf16[136,768]{1,0:T(8,128)(2,1)S(1)}, u32[]{:S(2)}, u32[]{:S(2)}) collective-permute-start(bf16[136,768]{1,0:T(8,128)(2,1)S(1)} %fusion.1.refs_0_), channel_id=1, source_target_pairs={{0,16},{4,20},{8,24},{12,28},{16,0},{20,4},{24,8},{28,12},{1,17},{... | collective-permute-start | bytes 626696 | tf_op jit(solution)/shard_map/ppermute | solution.py:30
  6.5 1.6 collective-permute-start.1
  8.0 1.5 collective-permute-start
  9.6 0.7 convert_bitcast_fusion
  10.2 0.7 reshape.51.refs_12_
  10.9 0.7 reshape.52.refs_19_
  11.6 0.7 reshape.50.refs_10_.bias_ref
  12.8 1.6 collective-permute-done.refs_1_
  14.4 1.5 collective-permute-start.8
  15.9 0.5 collective-permute-done.1.refs_2_
  16.8 5.1 %fetch.1 = (bf16[768,2304]{1,0:T(8,128)(2,1)S(1)}, bf16[768,768]{1,0:T(8,128)(2,1)S(1)}, bf16[768,3072]{1,0:T(8,128)(2,1)S(1)}, bf16[3072,768]{1,0:T(8,128)(2,1)S(1)}) custom-call(bf16[768,2304]{1,0:T(8,128)(2,1)} %qkv_in.3, bf16[768,768]{1,0:T(8,128)(2,1)} %refs_1_.1, bf16[768,3072]{1,0:T(8,128)(2,1)} %refs_2_.1, bf16[3072,768]{1,0:T(8,128)(2,1)} %refs_10_.1), custom_call_target="tpu_custom_call" | custom-call | flops 7000000000 | tf_op jit(solution)/shard_map/fetch/pallas_call | solution.py:67
  21.9 1.6 collective-permute-start.2
  23.5 0.5 collective-permute-start.4
  24.0 1.3 collective-permute-done.5.refs_6_
  25.4 1.5 collective-permute-start.6
  26.9 3.6 %part_weights.1 = (bf16[768,768]{1,0:T(8,128)(2,1)}, f32[1,768]{1,0:T(1,128)S(1)}) custom-call(bf16[768,3072]{1,0:T(8,128)(2,1)S(1)} %get-tuple-element.96.up_near.refs_16_.up_ref, f32[1,3072]{1,0:T(1,128)S(1)} %bitcast.15), custom_call_target="tpu_custom_call" | custom-call | flops 3000000000 | tf_op jit(solution)/shard_map/part_weights/pallas_call | solution.py:67
  30.5 4.0 %collective-permute-done.4.refs_5_ = bf16[136,768]{1,0:T(8,128)(2,1)S(1)} collective-permute-done((bf16[136,768]{1,0:T(8,128)(2,1)S(1)}, bf16[136,768]{1,0:T(8,128)(2,1)S(1)}, u32[]{:S(2)}, u32[]{:S(2)}) %collective-permute-start.4) | collective-permute-done | bytes 208928 | tf_op jit(solution)/shard_map/ppermute | solution.py:30
  34.5 3.1 %collective-permute-done.6.refs_7_ = bf16[136,768]{1,0:T(8,128)(2,1)S(1)} collective-permute-done((bf16[136,768]{1,0:T(8,128)(2,1)S(1)}, bf16[136,768]{1,0:T(8,128)(2,1)S(1)}, u32[]{:S(2)}, u32[]{:S(2)}) %collective-permute-start.6) | collective-permute-done | bytes 208928 | tf_op jit(solution)/shard_map/ppermute | solution.py:30
  37.7 12.5 %forward.1 = (bf16[1024,768]{1,0:T(8,128)(2,1)}, f32[128,128]{1,0:T(8,128)S(1)}, f32[128,768]{1,0:T(8,128)S(1)}, bf16[16,1024]{1,0:T(8,128)(2,1)S(1)}, f32[128,7...) custom-call(bf16[136,768]{1,0:T(8,128)(2,1)S(1)} %fusion.1.refs_0_, ...), custom_call_target="tpu_custom_call" | custom-call | flops 12000000000 | tf_op jit(solution)/shard_map/forward/pallas_call | solution.py:67
  50.2 5.8 %backward.1 = (bf16[8,176,128]{2,1,0:T(8,128)(2,1)}, f32[128,768]{1,0:T(8,128)}, f32[16,768]{1,0:T(8,128)}, bf16[16,1024]{1,0:T(8,128)(2,1)}, bf16[128,2304]{1,0...) custom-call(f32[128,768]{1,0:T(8,128)S(1)} %get-tuple-element.110.z1_ref, ...), custom_call_target="tpu_custom_call" | custom-call | flops 5000000000 | tf_op jit(solution)/shard_map/backward/pallas_call | solution.py:67
  56.0 5.8 %all-to-all-start = ((bf16[8,176,128]{2,1,0:T(8,128)(2,1)}), bf16[8,176,128]{2,1,0:T(8,128)(2,1)S(1)}, u32[]{:S(2)}, u32[]{:S(2)}) async-start(bf16[8,176,128]{2,1,0:T(8,128)(2,1)} %get-tuple-element.121), calls=%async_computation | async-start | bytes 720896 | tf_op jit(solution)/shard_map/all_to_all | solution.py:1027
  61.8 0.5 collective-permute-start.10
  62.3 2.0 %collective-permute-start.11 = (bf16[128,2304]{1,0:T(8,128)(2,1)}, bf16[128,2304]{1,0:T(8,128)(2,1)}, u32[]{:S(2)}, u32[]{:S(2)}) collective-permute-start(bf16[128,2304]{1,0:T(8,128)(2,1)} %get-tuple-element.128), channel_id=1, source_target_pairs={{0,4},{4,0},{8,12},{12,8},{16,20},{20,16},{24,28},{28,24},{1,5},{5... | collective-permute-start | bytes 1769480 | tf_op jit(solution)/shard_map/ppermute | solution.py:30
  64.3 0.9 collective-permute-start.12
  65.3 4.1 %heads.1 = (bf16[1024,128]{1,0:T(8,128)(2,1)}, bf16[1024,128]{1,0:T(8,128)(2,1)}, bf16[1024,128]{1,0:T(8,128)(2,1)}, bf16[768,384]{1,0:T(8,128)(2,1)}) custom-call(bf16[1024,768]{1,0:T(8,128)(2,1)} %get-tuple-element.105.x_in, bf16[768,2304]{1,0:T(8,128)(2,1)} %qkv_in.3, f32[1,1536]{1,0:T(1,128)S(1)} %reshape.50.refs_10_.bias_ref), custom_call_target="tpu_custom_call" | custom-call | flops 3000000000 | tf_op jit(solution)/shard_map/heads/pallas_call | solution.py:67
  69.4 2.3 %all-to-all-done.refs_6_ = bf16[8,176,128]{2,1,0:T(8,128)(2,1)S(1)} async-done(((bf16[8,176,128]{2,1,0:T(8,128)(2,1)}), bf16[8,176,128]{2,1,0:T(8,128)(2,1)S(1)}, u32[]{:S(2)}, u32[]{:S(2)}) %all-to-all-start) | async-done | bytes 360480 | tf_op jit(solution)/shard_map/all_to_all | solution.py:1027
  71.7 11.1 %head_grad.1 = (bf16[8,384,128]{2,1,0:T(8,128)(2,1)}, bf16[1024,288]{1,0:T(8,128)(2,1)}, f32[1,288]{1,0:T(1,128)S(1)}, f32[16,128]{1,0:T(8,128)S(1)}) custom-call(bf16[768,384]{1,0:T(8,128)(2,1)} %get-tuple-element.106.refs_0_, bf16[1024,128]{1,0:T(8,128)(2,1)} %get-tuple-element.107.refs_1_, bf16[1024,128]{1,0:T(8,128)(2,1)} %get-tuple-element.108.refs_2_, ...), custom_call_target="tpu_custom_call" | custom-call | flops 8999999488 | tf_op jit(solution)/shard_map/head_grad/pallas_call | solution.py:67
  82.8 9.5 %collective-permute-done.11.refs_2_ = bf16[128,2304]{1,0:T(8,128)(2,1)} collective-permute-done((bf16[128,2304]{1,0:T(8,128)(2,1)}, bf16[128,2304]{1,0:T(8,128)(2,1)}, u32[]{:S(2)}, u32[]{:S(2)}) %collective-permute-start.11) | collective-permute-done | bytes 589856 | tf_op jit(solution)/shard_map/ppermute | solution.py:30
  93.3 4.5 %all-to-all-start.1 = ((bf16[8,384,128]{2,1,0:T(8,128)(2,1)}), bf16[8,384,128]{2,1,0:T(8,128)(2,1)S(1)}, u32[]{:S(2)}, u32[]{:S(2)}) async-start(bf16[8,384,128]{2,1,0:T(8,128)(2,1)} %get-tuple-element.130), calls=%async_computation.1 | async-start | bytes 1572864 | tf_op jit(solution)/shard_map/all_to_all | solution.py:1059
  97.9 9.1 %feed_grad.1 = (f32[2,120,768]{2,1,0:T(8,128)S(1)}, bf16[2,120,768]{2,1,0:T(8,128)(2,1)S(1)}, f32[2,96,768]{2,1,0:T(8,128)S(1)}, bf16[2,96,768]{2,1,0:T(8,128)(2,1)S(1)}) custom-call(bf16[128,2304]{1,0:T(8,128)(2,1)} %get-tuple-element.141.refs_0_, bf16[128,2304]{1,0:T(8,128)(2,1)} %copy-done.13, bf16[128,2304]{1,0:T(8,128)(2,1)} %collective-permute-done.11.refs_2_, ...), custom_call_target="tpu_custom_call" | custom-call | flops 8000000000 | tf_op jit(solution)/shard_map/feed_grad/pallas_call | solution.py:67
  107.0 3.0 %collective-permute-start.24 = (bf16[2,96,768]{2,1,0:T(8,128)(2,1)S(1)}, bf16[2,96,768]{2,1,0:T(8,128)(2,1)S(1)}, u32[]{:S(2)}, u32[]{:S(2)}) collective-permute-start(bf16[2,96,768]{2,1,0:T(8,128)(2,1)S(1)} %get-tuple-element.149), channel_id=1, source_target_pairs={{0,16},{4,20},{8,24},{12,28},{16,0},{20,4},{24,8},{28,12},{1,17},{... | collective-permute-start | bytes 884744 | tf_op jit(solution)/shard_map/ppermute | solution.py:30
  110.0 1.5 collective-permute-start.23
  111.5 2.7 %head_weights.1 = (bf16[8,32,288]{2,1,0:T(8,128)(2,1)S(1)}, bf16[8,32,288]{2,1,0:T(8,128)(2,1)S(1)}, bf16[8,32,288]{2,1,0:T(8,128)(2,1)S(1)}, f32[8,32,288]{2,1,0:T(8,128)S(1)}) custom-call(bf16[1024,768]{1,0:T(8,128)(2,1)} %get-tuple-element.105.x_in, bf16[1024,288]{1,0:T(8,128)(2,1)} %get-tuple-element.134.heads_in, f32[1,288]{1,0:T(1,128)S(1)} %get-tuple-element.135.bias_ref), custom_call_target="tpu_custom_call" | custom-call | flops 2000000000 | tf_op jit(solution)/shard_map/head_weights/pallas_call | solution.py:67
  114.3 0.8 collective-permute-start.14
  115.1 1.1 collective-permute-start.15
  116.2 5.9 %collective-permute-done.14.b_ref = bf16[8,32,288]{2,1,0:T(8,128)(2,1)S(1)} collective-permute-done((bf16[8,32,288]{2,1,0:T(8,128)(2,1)S(1)}, bf16[8,32,288]{2,1,0:T(8,128)(2,1)S(1)}, u32[]{:S(2)}, u32[]{:S(2)}) %collective-permute-start.14) | collective-permute-done | bytes 147488 | tf_op jit(solution)/shard_map/ppermute | solution.py:30
  122.1 3.3 %collective-permute-done.15.c_ref = bf16[8,32,288]{2,1,0:T(8,128)(2,1)S(1)} collective-permute-done((bf16[8,32,288]{2,1,0:T(8,128)(2,1)S(1)}, bf16[8,32,288]{2,1,0:T(8,128)(2,1)S(1)}, u32[]{:S(2)}, u32[]{:S(2)}) %collective-permute-start.15) | collective-permute-done | bytes 147488 | tf_op jit(solution)/shard_map/ppermute | solution.py:30
  125.4 0.8 combine.1
  126.2 4.7 %collective-permute-done.24.refs_3_ = bf16[2,96,768]{2,1,0:T(8,128)(2,1)S(1)} collective-permute-done((bf16[2,96,768]{2,1,0:T(8,128)(2,1)S(1)}, bf16[2,96,768]{2,1,0:T(8,128)(2,1)S(1)}, u32[]{:S(2)}, u32[]{:S(2)}) %collective-permute-start.24) | collective-permute-done | bytes 294944 | tf_op jit(solution)/shard_map/ppermute | solution.py:30
  131.0 0.7 copy-done.9
  131.8 1.7 %collective-permute-start.25 = (bf16[120,768]{1,0:T(8,128)(2,1)S(1)}, bf16[120,768]{1,0:T(8,128)(2,1)S(1)}, u32[]{:S(2)}, u32[]{:S(2)}) collective-permute-start(bf16[120,768]{1,0:T(8,128)(2,1)S(1)} %get-tuple-element.152), channel_id=1, source_target_pairs={{0,16},{4,20},{8,24},{12,28},{16,0},{20,4},{24,8},{28,12},{1,17},{... | collective-permute-start | bytes 552968 | tf_op jit(solution)/shard_map/ppermute | solution.py:30
  133.4 4.8 %all-to-all-start.2 = ((bf16[8,32,288]{2,1,0:T(8,128)(2,1)}), bf16[8,32,288]{2,1,0:T(8,128)(2,1)S(1)}, u32[]{:S(2)}, u32[]{:S(2)}) async-start(bf16[8,32,288]{2,1,0:T(8,128)(2,1)} %combine.1), calls=%async_computation.2 | async-start | bytes 393216 | tf_op jit(solution)/shard_map/all_to_all | solution.py:1079
  138.3 4.6 %input_grad.1 = (f32[128,768]{1,0:T(8,128)}, f32[32,768]{1,0:T(8,128)S(1)}) custom-call(bf16[8,384,128]{2,1,0:T(8,128)(2,1)S(1)} %all-to-all-done.1.back_ref, f32[128,768]{1,0:T(8,128)} %get-tuple-element.131.dr1_in, bf16[768,2304]{1,0:T(8,128)(2,1)} %qkv_in.3, f32[16,128]{1,0:T(8,128)S(1)} %get-tuple-element.132.sums_ref), custom_call_target="tpu_custom_call" | custom-call | flops 2000000000 | tf_op jit(solution)/shard_map/input_grad/pallas_call | solution.py:67
  142.9 0.8 collective-permute-start.28
  143.7 3.9 %collective-permute-done.28.refs_6_ = f32[32,768]{1,0:T(8,128)S(1)} collective-permute-done((f32[32,768]{1,0:T(8,128)S(1)}, f32[32,768]{1,0:T(8,128)S(1)}, u32[]{:S(2)}, u32[]{:S(2)}) %collective-permute-start.28) | collective-permute-done | bytes 98336 | tf_op jit(solution)/shard_map/ppermute | solution.py:30
  147.6 0.7 collective-permute-start.17
  148.3 1.0 copy-done.10
  149.4 0.6 copy-done.2
  150.0 0.6 copy-done.4
  150.6 1.3 collective-permute-start.31
  152.0 3.3 %collective-permute-done.17.c_ref = bf16[8,32,288]{2,1,0:T(8,128)(2,1)S(1)} collective-permute-done((bf16[8,32,288]{2,1,0:T(8,128)(2,1)S(1)}, bf16[8,32,288]{2,1,0:T(8,128)(2,1)S(1)}, u32[]{:S(2)}, u32[]{:S(2)}) %collective-permute-start.17) | collective-permute-done | bytes 147488 | tf_op jit(solution)/shard_map/ppermute | solution.py:30
  155.3 0.5 collective-permute-start.30
  155.8 0.9 collective-permute-done.18.d_ref
  156.7 0.9 copy-done.3
  157.6 0.9 copy-done.5
  158.5 1.9 %time_grad.1 = (f32[96,768]{1,0:T(8,128)}, f32[4,96]{1,0:T(4,128)S(1)}, f32[2,96]{1,0:T(2,128)S(1)}, f32[1,384]{1,0:T(1,128)S(1)}) custom-call(bf16[16,768]{1,0:T(8,128)(2,1)} %copy-done.11, bf16[16,768]{1,0:T(8,128)(2,1)} %copy-done.15, bf16[16,768]{1,0:T(8,128)(2,1)} %copy-done.14, bf16[16,768]{1,0:T(8,128)(2,1)} %copy-done.16, ...), custom_call_target="tpu_custom_call" | custom-call | flops 1000000000 | tf_op jit(solution)/shard_map/time_grad/pallas_call | solution.py:67
  160.5 1.5 collective-permute-done.31.c_ref
  162.0 0.5 slice_bitcast_fusion
  162.5 0.6 reduce
  163.1 0.6 fusion.5
  163.7 1.3 finish_heads.1
  165.0 2.1 %finish_all.1 = (f32[96,3072]{1,0:T(8,128)}, f32[384,768]{1,0:T(8,128)}, f32[96,768]{1,0:T(8,128)}) custom-call(bf16[216,768]{1,0:T(8,128)(2,1)S(1)} %combine_all.1.a_ref, bf16[216,768]{1,0:T(8,128)(2,1)S(1)} %collective-permute-done.30.b_ref, bf16[216,768]{1,0:T(8,128)(2,1)S(1)} %collective-permute-done.31.c_ref, ...), custom_call_target="tpu_custom_call" | custom-call | flops 2000000000 | tf_op jit(solution)/shard_map/finish_all/pallas_call | solution.py:67
  (70 shorter events, 2.2 us)
Async XLA Ops:
  0.6 11.9 %copy-start = (bf16[768,768]{1,0:T(8,128)(2,1)S(1)}, bf16[768,768]{1,0:T(8,128)(2,1)}, u32[]{:S(2)}) copy-start(bf16[768,768]{1,0:T(8,128)(2,1)} %param.29) | copy-start | bytes 3538948
  2.4 21.1 %collective-permute-start.3 = (bf16[136,768]{1,0:T(8,128)(2,1)S(1)}, bf16[136,768]{1,0:T(8,128)(2,1)S(1)}, u32[]{:S(2)}, u32[]{:S(2)}) collective-permute-start(bf16[136,768]{1,0:T(8,128)(2,1)S(1)} %fusion.1.refs_0_), channel_id=1, source_target_pairs={{0,16},{4,20},{8,24},{12,28},{16,0},{20,4},{24,8},{28,12},{1,17},{... | collective-permute-start | bytes 626696 | tf_op jit(solution)/shard_map/ppermute | solution.py:30
  6.5 9.9 %collective-permute-start.1 = (bf16[136,768]{1,0:T(8,128)(2,1)S(1)}, bf16[136,768]{1,0:T(8,128)(2,1)S(1)}, u32[]{:S(2)}, u32[]{:S(2)}) collective-permute-start(bf16[136,768]{1,0:T(8,128)(2,1)S(1)} %fusion.1.refs_0_), channel_id=1, source_target_pairs={{0,8},{4,12},{8,0},{12,4},{16,24},{20,28},{24,16},{28,20},{1,9},{5... | collective-permute-start | bytes 626696 | tf_op jit(solution)/shard_map/ppermute | solution.py:30
  8.0 6.3 %collective-permute-start = (bf16[136,768]{1,0:T(8,128)(2,1)S(1)}, bf16[136,768]{1,0:T(8,128)(2,1)S(1)}, u32[]{:S(2)}, u32[]{:S(2)}) collective-permute-start(bf16[136,768]{1,0:T(8,128)(2,1)S(1)} %fusion.1.refs_0_), channel_id=1, source_target_pairs={{0,4},{4,0},{8,12},{12,8},{16,20},{20,16},{24,28},{28,24},{1,5},{5... | collective-permute-start | bytes 626696 | tf_op jit(solution)/shard_map/ppermute | solution.py:30
  12.5 9.4 %copy-start.11 = (bf16[16,768]{1,0:T(8,128)(2,1)}, bf16[16,768]{1,0:T(8,128)(2,1)S(1)}, u32[]{:S(2)}) copy-start(bf16[16,768]{1,0:T(8,128)(2,1)S(1)} %pad_maximum_fusion.refs_0_) | copy-start | bytes 73732
  12.8 14.1 %copy-start.6 = (f32[3072]{0:T(1024)S(1)}, f32[3072]{0:T(1024)}, u32[]{:S(2)}) copy-start(f32[3072]{0:T(1024)} %param.24) | copy-start | bytes 36868
  14.4 9.6 %collective-permute-start.8 = (bf16[16,768]{1,0:T(8,128)(2,1)S(1)}, bf16[16,768]{1,0:T(8,128)(2,1)S(1)}, u32[]{:S(2)}, u32[]{:S(2)}) collective-permute-start(bf16[16,768]{1,0:T(8,128)(2,1)S(1)} %pad_maximum_fusion.refs_0_), channel_id=1, source_target_pairs={{0,2},{1,3},{2,0},{3,1},{4,6},{5,7},{6,4},{7,5},{8,10},{9,11},{10,... | collective-permute-start | bytes 73736 | tf_op jit(solution)/shard_map/ppermute | solution.py:30
  15.9 14.6 %collective-permute-start.7 = (bf16[16,768]{1,0:T(8,128)(2,1)S(1)}, bf16[16,768]{1,0:T(8,128)(2,1)S(1)}, u32[]{:S(2)}, u32[]{:S(2)}) collective-permute-start(bf16[16,768]{1,0:T(8,128)(2,1)S(1)} %pad_maximum_fusion.refs_0_), channel_id=1, source_target_pairs={{0,1},{1,0},{2,3},{3,2},{4,5},{5,4},{6,7},{7,6},{8,9},{9,8},{10,11... | collective-permute-start | bytes 73736 | tf_op jit(solution)/shard_map/ppermute | solution.py:30
  16.4 9.0 %collective-permute-start.5 = (bf16[136,768]{1,0:T(8,128)(2,1)S(1)}, bf16[136,768]{1,0:T(8,128)(2,1)S(1)}, u32[]{:S(2)}, u32[]{:S(2)}) collective-permute-start(bf16[136,768]{1,0:T(8,128)(2,1)S(1)} %fusion.1.refs_0_), channel_id=1, source_target_pairs={{0,24},{4,28},{8,16},{12,20},{16,8},{20,12},{24,0},{28,4},{1,25},{... | collective-permute-start | bytes 626696 | tf_op jit(solution)/shard_map/ppermute | solution.py:30
  21.9 12.6 %collective-permute-start.2 = (bf16[136,768]{1,0:T(8,128)(2,1)S(1)}, bf16[136,768]{1,0:T(8,128)(2,1)S(1)}, u32[]{:S(2)}, u32[]{:S(2)}) collective-permute-start(bf16[136,768]{1,0:T(8,128)(2,1)S(1)} %collective-permute-done.1.refs_2_), channel_id=1, source_target_pairs={{0,4},{4,0},{8,12},{12,8},{16,20},{20,16},{24,28},{28,24},{1,5},{5... | collective-permute-start | bytes 626696 | tf_op jit(solution)/shard_map/ppermute | solution.py:30
  23.5 11.0 %collective-permute-start.4 = (bf16[136,768]{1,0:T(8,128)(2,1)S(1)}, bf16[136,768]{1,0:T(8,128)(2,1)S(1)}, u32[]{:S(2)}, u32[]{:S(2)}) collective-permute-start(bf16[136,768]{1,0:T(8,128)(2,1)S(1)} %collective-permute-done.3.refs_4_), channel_id=1, source_target_pairs={{0,4},{4,0},{8,12},{12,8},{16,20},{20,16},{24,28},{28,24},{1,5},{5... | collective-permute-start | bytes 626696 | tf_op jit(solution)/shard_map/ppermute | solution.py:30
  24.0 6.4 %copy-start.14 = (bf16[16,768]{1,0:T(8,128)(2,1)}, bf16[16,768]{1,0:T(8,128)(2,1)S(1)}, u32[]{:S(2)}) copy-start(bf16[16,768]{1,0:T(8,128)(2,1)S(1)} %collective-permute-done.8.refs_2_) | copy-start | bytes 73732
  24.0 6.5 %collective-permute-start.9 = (bf16[16,768]{1,0:T(8,128)(2,1)S(1)}, bf16[16,768]{1,0:T(8,128)(2,1)S(1)}, u32[]{:S(2)}, u32[]{:S(2)}) collective-permute-start(bf16[16,768]{1,0:T(8,128)(2,1)S(1)} %collective-permute-done.8.refs_2_), channel_id=1, source_target_pairs={{0,1},{1,0},{2,3},{3,2},{4,5},{5,4},{6,7},{7,6},{8,9},{9,8},{10,11... | collective-permute-start | bytes 73736 | tf_op jit(solution)/shard_map/ppermute | solution.py:30
  25.4 12.3 %collective-permute-start.6 = (bf16[136,768]{1,0:T(8,128)(2,1)S(1)}, bf16[136,768]{1,0:T(8,128)(2,1)S(1)}, u32[]{:S(2)}, u32[]{:S(2)}) collective-permute-start(bf16[136,768]{1,0:T(8,128)(2,1)S(1)} %collective-permute-done.5.refs_6_), channel_id=1, source_target_pairs={{0,4},{4,0},{8,12},{12,8},{16,20},{20,16},{24,28},{28,24},{1,5},{5... | collective-permute-start | bytes 626696 | tf_op jit(solution)/shard_map/ppermute | solution.py:30
  26.9 10.8 %copy-start.1 = (bf16[1,128,768]{2,1,0:T(8,128)(2,1)S(1)}, bf16[1,128,768]{2,1,0:T(8,128)(2,1)}, u32[]{:S(2)}) copy-start(bf16[1,128,768]{2,1,0:T(8,128)(2,1)} %param.16) | copy-start | bytes 589828
  26.9 10.8 %copy-start.7 = (f32[2,768]{1,0:T(2,128)S(1)}, f32[2,768]{1,0:T(2,128)}, u32[]{:S(2)}) copy-start(f32[2,768]{1,0:T(2,128)} %refs_14_.1) | copy-start | bytes 18436
  26.9 10.8 %copy-start.8 = (f32[2,768]{1,0:T(2,128)S(1)}, f32[2,768]{1,0:T(2,128)}, u32[]{:S(2)}) copy-start(f32[2,768]{1,0:T(2,128)} %gain_ref.1) | copy-start | bytes 18436
  30.5 7.2 %copy-start.15 = (bf16[16,768]{1,0:T(8,128)(2,1)}, bf16[16,768]{1,0:T(8,128)(2,1)S(1)}, u32[]{:S(2)}) copy-start(bf16[16,768]{1,0:T(8,128)(2,1)S(1)} %collective-permute-done.7.refs_1_) | copy-start | bytes 73732
  30.5 7.1 %copy-start.16 = (bf16[16,768]{1,0:T(8,128)(2,1)}, bf16[16,768]{1,0:T(8,128)(2,1)S(1)}, u32[]{:S(2)}) copy-start(bf16[16,768]{1,0:T(8,128)(2,1)S(1)} %collective-permute-done.9.refs_3_) | copy-start | bytes 73732
  56.0 15.7 %all-to-all-start = ((bf16[8,176,128]{2,1,0:T(8,128)(2,1)}), bf16[8,176,128]{2,1,0:T(8,128)(2,1)S(1)}, u32[]{:S(2)}, u32[]{:S(2)}) async-start(bf16[8,176,128]{2,1,0:T(8,128)(2,1)} %get-tuple-element.121), calls=%async_computation | async-start | bytes 720896 | tf_op jit(solution)/shard_map/all_to_all | solution.py:1027
  61.8 21.0 %collective-permute-start.10 = (bf16[128,2304]{1,0:T(8,128)(2,1)}, bf16[128,2304]{1,0:T(8,128)(2,1)S(1)}, u32[]{:S(2)}, u32[]{:S(2)}) collective-permute-start(bf16[128,2304]{1,0:T(8,128)(2,1)} %get-tuple-element.127), channel_id=1, source_target_pairs={{0,2},{1,3},{2,0},{3,1},{4,6},{5,7},{6,4},{7,5},{8,10},{9,11},{10,... | collective-permute-start | bytes 1769480 | tf_op jit(solution)/shard_map/ppermute | solution.py:30
  62.3 30.0 %collective-permute-start.11 = (bf16[128,2304]{1,0:T(8,128)(2,1)}, bf16[128,2304]{1,0:T(8,128)(2,1)}, u32[]{:S(2)}, u32[]{:S(2)}) collective-permute-start(bf16[128,2304]{1,0:T(8,128)(2,1)} %get-tuple-element.128), channel_id=1, source_target_pairs={{0,4},{4,0},{8,12},{12,8},{16,20},{20,16},{24,28},{28,24},{1,5},{5... | collective-permute-start | bytes 1769480 | tf_op jit(solution)/shard_map/ppermute | solution.py:30
  64.3 28.0 %collective-permute-start.12 = (bf16[128,2304]{1,0:T(8,128)(2,1)}, bf16[128,2304]{1,0:T(8,128)(2,1)}, u32[]{:S(2)}, u32[]{:S(2)}) collective-permute-start(bf16[128,2304]{1,0:T(8,128)(2,1)} %get-tuple-element.129), channel_id=1, source_target_pairs={{0,6},{1,7},{2,4},{3,5},{4,2},{5,3},{6,0},{7,1},{8,14},{9,15},{10,... | collective-permute-start | bytes 1769480 | tf_op jit(solution)/shard_map/ppermute | solution.py:808
  71.7 20.6 %copy-start.12 = (bf16[128,2304]{1,0:T(8,128)(2,1)S(1)}, bf16[128,2304]{1,0:T(8,128)(2,1)}, u32[]{:S(2)}) copy-start(bf16[128,2304]{1,0:T(8,128)(2,1)} %get-tuple-element.141.refs_0_) | copy-start | bytes 1769476
  82.8 15.1 %copy-start.13 = (bf16[128,2304]{1,0:T(8,128)(2,1)}, bf16[128,2304]{1,0:T(8,128)(2,1)S(1)}, u32[]{:S(2)}) copy-start(bf16[128,2304]{1,0:T(8,128)(2,1)S(1)} %collective-permute-done.10.refs_1_) | copy-start | bytes 1769476
  92.3 5.6 %collective-permute-start.19 = (bf16[128,2304]{1,0:T(8,128)(2,1)S(1)}, bf16[128,2304]{1,0:T(8,128)(2,1)}, u32[]{:S(2)}, u32[]{:S(2)}) collective-permute-start(bf16[128,2304]{1,0:T(8,128)(2,1)S(1)} %copy-done.12), channel_id=1, source_target_pairs={{0,1},{1,0},{2,3},{3,2},{4,5},{5,4},{6,7},{7,6},{8,9},{9,8},{10,11... | collective-permute-start | bytes 1769480 | tf_op jit(solution)/shard_map/ppermute | solution.py:30
  92.3 5.6 %collective-permute-start.20 = (bf16[128,2304]{1,0:T(8,128)(2,1)S(1)}, bf16[128,2304]{1,0:T(8,128)(2,1)}, u32[]{:S(2)}, u32[]{:S(2)}) collective-permute-start(bf16[128,2304]{1,0:T(8,128)(2,1)S(1)} %collective-permute-done.10.refs_1_), channel_id=1, source_target_pairs={{0,1},{1,0},{2,3},{3,2},{4,5},{5,4},{6,7},{7,6},{8,9},{9,8},{10,11... | collective-permute-start | bytes 1769480 | tf_op jit(solution)/shard_map/ppermute | solution.py:30
  92.8 5.1 %collective-permute-start.21 = (bf16[128,2304]{1,0:T(8,128)(2,1)}, bf16[128,2304]{1,0:T(8,128)(2,1)}, u32[]{:S(2)}, u32[]{:S(2)}) collective-permute-start(bf16[128,2304]{1,0:T(8,128)(2,1)} %collective-permute-done.11.refs_2_), channel_id=1, source_target_pairs={{0,1},{1,0},{2,3},{3,2},{4,5},{5,4},{6,7},{7,6},{8,9},{9,8},{10,11... | collective-permute-start | bytes 1769480 | tf_op jit(solution)/shard_map/ppermute | solution.py:30
  92.9 5.0 %collective-permute-start.22 = (bf16[128,2304]{1,0:T(8,128)(2,1)}, bf16[128,2304]{1,0:T(8,128)(2,1)}, u32[]{:S(2)}, u32[]{:S(2)}) collective-permute-start(bf16[128,2304]{1,0:T(8,128)(2,1)} %collective-permute-done.12.refs_3_), channel_id=1, source_target_pairs={{0,1},{1,0},{2,3},{3,2},{4,5},{5,4},{6,7},{7,6},{8,9},{9,8},{10,11... | collective-permute-start | bytes 1769480 | tf_op jit(solution)/shard_map/ppermute | solution.py:30
  93.3 40.1 %all-to-all-start.1 = ((bf16[8,384,128]{2,1,0:T(8,128)(2,1)}), bf16[8,384,128]{2,1,0:T(8,128)(2,1)S(1)}, u32[]{:S(2)}, u32[]{:S(2)}) async-start(bf16[8,384,128]{2,1,0:T(8,128)(2,1)} %get-tuple-element.130), calls=%async_computation.1 | async-start | bytes 1572864 | tf_op jit(solution)/shard_map/all_to_all | solution.py:1059
  107.0 23.9 %collective-permute-start.24 = (bf16[2,96,768]{2,1,0:T(8,128)(2,1)S(1)}, bf16[2,96,768]{2,1,0:T(8,128)(2,1)S(1)}, u32[]{:S(2)}, u32[]{:S(2)}) collective-permute-start(bf16[2,96,768]{2,1,0:T(8,128)(2,1)S(1)} %get-tuple-element.149), channel_id=1, source_target_pairs={{0,16},{4,20},{8,24},{12,28},{16,0},{20,4},{24,8},{28,12},{1,17},{... | collective-permute-start | bytes 884744 | tf_op jit(solution)/shard_map/ppermute | solution.py:30
  110.0 20.9 %collective-permute-start.23 = (bf16[2,120,768]{2,1,0:T(8,128)(2,1)S(1)}, bf16[2,120,768]{2,1,0:T(8,128)(2,1)S(1)}, u32[]{:S(2)}, u32[]{:S(2)}) collective-permute-start(bf16[2,120,768]{2,1,0:T(8,128)(2,1)S(1)} %get-tuple-element.148), channel_id=1, source_target_pairs={{0,8},{4,12},{8,0},{12,4},{16,24},{20,28},{24,16},{28,20},{1,9},{5... | collective-permute-start | bytes 1105928 | tf_op jit(solution)/shard_map/ppermute | solution.py:30
  114.2 1.9 %collective-permute-start.13 = (bf16[8,32,288]{2,1,0:T(8,128)(2,1)S(1)}, bf16[8,32,288]{2,1,0:T(8,128)(2,1)S(1)}, u32[]{:S(2)}, u32[]{:S(2)}) collective-permute-start(bf16[8,32,288]{2,1,0:T(8,128)(2,1)S(1)} %get-tuple-element.137), channel_id=1, source_target_pairs={{0,1},{1,0},{2,3},{3,2},{4,5},{5,4},{6,7},{7,6},{8,9},{9,8},{10,11... | collective-permute-start | bytes 442376 | tf_op jit(solution)/shard_map/ppermute | solution.py:30
  114.3 7.8 %collective-permute-start.14 = (bf16[8,32,288]{2,1,0:T(8,128)(2,1)S(1)}, bf16[8,32,288]{2,1,0:T(8,128)(2,1)S(1)}, u32[]{:S(2)}, u32[]{:S(2)}) collective-permute-start(bf16[8,32,288]{2,1,0:T(8,128)(2,1)S(1)} %get-tuple-element.138), channel_id=1, source_target_pairs={{0,2},{1,3},{2,0},{3,1},{4,6},{5,7},{6,4},{7,5},{8,10},{9,11},{10,... | collective-permute-start | bytes 442376 | tf_op jit(solution)/shard_map/ppermute | solution.py:30
  115.1 10.3 %collective-permute-start.15 = (bf16[8,32,288]{2,1,0:T(8,128)(2,1)S(1)}, bf16[8,32,288]{2,1,0:T(8,128)(2,1)S(1)}, u32[]{:S(2)}, u32[]{:S(2)}) collective-permute-start(bf16[8,32,288]{2,1,0:T(8,128)(2,1)S(1)} %get-tuple-element.139), channel_id=1, source_target_pairs={{0,3},{1,2},{2,1},{3,0},{4,7},{5,6},{6,5},{7,4},{8,11},{9,10},{10,... | collective-permute-start | bytes 442376 | tf_op jit(solution)/shard_map/ppermute | solution.py:30
  131.0 0.7 copy-start.9
  131.8 16.5 %collective-permute-start.26 = (bf16[96,768]{1,0:T(8,128)(2,1)S(1)}, bf16[96,768]{1,0:T(8,128)(2,1)S(1)}, u32[]{:S(2)}, u32[]{:S(2)}) collective-permute-start(bf16[96,768]{1,0:T(8,128)(2,1)S(1)} %get-tuple-element.153), channel_id=1, source_target_pairs={{0,8},{4,12},{8,0},{12,4},{16,24},{20,28},{24,16},{28,20},{1,9},{5... | collective-permute-start | bytes 442376 | tf_op jit(solution)/shard_map/ppermute | solution.py:30
  131.8 16.5 %collective-permute-start.25 = (bf16[120,768]{1,0:T(8,128)(2,1)S(1)}, bf16[120,768]{1,0:T(8,128)(2,1)S(1)}, u32[]{:S(2)}, u32[]{:S(2)}) collective-permute-start(bf16[120,768]{1,0:T(8,128)(2,1)S(1)} %get-tuple-element.152), channel_id=1, source_target_pairs={{0,16},{4,20},{8,24},{12,28},{16,0},{20,4},{24,8},{28,12},{1,17},{... | collective-permute-start | bytes 552968 | tf_op jit(solution)/shard_map/ppermute | solution.py:30
  133.4 14.1 %all-to-all-start.2 = ((bf16[8,32,288]{2,1,0:T(8,128)(2,1)}), bf16[8,32,288]{2,1,0:T(8,128)(2,1)S(1)}, u32[]{:S(2)}, u32[]{:S(2)}) async-start(bf16[8,32,288]{2,1,0:T(8,128)(2,1)} %combine.1), calls=%async_computation.2 | async-start | bytes 393216 | tf_op jit(solution)/shard_map/all_to_all | solution.py:1079
  142.9 4.7 %collective-permute-start.28 = (f32[32,768]{1,0:T(8,128)S(1)}, f32[32,768]{1,0:T(8,128)S(1)}, u32[]{:S(2)}, u32[]{:S(2)}) collective-permute-start(f32[32,768]{1,0:T(8,128)S(1)} %get-tuple-element.165.refs_4_), channel_id=1, source_target_pairs={{0,2},{1,3},{2,0},{3,1},{4,6},{5,7},{6,4},{7,5},{8,10},{9,11},{10,... | collective-permute-start | bytes 294920 | tf_op jit(solution)/shard_map/ppermute | solution.py:30
  143.7 5.7 %collective-permute-start.27 = (f32[32,768]{1,0:T(8,128)S(1)}, f32[32,768]{1,0:T(8,128)S(1)}, u32[]{:S(2)}, u32[]{:S(2)}) collective-permute-start(f32[32,768]{1,0:T(8,128)S(1)} %get-tuple-element.165.refs_4_), channel_id=1, source_target_pairs={{0,1},{1,0},{2,3},{3,2},{4,5},{5,4},{6,7},{7,6},{8,9},{9,8},{10,11... | collective-permute-start | bytes 294920 | tf_op jit(solution)/shard_map/ppermute | solution.py:30
  147.6 2.4 %collective-permute-start.29 = (f32[32,768]{1,0:T(8,128)S(1)}, f32[32,768]{1,0:T(8,128)S(1)}, u32[]{:S(2)}, u32[]{:S(2)}) collective-permute-start(f32[32,768]{1,0:T(8,128)S(1)} %collective-permute-done.28.refs_6_), channel_id=1, source_target_pairs={{0,1},{1,0},{2,3},{3,2},{4,5},{5,4},{6,7},{7,6},{8,9},{9,8},{10,11... | collective-permute-start | bytes 294920 | tf_op jit(solution)/shard_map/ppermute | solution.py:30
  147.6 7.7 %collective-permute-start.17 = (bf16[8,32,288]{2,1,0:T(8,128)(2,1)S(1)}, bf16[8,32,288]{2,1,0:T(8,128)(2,1)S(1)}, u32[]{:S(2)}, u32[]{:S(2)}) collective-permute-start(bf16[8,32,288]{2,1,0:T(8,128)(2,1)S(1)} %all-to-all-done.2.a_ref), channel_id=1, source_target_pairs={{0,2},{1,3},{2,0},{3,1},{4,6},{5,7},{6,4},{7,5},{8,10},{9,11},{10,... | collective-permute-start | bytes 442376 | tf_op jit(solution)/shard_map/ppermute | solution.py:30
  148.3 1.0 copy-start.10
  149.4 0.6 copy-start.2
  150.0 0.6 copy-start.4
  150.6 11.4 %collective-permute-start.31 = (bf16[216,768]{1,0:T(8,128)(2,1)S(1)}, bf16[216,768]{1,0:T(8,128)(2,1)S(1)}, u32[]{:S(2)}, u32[]{:S(2)}) collective-permute-start(bf16[216,768]{1,0:T(8,128)(2,1)S(1)} %combine_all.1.a_ref), channel_id=1, source_target_pairs={{0,2},{1,3},{2,0},{3,1},{4,6},{5,7},{6,4},{7,5},{8,10},{9,11},{10,... | collective-permute-start | bytes 995336 | tf_op jit(solution)/shard_map/ppermute | solution.py:30
  152.0 3.8 %collective-permute-start.16 = (bf16[8,32,288]{2,1,0:T(8,128)(2,1)S(1)}, bf16[8,32,288]{2,1,0:T(8,128)(2,1)S(1)}, u32[]{:S(2)}, u32[]{:S(2)}) collective-permute-start(bf16[8,32,288]{2,1,0:T(8,128)(2,1)S(1)} %all-to-all-done.2.a_ref), channel_id=1, source_target_pairs={{0,1},{1,0},{2,3},{3,2},{4,5},{5,4},{6,7},{7,6},{8,9},{9,8},{10,11... | collective-permute-start | bytes 442376 | tf_op jit(solution)/shard_map/ppermute | solution.py:30
  155.3 1.4 collective-permute-start.18
  155.3 8.4 %collective-permute-start.30 = (bf16[216,768]{1,0:T(8,128)(2,1)S(1)}, bf16[216,768]{1,0:T(8,128)(2,1)S(1)}, u32[]{:S(2)}, u32[]{:S(2)}) collective-permute-start(bf16[216,768]{1,0:T(8,128)(2,1)S(1)} %combine_all.1.a_ref), channel_id=1, source_target_pairs={{0,1},{1,0},{2,3},{3,2},{4,5},{5,4},{6,7},{7,6},{8,9},{9,8},{10,11... | collective-permute-start | bytes 995336 | tf_op jit(solution)/shard_map/ppermute | solution.py:30
  156.7 0.9 copy-start.3
  157.6 0.9 copy-start.5
  162.0 1.7 %collective-permute-start.32 = (bf16[216,768]{1,0:T(8,128)(2,1)S(1)}, bf16[216,768]{1,0:T(8,128)(2,1)S(1)}, u32[]{:S(2)}, u32[]{:S(2)}) collective-permute-start(bf16[216,768]{1,0:T(8,128)(2,1)S(1)} %collective-permute-done.31.c_ref), channel_id=1, source_target_pairs={{0,1},{1,0},{2,3},{3,2},{4,5},{5,4},{6,7},{7,6},{8,9},{9,8},{10,11... | collective-permute-start | bytes 995336 | tf_op jit(solution)/shard_map/ppermute | solution.py:30
where the time goes:
time: 168 us; the launch traced here: 167 us
  Pallas kernels  65 us (39%)
  waiting for transfers between devices  46 us (27%)
  starting transfers between devices  43.7 us (26%)
  local copies, waits for them, and re-layouts  7.94 us (5%)
  other arithmetic  3.14 us (2%)
    pallas_call x15, Pallas kernels, call(): pl.pallas_call(kernel, out_shape=tuple(((pltpu.HBM if FAR in one else plt...  65 us
    ppermute x32, waiting for transfers between devices, swap(): lax.ppermute(block, axis, [(i, i ^ bit) for i in range(lax.axis_size(axis...  43.7 us
    ppermute x32, starting transfers between devices, swap(): lax.ppermute(block, axis, [(i, i ^ bit) for i in range(lax.axis_size(axis...  27.6 us
    all_to_all x1, starting transfers between devices, body(): arrived = lax.all_to_all(gate('DA', packed), 'seq', 0, 0, tiled=True)  5.78 us
    all_to_all x1, starting transfers between devices, body(): spread = lax.all_to_all(gate('GA2A', mine), 'seq', 0, 0, tiled=True)  4.82 us
    unnamed x34, local copies, waits for them, and re-layouts  4.78 us
    all_to_all x1, starting transfers between devices, body(): back = lax.all_to_all(gate('BACK', back), 'seq', 0, 0, tiled=True)  4.54 us
  transfers between devices with their start and end apart: 36, of which 14 were waited for; matrix products, arithmetic and copies ran while one was open for 3% of the time, Pallas kernels for 26%

commit v1 on v0

--- a/solution.py
+++ b/solution.py
@@ -121,7 +121,7 @@
     return jnp.concatenate([jnp.sin(phases), jnp.cos(phases)], axis=-1)
 
 
-def gather_seq(block, known, gate):
+def gather_seq(block, known, gate, meanwhile):
     size = lax.axis_size("seq")
     inner = size // Z_STEPS
     found = [None] * size
@@ -131,6 +131,8 @@
         found[far * inner] = swap(gate(name, block), "seq", far * inner)
         known[name] = found[far * inner]
     for far in range(Z_STEPS):
+        if far == 2:
+            meanwhile()
         name = "Y%d" % far
         held = gate(name, found[far * inner])
         for near in range(1, inner):
@@ -140,23 +142,20 @@
 
 
 ORDER = {
+    "Etwin": ("part", ),
+    "RS1": ("feed", "part", ),
+    "all": ("AGG", "time", ),
+    "backward": ("Y3", "forward", ),
     "fetch": ("Y0", ),
-    "part": ("Z1", ),
-    "feat": ("Y0", ),
-    "Z3": ("Z1", ),
-    "backward": ("forward", ),
+    "finf": ("finh", ),
+    "forward": ("Y3", ),
+    "half": ("DOCS", "in", ),
     "head": ("heads", ),
-    "Etwin": ("head", ),
-    "headend": ("E", ),
-    "half": ("hw", ),
-    "all": ("GA2A", "in", ),
-    "finh": ("AGF", ),
-    "AGF": ("DOCS", ),
-    "time": ("AGG", ),
+    "part": ("E0", "head", ),
 }
 COSTS = {
     "fetch": 7, "forward": 12, "backward": 5, "heads": 3, "part_weights": 3, "feed_grad": 8,
-    "head_grad": 9, "head_weights": 2, "input_grad": 2, "combine": 1, "combine_half": 1,
+    "head_grad": 12, "input_grad": 5, "combine_half": 1,
     "combine_all": 1, "finish_all": 2, "finish_heads": 1, "time_grad": 1,
 }
 
@@ -416,19 +415,20 @@
     wait(moved)
 
 
-def head_grad_kernel(step, share, *refs):
-    w_in, q_in, k_in, v_in, hot_in, docs_in, da_ref = refs[:7]
-    back_ref, heads_out, bias_ref, sums_ref = refs[7:11]
-    refs = refs[1:]
-    w_ref, q_ref, k_ref, v_ref, hot_ref, docs_ref = refs[10:16]
-    dq_ref, dk_ref, dv_ref, heads_ref, sems = refs[16:]
+def head_grad_kernel(step, share, split, *refs):
+    w_in, q_in, k_in, v_in, hot_in, docs_in, x_in, da_ref, back_ref, sums_ref = refs[:10]
+    w_ref, q_ref, k_ref, v_ref, hot_ref, docs_ref, x_ref = refs[-13:-6]
+    dq_ref, dk_ref, dv_ref, heads_ref, grad_ref, sems = refs[-6:]
+    outs = refs[10:-13]
+    if split:
+        *outs, own_ref = outs
     length = q_ref.shape[0]
     rows = length // (D // share)
     seq = lax.axis_index("seq")
     loads = copies(
         (
             (hot_in, hot_ref), (v_in, v_ref), (k_in, k_ref), (q_in, q_ref),
-            (w_in, w_ref), (docs_in, docs_ref),
+            (w_in, w_ref), (docs_in, docs_ref), (x_in, x_ref),
         ),
         sems,
         0,
@@ -475,9 +475,7 @@
             [pltpu.roll(ref[piece, :], left, 1)[:, :share] for ref in (dq_ref, dk_ref, dv_ref)],
             axis=1,
         ).astype(BF)
-    moved = copy(heads_ref, heads_out, sems, 6)
     doc_sums = nn(hot_ref[...], heads_ref[...])
-    bias_ref[...] = total(doc_sums)
     docs = docs_ref[...]
     for kind in range(3):
         piece = doc_sums[:, kind * share : (kind + 1) * share]
@@ -506,64 +504,72 @@
             back_ref[at, extra + col * DOCS : extra + (col + 1) * DOCS, :] = docs[
                 :, col * PAIR : (col + 1) * PAIR
             ]
-    moved.wait()
-
-
-def head_weights_kernel(share, split, x_in, heads_in, bias_ref, *refs):
-    outs, (x_ref, heads_ref, grad_ref, sems) = refs[:-4], refs[-4:]
-    wait(copies(((heads_in, heads_ref), (x_in, x_ref)), sems, 0))
     if not split:
         outs[0][...] = tn(x_ref[...], heads_ref[...])
+        outs[1][...] = total(doc_sums)
         return
-    *sent, mine_ref = outs
+    *sent, mine_out = outs
     grad_ref[...] = tn(x_ref[...], heads_ref[...])
     rank = lax.axis_index("rows")
     part = share // split
-    high, low = split2(jnp.broadcast_to(bias_ref[...], (8, 3 * share)))
+    high, low = split2(jnp.broadcast_to(total(doc_sums), (8, 3 * share)))
     row = lax.broadcasted_iota(jnp.int32, (8, 3 * share), 0)
     tail = jnp.where(row == 0, high.astype(F32), jnp.where(row == 1, low.astype(F32), 0.0))
-    for to, ref in enumerate([mine_ref] + list(sent)):
+    for to, ref in enumerate([own_ref] + list(sent)):
         for at in range(D // share):
             here = pl.ds(pl.multiple_of(at * share + (rank ^ to) * part, 8), part)
             ref[at, :part, :] = grad_ref[here, :].astype(ref.dtype)
             ref[at, part:, :] = tail.astype(ref.dtype)
-
-
-def head_grad(apart, da, share):
+        if to == 0:
+            moved = copy(own_ref, mine_out, sems, 7)
+    moved.wait()
+
+
+def head_grad(apart, da, share, split):
     length = apart[1].shape[0]
     count = D // share
     rows = length // count
-    outs = [((count, rows * 3 * share // PAIR + 6 * DOCS, PAIR), BF)]
-    outs += [((length, 3 * share), BF, FAR), ((1, 3 * share), F32), ((SUMS, rows), F32)]
-    scratch = [(one.shape, one.dtype) for one in apart] + [((length, PAIR), F32)] * 3
-    scratch += [((length, 3 * share), BF)]
+    outs = [((count, rows * 3 * share // PAIR + 6 * DOCS, PAIR), BF), ((SUMS, rows), F32)]
+    if split:
+        block = (count, share // split + 8, 3 * share)
+        outs += [(block, BF)] * (split - 1) + [(block, F32, FAR)]
+    else:
+        outs += [((D, 3 * share), F32), ((1, 3 * share), F32)]
+    scratch = [(block, F32)] if split else []
+    scratch += [(one.shape, one.dtype) for one in apart] + [((length, PAIR), F32)] * 3
+    scratch += [((length, 3 * share), BF), ((D, 3 * share), F32)]
     return call(
-        functools.partial(head_grad_kernel, 512, share),
+        functools.partial(head_grad_kernel, 512, share, split),
         "head_grad",
         (*(far(one) for one in apart), da),
         outs,
         scratch,
-        20 if length <= 1024 else 40,
-        7,
-    )
-
-
-def head_weights(x_low, heads, bias, share, split):
-    block = (D // share, share // split + 8, 3 * share) if split else (D, 3 * share)
-    return call(
-        functools.partial(head_weights_kernel, share, split),
-        "head_weights",
-        (far(x_low), far(heads), bias),
-        [(block, BF)] * (split - 1) + [(block, F32)] if split else [(block, F32)],
-        [(x_low.shape, BF), (heads.shape, BF), ((D, 3 * share), F32)],
-        16,
-        2,
-    )
-
-
-def input_grad_kernel(
-    share, back_ref, dr1_in, qkv_in, sums_ref, grad_ref, docs_ref, dr1_ref, qkv_ref, sems
-):
+        24 if length <= 1024 else 44,
+        8,
+    )
+
+
+def combine(blocks, out_ref):
+    value = blocks[0][...]
+    for ref in blocks[1:]:
+        value = value + ref[...].astype(F32)
+    count, rows, wide = value.shape
+    out_ref[:, : rows - 8, :] = value[:, : rows - 8].astype(out_ref.dtype)
+    row = lax.broadcasted_iota(jnp.int32, (8, wide), 0)
+    for at in range(count):
+        last = value[at, rows - 8 :]
+        high, low = split2(jnp.broadcast_to(last[0:1] + last[1:2], (8, wide)))
+        out_ref[at, rows - 8 :, :] = jnp.where(
+            row == 0, high.astype(F32), jnp.where(row == 1, low.astype(F32), 0.0)
+        ).astype(out_ref.dtype)
+
+
+def input_grad_kernel(share, back_ref, dr1_in, qkv_in, sums_ref, *refs):
+    blocks = ()
+    if len(refs) > 5:
+        blocks, held, refs = refs[:4], refs[-5:-1], refs[4:-5] + refs[-1:]
+    grad_ref, docs_ref, *mine_ref, dr1_ref, qkv_ref, sems = refs
+    blocks = copies(zip(blocks, held), sems, 4) if blocks else ()
     loads = copies(
         [(qkv_in.at[:, c], qkv_ref.at[:, c]) for c in [slice(i * D, i * D + D) for i in range(3)]],
         sems,
@@ -600,37 +606,48 @@
         loads[kind].wait()
         result = result + nt(jnp.concatenate(kinds[kind], axis=1), qkv_ref[:, cols])
     grad_ref[...] = result
+    if blocks:
+        wait(blocks)
+        combine(held, mine_ref[0])
 
 
 def unit_share(at):
     return 2 * (at % 4) + at // 4
 
 
-def part_weights_kernel(up_near, bu_ref, up_out, bu_out, up_ref, sems):
+def part_weights_kernel(up_in, bu_ref, up_out, bu_out, held_ref, up_ref, sems):
     back = (384 - lax.axis_index("rows") * 96) % 384
+    loads = copies(
+        [
+            (up_in.at[:, unit_share(at) * 384 : (unit_share(at) + 1) * 384], held_ref.at[at])
+            for at in range(8)
+        ],
+        sems,
+        0,
+    )
     ups, biases = [], []
     for at in range(8):
         cols = slice(unit_share(at) * 384, (unit_share(at) + 1) * 384)
-        ups.append(pltpu.roll(up_near[:, cols].astype(F32), back, 1)[:, :96].astype(BF))
+        loads[at].wait()
+        ups.append(pltpu.roll(held_ref[at].astype(F32), back, 1)[:, :96].astype(BF))
         bias = jnp.broadcast_to(bu_ref[:, cols], (8, 384))
         biases.append(pltpu.roll(bias, back, 1)[:1, :96])
     up_ref[...] = jnp.concatenate(ups, axis=1)
-    moved = copy(up_ref, up_out, sems, 0)
+    moved = copy(up_ref, up_out, sems, 8)
     bu_out[...] = jnp.concatenate(biases, axis=1)
     moved.wait()
 
 
 def feed_grad_kernel(*refs):
     pieces = refs[:8]
-    up_in, bu_ref, down_in, up_own_ref, up_sent_ref, down_own_ref, down_sent_ref = refs[8:15]
-    y1_ref, df_ref, up_ref, down_ref, g_ref, du_ref, attn_ref, do_ref = refs[15:23]
-    up_grad_ref, down_grad_ref, out_grad_ref, sems = refs[23:]
+    up_in, bu_ref, down_in, up_own_out, up_sent_ref, down_own_out, down_sent_ref = refs[8:15]
+    all_ref, up_ref, down_ref, g_ref, du_ref = refs[15:20]
+    up_grad_ref, down_grad_ref, out_grad_ref, up_own_ref, down_own_ref, sems = refs[20:]
     seq, rank = lax.axis_index("seq"), lax.axis_index("rows")
     near, z = seq % 2, seq // 2
     rows = pieces[0].shape[0]
-    here = [slice(at * rows, (at + 1) * rows) for at in range(8)]
-    loads = [copy(up_in, up_ref, sems, 16)]
-    loads += copies([(piece.at[:, :D], y1_ref.at[r, :]) for piece, r in zip(pieces, here)], sems, 0)
+    loads = [copy(up_in, up_ref, sems, 8)]
+    loads += copies([(pieces[at], all_ref.at[at]) for at in range(2)], sems, 0)
     first = rank * 96
     downs = copies(
         [
@@ -641,33 +658,32 @@
             for at in range(8)
         ],
         sems,
-        17,
-    )
-    grads = copies([(piece.at[:, D : 2 * D], df_ref.at[r, :]) for piece, r in zip(pieces, here)], sems, 8)
+        9,
+    )
+    loads += copies([(pieces[at], all_ref.at[at]) for at in range(2, 8)], sems, 2)
+    loads[0].wait()
+    step = 2 * rows
+    for at in range(4):
+        wait(loads[1 + 2 * at : 3 + 2 * at])
+        piece = slice(at * step, (at + 1) * step)
+        two = slice(2 * at, 2 * at + 2)
+        u = nn(all_ref[two, :, :D].reshape(step, D), up_ref[...]) + bu_ref[...]
+        phi, slope = gelu_parts(u)
+        if at == 0:
+            wait(downs)
+        g_ref[piece, :] = (u * phi).astype(BF)
+        df = all_ref[two, :, D : 2 * D].reshape(step, D)
+        du_ref[piece, :] = (nt(df, down_ref[...]) * slope).astype(BF)
+
+    tokens = 8 * rows
+    df = all_ref[:, :, D : 2 * D].reshape(tokens, D)
+    down_grad_ref[...] = tn(g_ref[:, at_lanes(near, 384)], df)
+    up_grad_ref[...] = tn(all_ref[:, :, :D].reshape(tokens, D), du_ref[...])
     base = pl.multiple_of(2 * D + D // 2 + (rank % 2) * 128, 128)
-    attns = slice(2 * D, 2 * D + D // 2)
-    outs = copies([(piece.at[:, attns], attn_ref.at[r, :]) for piece, r in zip(pieces, here)], sems, 25)
-    outs += copies(
-        [(piece.at[:, pl.ds(base, 256)], do_ref.at[r, :]) for piece, r in zip(pieces, here)], sems, 33
-    )
-    step = 2 * rows
-    wait(loads)
-    wait(downs)
-    wait(grads)
-
-    @functools.partial(loop, 4)
-    def _(at):
-        piece = at_rows(at, step)
-        u = nn(y1_ref[piece, :], up_ref[...]) + bu_ref[...]
-        phi, slope = gelu_parts(u)
-        g_ref[piece, :] = (u * phi).astype(BF)
-        du_ref[piece, :] = (nt(df_ref[piece, :], down_ref[...]) * slope).astype(BF)
-
-    down_grad_ref[...] = tn(g_ref[:, at_lanes(near, 384)], df_ref[...])
-    up_grad_ref[...] = tn(y1_ref[...], du_ref[...])
-    wait(outs)
+    attn = all_ref[:, :, 2 * D : 2 * D + D // 2].reshape(tokens, D // 2)
+    do = all_ref[:, :, pl.ds(base, 256)].reshape(tokens, 256)
     back = (256 - (rank % 2) * 64) % 256
-    out_grad_ref[...] = pltpu.roll(tn(attn_ref[...], do_ref[...]), back, 1)
+    out_grad_ref[...] = pltpu.roll(tn(attn, do), back, 1)
     for to in range(4):
         up_rows = pl.ds(pl.multiple_of((2 * (z ^ to) + near) * 96, 8), 96)
         down_rows = pl.ds(pl.multiple_of((z ^ to) * 96, 8), 96)
@@ -679,6 +695,7 @@
         ).astype(ref.dtype)
         ref = down_own_ref.at[to % 2] if to < 2 else down_sent_ref.at[to % 2]
         ref[...] = down_grad_ref[down_rows, :].astype(ref.dtype)
+    wait(copies(((up_own_ref, up_own_out), (down_own_ref, down_own_out)), sems, 17))
 
 
 def feed_grad(pieces, up, bias, down):
@@ -689,25 +706,33 @@
         feed_grad_kernel,
         "feed_grad",
         (*(far(one) for one in pieces), far(up), bias, far(down)),
-        [(block, dtype) for block in blocks for dtype in (F32, BF)],
+        [one for block in blocks for one in ((block, F32, FAR), (block, BF))],
         [
-            wide, wide, ((D, D), BF), ((D, D), BF), wide, wide, ((tokens, D // 2), BF),
-            ((tokens, 256), BF), ((D, D), F32), ((384, D), F32), ((384, 256), F32),
+            ((8, tokens // 8, 3 * D), BF), ((D, D), BF), ((D, D), BF), wide, wide,
+            ((D, D), F32), ((384, D), F32), ((384, 256), F32),
+            *((block, F32) for block in blocks),
         ],
-        26,
-        41,
-    )
-
-
-def combine_half_kernel(*refs):
-    for own_ref, got_ref, mine_ref, sent_ref in (refs[0::2], refs[1::2]):
-        mine_ref[...] = own_ref[0] + got_ref[0].astype(F32)
-        sent_ref[...] = (own_ref[1] + got_ref[1].astype(F32)).astype(BF)
-
-
-def combine_all_kernel(up_ref, down_ref, up_got_ref, down_got_ref, out_ref):
-    out_ref[:120, :] = (up_ref[...] + up_got_ref[...].astype(F32)).astype(BF)
-    out_ref[120:, :] = (down_ref[...] + down_got_ref[...].astype(F32)).astype(BF)
+        28,
+        19,
+    )
+
+
+def combine_half_kernel(up_in, down_in, up_got_in, down_got_in, up_ref, down_ref, *refs):
+    *held, sems = refs
+    loads = copies(zip((up_in, down_in, up_got_in, down_got_in), held), sems, 0)
+    wait(loads)
+    up_ref[...] = (held[0][1] + held[2][1].astype(F32)).astype(BF)
+    down_ref[...] = (held[1][1] + held[3][1].astype(F32)).astype(BF)
+
+
+def combine_all_kernel(up_in, down_in, up_got_in, down_got_in, up_last_ref, down_last_ref, out_ref, *refs):
+    *held, sems = refs
+    sources = [one.at[0] for one in (up_in, down_in, up_got_in, down_got_in)]
+    wait(copies(zip(sources, held), sems, 0))
+    up = held[0][...] + held[2][...].astype(F32) + up_last_ref[...].astype(F32)
+    down = held[1][...] + held[3][...].astype(F32) + down_last_ref[...].astype(F32)
+    out_ref[:120, :] = up.astype(BF)
+    out_ref[120:, :] = down.astype(BF)
 
 
 def finish_all_kernel(a_ref, b_ref, c_ref, d_ref, up_ref, down_ref, out_ref, held_ref):
@@ -759,30 +784,6 @@
     sums = jnp.concatenate([sums[:, :D], sums[:, 2 * D :]], axis=1)
     back = (2 * D - lax.axis_index("seq") * 192) % (2 * D)
     bias_ref[...] = pltpu.roll(jnp.broadcast_to(sums, (8, 2 * D)), back, 1)[:1, :192]
-
-
-def combine_kernel(tail, own_ref, a_ref, b_ref, c_ref, out_ref):
-    value = own_ref[...]
-    for ref in (a_ref, b_ref, c_ref):
-        value = value + ref[...].astype(F32)
-    if tail:
-        count, rows, wide = value.shape
-        out_ref[:, : rows - 8, :] = value[:, : rows - 8].astype(out_ref.dtype)
-        row = lax.broadcasted_iota(jnp.int32, (8, wide), 0)
-        for at in range(count):
-            last = value[at, rows - 8 :]
-            high, low = split2(jnp.broadcast_to(last[0:1] + last[1:2], (8, wide)))
-            out_ref[at, rows - 8 :, :] = jnp.where(
-                row == 0, high.astype(F32), jnp.where(row == 1, low.astype(F32), 0.0)
-            ).astype(out_ref.dtype)
-    else:
-        out_ref[...] = value.astype(out_ref.dtype)
-
-
-def combine(blocks, dtype, tail=False):
-    return call(
-        functools.partial(combine_kernel, tail), "combine", blocks, [(blocks[0].shape, dtype)]
-    )[0]
 
 
 def after(value, *others):
@@ -943,47 +944,36 @@
     fast = seqs == 8 and ranks == 4
     starts = [min(i * share // HD, H - 2) * HD for i in range(seqs)]
 
+    known, gate = gates(ORDER if fast else {})
+    features = time_features(timesteps[0]).astype(BF)
+    up_row = up_bias.reshape(1, -1)
+    weights = [((D, 3 * D), BF), ((D, D), BF), ((D, FF), BF), ((FF, D), BF)]
+
+    def meanwhile():
+        known["weights"] = call(
+            fetch_kernel,
+            "fetch",
+            (far(gate("fetch", qkv_weight)), far(out_weight), far(up_weight), far(down_weight)),
+            [(*one, NEAR) for one in weights],
+            (),
+            2,
+            4,
+        )
+        known["fetch"] = known["weights"][1]
+
     ids = jnp.pad(segment_ids.astype(BF), ((0, 7), (0, D - rows)))
-    known, gate = gates(ORDER if fast else {})
-    shards = gather_seq(jnp.concatenate([hidden[0], ids], axis=0), known, gate)
-
-    features = time_features(timesteps[0]).astype(BF)
+    shards = gather_seq(jnp.concatenate([hidden[0], ids], axis=0), known, gate, meanwhile)
+    qkv_near, out_near, up_near, down_near = known["weights"]
     embed = nn(features, time_weight)
-    if fast:
-        all_features = spread_rows(gate("feat", features))
-        known["feat"] = all_features[1:]
-    else:
+    if not fast:
         all_features = gather_rows(features, rank)
         all_features = lax.dynamic_slice_in_dim(all_features, seq * share, share, 2)
-    qv_row, up_row = qv_bias.reshape(1, -1), up_bias.reshape(1, -1)
+    qv_row = qv_bias.reshape(1, -1)
     tile = ((rows, D), BF)
     tile32 = ((rows, D), F32)
     narrow32 = ((rows, 128), F32)
     wide = ((length, D), BF)
-    weights = [((D, 3 * D), BF), ((D, D), BF), ((D, FF), BF), ((FF, D), BF)]
-    qkv_near, out_near, up_near, down_near = call(
-        fetch_kernel,
-        "fetch",
-        (far(gate("fetch", qkv_weight)), far(out_weight), far(up_weight), far(down_weight)),
-        [(*one, NEAR) for one in weights],
-        (),
-        2,
-        4,
-    )
     out_row, down_row = out_bias.reshape(1, -1), down_bias.reshape(1, -1)
-    known["fetch"] = out_near
-    if fast:
-        up_part, bias_part = call(
-            part_weights_kernel,
-            "part_weights",
-            (up_near, gate("part", up_row)),
-            [((D, D), BF, FAR), ((1, D), F32)],
-            [((D, D), BF)],
-            14,
-            1,
-        )
-        known["part"] = bias_part
-        embed = after(embed, bias_part, all_features)
     x_low, lse, attn, hot, z1, inverse1, result, ydf, dr2, slope, z2_sum = call(
         functools.partial(forward_kernel, seqs),
         "forward",
@@ -1024,8 +1014,6 @@
     )
     known["backward"] = packed
 
-    arrived = lax.all_to_all(gate("DA", packed), "seq", 0, 0, tiled=True)
-    known["DA"] = arrived
     pair = ((length, PAIR), BF)
     head_shape = ((D, 3 * PAIR), BF)
     q_two, k_two, v_two, head_weight = call(
@@ -1041,14 +1029,34 @@
     if fast:
         near_all = from_chips(*gate("E", ado))
         known["E"] = near_all[1:]
-    back, heads, head_sums, sums = head_grad(
-        (head_weight, q_two, k_two, v_two, hot, docs), gate("head", arrived), share
-    )
-    back, heads, head_sums, sums = gate("headend", (back, heads, head_sums, sums))
+        own_twin = swap(gate("E0", near_all[0]), "rows", 1)
+        known["E0"] = own_twin
+    arrived = lax.all_to_all(gate("DA", packed), "seq", 0, 0, tiled=True)
+    known["DA"] = arrived
+    back, sums, *grads = gate(
+        "headend",
+        head_grad(
+            (head_weight, q_two, k_two, v_two, hot, docs, x_low), gate("head", arrived), share,
+            4 if fast else 0,
+        ),
+    )
     known["head"] = back
     if fast:
-        near_all = with_twin(gate("Etwin", near_all))
-        known["Etwin"] = near_all[4:]
+        up_part, bias_part = call(
+            part_weights_kernel,
+            "part_weights",
+            (far(up_weight), gate("part", up_row)),
+            [((D, D), BF, FAR), ((1, D), F32)],
+            [((8, D, 384), BF), ((D, D), BF)],
+            14,
+            9,
+        )
+        known["part"] = bias_part
+        all_features = spread_rows(gate("feat", features))
+        known["feat"] = all_features[1:]
+        twins = with_twin(gate("Etwin", near_all[1:]))
+        near_all = [near_all[0], own_twin, *twins]
+        known["Etwin"] = twins[3:]
         up_own, up_sent, down_own, down_sent = feed_grad(
             near_all, up_part, gate("feed", bias_part), down_weight
         )
@@ -1058,49 +1066,40 @@
         known["RS1"] = (up_got, down_got)
     back = lax.all_to_all(gate("BACK", back), "seq", 0, 0, tiled=True)
     known["BACK"] = back
-    if fast:
-        up_got, down_got = gate("half", (up_got, down_got))
-        up_mine, down_mine, up_sent, down_sent = call(
-            combine_half_kernel, "combine_half", (up_own, down_own, up_got, down_got),
-            [((120, D), F32), ((96, D), F32), ((120, D), BF), ((96, D), BF)],
-        )
-        known["half"] = up_mine
-        up_sent, down_sent = gate("RS2", (up_sent, down_sent))
-        up_got, down_got = swap(up_sent, "seq", 4), swap(down_sent, "seq", 2)
-        known["RS2"] = (up_got, down_got)
-    grads = head_weights(x_low, heads, gate("hw", head_sums), share, 4 if fast else 0)
-    known["hw"] = grads
+    blocks, mines = (), ()
     if fast:
         *sent, own = gate("GRS", grads)
         sent = [swap(block, "rows", to + 1) for to, block in enumerate(sent)]
         known["GRS"] = sent
-        mine = combine((own, *gate("gc", sent)), BF, True)
-        known["gc"] = mine
-        spread = lax.all_to_all(gate("GA2A", mine), "seq", 0, 0, tiled=True)
-        known["GA2A"] = spread
-    input_grad, doc_grad = call(
+        blocks, mines = (own, *sent), ((own.shape, BF),)
+    input_grad, doc_grad, *mine = call(
         functools.partial(input_grad_kernel, share),
         "input_grad",
-        (gate("in", back), far(dr1), far(qkv_weight), sums),
-        [tile32, ((DOCS + SUMS, D), F32)],
-        [tile32, ((D, 3 * D), BF)],
-        10,
-        4,
+        (gate("in", back), far(dr1), far(qkv_weight), sums, *(far(one) for one in blocks)),
+        [tile32, ((DOCS + SUMS, D), F32), *mines],
+        [tile32, ((D, 3 * D), BF), *((one.shape, one.dtype) for one in blocks)],
+        12,
+        8,
     )
     known["in"] = input_grad
     if fast:
+        spread = lax.all_to_all(gate("GA2A", mine[0]), "seq", 0, 0, tiled=True)
+        known["GA2A"] = spread
         docs_all = spread_rows(gate("DOCS", doc_grad))
         known["DOCS"] = docs_all[1:]
-        up_got, down_got = gate("all", (up_got, down_got))
-        merged = call(
-            combine_all_kernel, "combine_all", (up_mine, down_mine, up_got, down_got),
-            [((216, D), BF)],
-        )[0]
-        known["all"] = merged
-        feed_all = spread_rows(gate("AGF", merged))
-        known["AGF"] = feed_all[1:]
-        heads_all = spread_rows(gate("AGG", spread))
-        known["AGG"] = heads_all[1:]
+        up_got, down_got = gate("half", (up_got, down_got))
+        halves = [far(one) for one in (up_own, down_own, up_got, down_got)]
+        up_sent, down_sent = call(
+            combine_half_kernel, "combine_half", halves,
+            [((120, D), BF), ((96, D), BF)],
+            [(one[1].shape, one[1].dtype) for one in halves],
+            8,
+            4,
+        )
+        known["half"] = up_sent
+        up_sent, down_sent = gate("RS2", (up_sent, down_sent))
+        up_last, down_last = swap(up_sent, "seq", 4), swap(down_sent, "seq", 2)
+        known["RS2"] = (up_last, down_last)
         grad_time_weight, norm_sums, bias_sums, grad_up_bias = call(
             time_grad_kernel, "time_grad",
             (*(far(one) for one in all_features), *gate("time", docs_all)),
@@ -1110,16 +1109,30 @@
             4,
         )
         known["time"] = grad_time_weight
+        heads_all = spread_rows(gate("AGG", spread))
+        known["AGG"] = heads_all[1:]
+        up_last, down_last = gate("all", (up_last, down_last))
+        merged = call(
+            combine_all_kernel, "combine_all", (*halves, up_last, down_last),
+            [((216, D), BF)],
+            [(one[1].shape[1:], one[1].dtype) for one in halves],
+            8,
+            4,
+        )[0]
+        known["all"] = merged
+        feed_all = spread_rows(gate("AGF", merged))
+        known["AGF"] = feed_all[1:]
+        grad_qkv_weight, grad_qv_bias = call(
+            finish_heads_kernel, "finish_heads", gate("finh", heads_all),
+            [((share, 3 * D), F32), ((1, 192), F32)],
+        )
+        known["finh"] = grad_qkv_weight
         grad_up_weight, grad_down_weight, grad_out_weight = call(
             finish_all_kernel, "finish_all", gate("finf", feed_all),
             [((share, FF), F32), ((FF // seqs, D), F32), ((share, D), F32)],
             [((4, 120, D), F32)],
         )
         known["finf"] = grad_out_weight
-        grad_qkv_weight, grad_qv_bias = call(
-            finish_heads_kernel, "finish_heads", gate("finh", heads_all),
-            [((share, 3 * D), F32), ((1, 192), F32)],
-        )
         grad_qv_bias, grad_up_bias = grad_qv_bias[0], grad_up_bias[0]
         grad_out_bias, grad_down_bias = bias_sums[0], bias_sums[1]
         grad_norm_gain, grad_norm_bias = norm_sums[:2], norm_sums[2:]
@@ -1132,7 +1145,7 @@
             precision=precise,
         )
         grad_qkv_weight, qv_sums, grad_out_weight, grad_up_weight, grad_down_weight, totals = (
-            general_grads(ydf, ado[0], grads[0], head_sums, up_weight, up_bias, down_weight)
+            general_grads(ydf, ado[0], grads[0], grads[1], up_weight, up_bias, down_weight)
         )
 
         def part_of(vector, axis=0):

time: 168 us -> 158 us (0.940)
  starting transfers between devices: 43.7 us -> 37.4 us
  waiting for transfers between devices: 46 us -> 41 us
  Pallas kernels: 65 us -> 67.1 us
    ppermute x32, waiting for transfers between devices: 43.7 us -> 37.9 us  [swap(): lax.ppermute(block, axis, [(i, i ^ bit) for i in range(lax.axis_size(axis...]
    ppermute x32, starting transfers between devices: 27.6 us -> 23.7 us  [swap(): lax.ppermute(block, axis, [(i, i ^ bit) for i in range(lax.axis_size(axis...]
    pallas_call x15 -> x13, Pallas kernels: 65 us -> 67.1 us  [call(): pl.pallas_call(kernel, out_shape=tuple(((pltpu.HBM if FAR in one else plt...]
    all_to_all x1, waiting for transfers between devices: 0.01 us -> 1.73 us  [body(): spread = lax.all_to_all(gate('GA2A', mine[0]), 'seq', 0, 0, tiled=True)]
    unnamed x34 -> x38, local copies, waits for them, and re-layouts: 4.78 us -> 4.1 us
  transfers between devices with their start and end apart: 36 -> 36, of which waited for: 14 -> 18; matrix products, arithmetic and copies ran while one was open for 3% -> 3% of each run, Pallas kernels for 26% -> 29%
where the time goes in v1:
time: 158 us; the launch traced here: 157 us
  Pallas kernels  67.1 us (42%)
  waiting for transfers between devices  41 us (26%)
  starting transfers between devices  37.4 us (24%)
  local copies, waits for them, and re-layouts  7.26 us (5%)
  other arithmetic  3.13 us (2%)
    pallas_call x13, Pallas kernels, call(): pl.pallas_call(kernel, out_shape=tuple(((pltpu.HBM if FAR in one else plt...  67.1 us
    ppermute x32, waiting for transfers between devices, swap(): lax.ppermute(block, axis, [(i, i ^ bit) for i in range(lax.axis_size(axis...  37.9 us
    ppermute x32, starting transfers between devices, swap(): lax.ppermute(block, axis, [(i, i ^ bit) for i in range(lax.axis_size(axis...  23.7 us
    all_to_all x1, starting transfers between devices, body(): arrived = lax.all_to_all(gate('DA', packed), 'seq', 0, 0, tiled=True)  4.71 us
    all_to_all x1, starting transfers between devices, body(): back = lax.all_to_all(gate('BACK', back), 'seq', 0, 0, tiled=True)  4.6 us
    all_to_all x1, starting transfers between devices, body(): spread = lax.all_to_all(gate('GA2A', mine[0]), 'seq', 0, 0, tiled=True)  4.25 us
    unnamed x38, local copies, waits for them, and re-layouts  4.1 us
  transfers between devices with their start and end apart: 36, of which 18 were waited for; matrix products, arithmetic and copies ran while one was open for 3% of the time, Pallas kernels for 29%

profile of v1, /device:TPU:0, one launch (start us, length us, event | category | flops | bytes accessed | tf_op | source)
XLA Modules:
  0.0 157.0 jit_solution(16722712951193882525)
XLA Ops:
  0.7 0.8 convert_element_type.16
  1.4 0.9 fusion.1.refs_0_
  2.4 3.0 %collective-permute-start = (bf16[136,768]{1,0:T(8,128)(2,1)S(1)}, bf16[136,768]{1,0:T(8,128)(2,1)S(1)}, u32[]{:S(2)}, u32[]{:S(2)}) collective-permute-start(bf16[136,768]{1,0:T(8,128)(2,1)S(1)} %fusion.1.refs_0_), channel_id=1, source_target_pairs={{0,4},{4,0},{8,12},{12,8},{16,20},{20,16},{24,28},{28,24},{1,5},{5... | collective-permute-start | bytes 626696 | tf_op jit(solution)/shard_map/ppermute | solution.py:30
  5.4 3.6 %collective-permute-start.5 = (bf16[136,768]{1,0:T(8,128)(2,1)S(1)}, bf16[136,768]{1,0:T(8,128)(2,1)S(1)}, u32[]{:S(2)}, u32[]{:S(2)}) collective-permute-start(bf16[136,768]{1,0:T(8,128)(2,1)S(1)} %fusion.1.refs_0_), channel_id=1, source_target_pairs={{0,24},{4,28},{8,16},{12,20},{16,8},{20,12},{24,0},{28,4},{1,25},{... | collective-permute-start | bytes 626696 | tf_op jit(solution)/shard_map/ppermute | solution.py:30
  9.0 0.8 collective-permute-start.3
  9.8 0.7 convert_bitcast_fusion
  10.5 0.7 reshape.49.refs_10_.bias_ref
  11.2 0.7 reshape.50.refs_12_
  11.8 0.7 reshape.52.refs_19_
  13.0 2.2 %collective-permute-done.5.refs_6_ = bf16[136,768]{1,0:T(8,128)(2,1)S(1)} collective-permute-done((bf16[136,768]{1,0:T(8,128)(2,1)S(1)}, bf16[136,768]{1,0:T(8,128)(2,1)S(1)}, u32[]{:S(2)}, u32[]{:S(2)}) %collective-permute-start.5) | collective-permute-done | bytes 208928 | tf_op jit(solution)/shard_map/ppermute | solution.py:30
  15.5 3.8 %collective-permute-done.1.refs_2_ = bf16[136,768]{1,0:T(8,128)(2,1)S(1)} collective-permute-done((bf16[136,768]{1,0:T(8,128)(2,1)S(1)}, bf16[136,768]{1,0:T(8,128)(2,1)S(1)}, u32[]{:S(2)}, u32[]{:S(2)}) %collective-permute-start.1) | collective-permute-done | bytes 208928 | tf_op jit(solution)/shard_map/ppermute | solution.py:30
  19.3 0.6 collective-permute-start.2
  19.9 6.6 %collective-permute-done.3.refs_4_ = bf16[136,768]{1,0:T(8,128)(2,1)S(1)} collective-permute-done((bf16[136,768]{1,0:T(8,128)(2,1)S(1)}, bf16[136,768]{1,0:T(8,128)(2,1)S(1)}, u32[]{:S(2)}, u32[]{:S(2)}) %collective-permute-start.3) | collective-permute-done | bytes 208928 | tf_op jit(solution)/shard_map/ppermute | solution.py:30
  26.5 0.5 collective-permute-start.4
  27.0 5.1 %fetch.1 = (bf16[768,2304]{1,0:T(8,128)(2,1)S(1)}, bf16[768,768]{1,0:T(8,128)(2,1)S(1)}, bf16[768,3072]{1,0:T(8,128)(2,1)S(1)}, bf16[3072,768]{1,0:T(8,128)(2,1)S(1)}) custom-call(bf16[768,2304]{1,0:T(8,128)(2,1)} %qkv_in.3, bf16[768,768]{1,0:T(8,128)(2,1)} %refs_1_.1, bf16[768,3072]{1,0:T(8,128)(2,1)} %up_in.1, bf16[3072,768]{1,0:T(8,128)(2,1)} %refs_10_.1), custom_call_target="tpu_custom_call" | custom-call | flops 7000000000 | tf_op jit(solution)/shard_map/fetch/pallas_call | solution.py:67
  32.1 0.5 collective-permute-done.4.refs_5_
  32.7 12.3 %forward.1 = (bf16[1024,768]{1,0:T(8,128)(2,1)}, f32[128,128]{1,0:T(8,128)S(1)}, f32[128,768]{1,0:T(8,128)S(1)}, bf16[16,1024]{1,0:T(8,128)(2,1)S(1)}, f32[128,7...) custom-call(bf16[136,768]{1,0:T(8,128)(2,1)S(1)} %fusion.1.refs_0_, ...), custom_call_target="tpu_custom_call" | custom-call | flops 12000000000 | tf_op jit(solution)/shard_map/forward/pallas_call | solution.py:67
  45.0 5.9 %backward.1 = (bf16[8,176,128]{2,1,0:T(8,128)(2,1)}, f32[128,768]{1,0:T(8,128)}, f32[16,768]{1,0:T(8,128)}, bf16[16,1024]{1,0:T(8,128)(2,1)}, bf16[128,2304]{1,0...) custom-call(f32[128,768]{1,0:T(8,128)S(1)} %get-tuple-element.95.z1_ref, ...), custom_call_target="tpu_custom_call" | custom-call | flops 5000000000 | tf_op jit(solution)/shard_map/backward/pallas_call | solution.py:67
  50.9 4.7 %all-to-all-start = ((bf16[8,176,128]{2,1,0:T(8,128)(2,1)}), bf16[8,176,128]{2,1,0:T(8,128)(2,1)S(1)}, u32[]{:S(2)}, u32[]{:S(2)}) async-start(bf16[8,176,128]{2,1,0:T(8,128)(2,1)} %get-tuple-element.106), calls=%async_computation | async-start | bytes 720896 | tf_op jit(solution)/shard_map/all_to_all | solution.py:1034
  55.6 1.5 collective-permute-start.14
  57.1 2.0 %collective-permute-start.15 = (bf16[128,2304]{1,0:T(8,128)(2,1)}, bf16[128,2304]{1,0:T(8,128)(2,1)}, u32[]{:S(2)}, u32[]{:S(2)}) collective-permute-start(bf16[128,2304]{1,0:T(8,128)(2,1)} %get-tuple-element.121), channel_id=1, source_target_pairs={{0,4},{4,0},{8,12},{12,8},{16,20},{20,16},{24,28},{28,24},{1,5},{5... | collective-permute-start | bytes 1769480 | tf_op jit(solution)/shard_map/ppermute | solution.py:30
  59.1 4.1 %heads.1 = (bf16[1024,128]{1,0:T(8,128)(2,1)}, bf16[1024,128]{1,0:T(8,128)(2,1)}, bf16[1024,128]{1,0:T(8,128)(2,1)}, bf16[768,384]{1,0:T(8,128)(2,1)}) custom-call(bf16[1024,768]{1,0:T(8,128)(2,1)} %get-tuple-element.89.x_in.refs_6_, bf16[768,2304]{1,0:T(8,128)(2,1)} %qkv_in.3, f32[1,1536]{1,0:T(1,128)S(1)} %reshape.49.refs_10_.bias_ref), custom_call_target="tpu_custom_call" | custom-call | flops 3000000000 | tf_op jit(solution)/shard_map/heads/pallas_call | solution.py:67
  63.3 1.4 all-to-all-done.refs_7_
  64.6 12.1 %head_grad.1 = (bf16[8,384,128]{2,1,0:T(8,128)(2,1)}, f32[16,128]{1,0:T(8,128)S(1)}, bf16[8,32,288]{2,1,0:T(8,128)(2,1)S(1)}, bf16[8,32,288]{2,1,0:T(8,128)(2,1)...) custom-call(bf16[768,384]{1,0:T(8,128)(2,1)} %get-tuple-element.90.refs_0_, ...), custom_call_target="tpu_custom_call" | custom-call | flops 12000000000 | tf_op jit(solution)/shard_map/head_grad/pallas_call | solution.py:67
  76.8 4.6 %all-to-all-start.1 = ((bf16[8,384,128]{2,1,0:T(8,128)(2,1)}), bf16[8,384,128]{2,1,0:T(8,128)(2,1)S(1)}, u32[]{:S(2)}, u32[]{:S(2)}) async-start(bf16[8,384,128]{2,1,0:T(8,128)(2,1)} %get-tuple-element.108), calls=%async_computation.1 | async-start | bytes 1572864 | tf_op jit(solution)/shard_map/all_to_all | solution.py:1067
  81.4 5.2 %part_weights.1 = (bf16[768,768]{1,0:T(8,128)(2,1)}, f32[1,768]{1,0:T(1,128)S(1)}) custom-call(bf16[768,3072]{1,0:T(8,128)(2,1)} %up_in.1, f32[1,3072]{1,0:T(1,128)S(1)} %bitcast.16), custom_call_target="tpu_custom_call" | custom-call | flops 3000000000 | tf_op jit(solution)/shard_map/part_weights/pallas_call | solution.py:67
  86.7 5.6 %collective-permute-done.15.refs_3_ = bf16[128,2304]{1,0:T(8,128)(2,1)} collective-permute-done((bf16[128,2304]{1,0:T(8,128)(2,1)}, bf16[128,2304]{1,0:T(8,128)(2,1)}, u32[]{:S(2)}, u32[]{:S(2)}) %collective-permute-start.15) | collective-permute-done | bytes 589856 | tf_op jit(solution)/shard_map/ppermute | solution.py:30
  92.2 0.5 collective-permute-start.18
  92.8 0.5 collective-permute-start.7
  93.3 1.2 collective-permute-done.17.refs_5_
  94.6 1.0 collective-permute-done.18.refs_6_
  95.6 0.8 collective-permute-done.19.refs_7_
  96.4 0.8 copy-done.13
  97.2 8.9 %feed_grad.1 = (f32[2,120,768]{2,1,0:T(8,128)}, bf16[2,120,768]{2,1,0:T(8,128)(2,1)S(1)}, f32[2,96,768]{2,1,0:T(8,128)}, bf16[2,96,768]{2,1,0:T(8,128)(2,1)S(1)}) custom-call(bf16[128,2304]{1,0:T(8,128)(2,1)} %get-tuple-element.119.refs_0_, bf16[128,2304]{1,0:T(8,128)(2,1)} %copy-done.10, bf16[128,2304]{1,0:T(8,128)(2,1)} %collective-permute-done.14.refs_2_, ...), custom_call_target="tpu_custom_call" | custom-call | flops 8000000000 | tf_op jit(solution)/shard_map/feed_grad/pallas_call | solution.py:67
  106.2 3.1 %collective-permute-start.21 = (bf16[2,96,768]{2,1,0:T(8,128)(2,1)S(1)}, bf16[2,96,768]{2,1,0:T(8,128)(2,1)}, u32[]{:S(2)}, u32[]{:S(2)}) collective-permute-start(bf16[2,96,768]{2,1,0:T(8,128)(2,1)S(1)} %get-tuple-element.134), channel_id=1, source_target_pairs={{0,16},{4,20},{8,24},{12,28},{16,0},{20,4},{24,8},{28,12},{1,17},{... | collective-permute-start | bytes 884744 | tf_op jit(solution)/shard_map/ppermute | solution.py:30
  109.3 0.7 copy-done.14
  110.0 0.7 copy-done.15
  110.7 5.1 %input_grad.1 = (f32[128,768]{1,0:T(8,128)}, f32[32,768]{1,0:T(8,128)S(1)}, bf16[8,32,288]{2,1,0:T(8,128)(2,1)}) custom-call(bf16[8,384,128]{2,1,0:T(8,128)(2,1)S(1)} %all-to-all-done.1.back_ref, f32[128,768]{1,0:T(8,128)} %get-tuple-element.109.dr1_in, bf16[768,2304]{1,0:T(8,128)(2,1)} %qkv_in.3, f32[16,128]{1,0:T(8,128)S(1)} %get-tuple-element.110.sums_ref, ...), custom_call_target="tpu_custom_call" | custom-call | flops 5000000000 | tf_op jit(solution)/shard_map/input_grad/pallas_call | solution.py:67
  115.7 4.2 %all-to-all-start.2 = ((bf16[8,32,288]{2,1,0:T(8,128)(2,1)}), bf16[8,32,288]{2,1,0:T(8,128)(2,1)S(1)}, u32[]{:S(2)}, u32[]{:S(2)}) async-start(bf16[8,32,288]{2,1,0:T(8,128)(2,1)} %get-tuple-element.116), calls=%async_computation.2 | async-start | bytes 393216 | tf_op jit(solution)/shard_map/all_to_all | solution.py:1086
  120.0 0.4 collective-permute-start.23
  120.4 4.2 %collective-permute-done.23.refs_6_ = f32[32,768]{1,0:T(8,128)S(1)} collective-permute-done((f32[32,768]{1,0:T(8,128)S(1)}, f32[32,768]{1,0:T(8,128)S(1)}, u32[]{:S(2)}, u32[]{:S(2)}) %collective-permute-start.23) | collective-permute-done | bytes 98336 | tf_op jit(solution)/shard_map/ppermute | solution.py:30
  124.6 0.6 copy-done.2
  125.3 0.6 collective-permute-done.24.refs_7_
  125.9 0.6 copy-done.4
  126.6 1.7 %all-to-all-done.2.a_ref = bf16[8,32,288]{2,1,0:T(8,128)(2,1)S(1)} async-done(((bf16[8,32,288]{2,1,0:T(8,128)(2,1)}), bf16[8,32,288]{2,1,0:T(8,128)(2,1)S(1)}, u32[]{:S(2)}, u32[]{:S(2)}) %all-to-all-start.2) | async-done | bytes 147488 | tf_op jit(solution)/shard_map/all_to_all | solution.py:1086
  128.5 1.6 %combine_half.1 = (bf16[120,768]{1,0:T(8,128)(2,1)S(1)}, bf16[96,768]{1,0:T(8,128)(2,1)S(1)}) custom-call(f32[2,120,768]{2,1,0:T(8,128)} %get-tuple-element.129.up_in, f32[2,96,768]{2,1,0:T(8,128)} %get-tuple-element.130.down_in, bf16[2,120,768]{2,1,0:T(8,128)(2,1)} %collective-permute-done.20.up_got_in, bf16[2,96,768]{2,1,0:T(8,128)(2,1)} %collective-permute-done.21.down_got_in), custom_call_target="tpu_custom_call" | custom-call | flops 1000000000 | tf_op jit(solution)/shard_map/combine_half/pallas_call | solution.py:67
  130.2 1.7 %collective-permute-start.25 = (bf16[120,768]{1,0:T(8,128)(2,1)S(1)}, bf16[120,768]{1,0:T(8,128)(2,1)S(1)}, u32[]{:S(2)}, u32[]{:S(2)}) collective-permute-start(bf16[120,768]{1,0:T(8,128)(2,1)S(1)} %get-tuple-element.138), channel_id=1, source_target_pairs={{0,16},{4,20},{8,24},{12,28},{16,0},{20,4},{24,8},{28,12},{1,17},{... | collective-permute-start | bytes 552968 | tf_op jit(solution)/shard_map/ppermute | solution.py:30
  131.8 1.6 %collective-permute-start.28 = (bf16[16,768]{1,0:T(8,128)(2,1)S(1)}, bf16[16,768]{1,0:T(8,128)(2,1)S(1)}, u32[]{:S(2)}, u32[]{:S(2)}) collective-permute-start(bf16[16,768]{1,0:T(8,128)(2,1)S(1)} %pad_maximum_fusion.refs_0_), channel_id=1, source_target_pairs={{0,2},{1,3},{2,0},{3,1},{4,6},{5,7},{6,4},{7,5},{8,10},{9,11},{10,... | collective-permute-start | bytes 73736 | tf_op jit(solution)/shard_map/ppermute | solution.py:30
  133.5 1.2 collective-permute-start.26
  134.8 0.4 collective-permute-start.12
  135.2 0.5 collective-permute-done.28.refs_2_
  135.7 1.2 collective-permute-done.27.refs_1_
  137.0 1.0 collective-permute-done.29.refs_3_
  138.1 0.6 copy-done.18
  138.7 1.9 %time_grad.1 = (f32[96,768]{1,0:T(8,128)}, f32[4,96]{1,0:T(4,128)S(1)}, f32[2,96]{1,0:T(2,128)S(1)}, f32[1,384]{1,0:T(1,128)S(1)}) custom-call(bf16[16,768]{1,0:T(8,128)(2,1)} %copy-done.9, bf16[16,768]{1,0:T(8,128)(2,1)} %copy-done.17, bf16[16,768]{1,0:T(8,128)(2,1)} %copy-done.16, bf16[16,768]{1,0:T(8,128)(2,1)} %copy-done.18, ...), custom_call_target="tpu_custom_call" | custom-call | flops 1000000000 | tf_op jit(solution)/shard_map/time_grad/pallas_call | solution.py:67
  140.6 0.5 collective-permute-done.26.down_last_ref
  141.2 1.3 combine_all.1.a_ref
  142.5 1.5 collective-permute-start.31
  144.0 8.0 %collective-permute-done.31.c_ref = bf16[216,768]{1,0:T(8,128)(2,1)S(1)} collective-permute-done((bf16[216,768]{1,0:T(8,128)(2,1)S(1)}, bf16[216,768]{1,0:T(8,128)(2,1)S(1)}, u32[]{:S(2)}, u32[]{:S(2)}) %collective-permute-start.31) | collective-permute-done | bytes 331808 | tf_op jit(solution)/shard_map/ppermute | solution.py:30
  151.9 0.5 slice_bitcast_fusion
  152.5 0.6 reduce
  153.1 0.6 fusion.5
  153.6 1.3 finish_heads.1
  154.9 2.1 %finish_all.1 = (f32[96,3072]{1,0:T(8,128)}, f32[384,768]{1,0:T(8,128)}, f32[96,768]{1,0:T(8,128)}) custom-call(bf16[216,768]{1,0:T(8,128)(2,1)S(1)} %combine_all.1.a_ref, bf16[216,768]{1,0:T(8,128)(2,1)S(1)} %collective-permute-done.30.b_ref, bf16[216,768]{1,0:T(8,128)(2,1)S(1)} %collective-permute-done.31.c_ref, ...), custom_call_target="tpu_custom_call" | custom-call | flops 2000000000 | tf_op jit(solution)/shard_map/finish_all/pallas_call | solution.py:67
  (72 shorter events, 1.7 us)
Async XLA Ops:
  0.6 12.1 %copy-start = (bf16[768,768]{1,0:T(8,128)(2,1)S(1)}, bf16[768,768]{1,0:T(8,128)(2,1)}, u32[]{:S(2)}) copy-start(bf16[768,768]{1,0:T(8,128)(2,1)} %param.29) | copy-start | bytes 3538948
  2.4 10.7 %collective-permute-start = (bf16[136,768]{1,0:T(8,128)(2,1)S(1)}, bf16[136,768]{1,0:T(8,128)(2,1)S(1)}, u32[]{:S(2)}, u32[]{:S(2)}) collective-permute-start(bf16[136,768]{1,0:T(8,128)(2,1)S(1)} %fusion.1.refs_0_), channel_id=1, source_target_pairs={{0,4},{4,0},{8,12},{12,8},{16,20},{20,16},{24,28},{28,24},{1,5},{5... | collective-permute-start | bytes 626696 | tf_op jit(solution)/shard_map/ppermute | solution.py:30
  5.4 9.9 %collective-permute-start.5 = (bf16[136,768]{1,0:T(8,128)(2,1)S(1)}, bf16[136,768]{1,0:T(8,128)(2,1)S(1)}, u32[]{:S(2)}, u32[]{:S(2)}) collective-permute-start(bf16[136,768]{1,0:T(8,128)(2,1)S(1)} %fusion.1.refs_0_), channel_id=1, source_target_pairs={{0,24},{4,28},{8,16},{12,20},{16,8},{20,12},{24,0},{28,4},{1,25},{... | collective-permute-start | bytes 626696 | tf_op jit(solution)/shard_map/ppermute | solution.py:30
  9.0 10.3 %collective-permute-start.1 = (bf16[136,768]{1,0:T(8,128)(2,1)S(1)}, bf16[136,768]{1,0:T(8,128)(2,1)S(1)}, u32[]{:S(2)}, u32[]{:S(2)}) collective-permute-start(bf16[136,768]{1,0:T(8,128)(2,1)S(1)} %fusion.1.refs_0_), channel_id=1, source_target_pairs={{0,8},{4,12},{8,0},{12,4},{16,24},{20,28},{24,16},{28,20},{1,9},{5... | collective-permute-start | bytes 626696 | tf_op jit(solution)/shard_map/ppermute | solution.py:30
  9.0 17.5 %collective-permute-start.3 = (bf16[136,768]{1,0:T(8,128)(2,1)S(1)}, bf16[136,768]{1,0:T(8,128)(2,1)S(1)}, u32[]{:S(2)}, u32[]{:S(2)}) collective-permute-start(bf16[136,768]{1,0:T(8,128)(2,1)S(1)} %fusion.1.refs_0_), channel_id=1, source_target_pairs={{0,16},{4,20},{8,24},{12,28},{16,0},{20,4},{24,8},{28,12},{1,17},{... | collective-permute-start | bytes 626696 | tf_op jit(solution)/shard_map/ppermute | solution.py:30
  13.0 19.7 %copy-start.1 = (bf16[1,128,768]{2,1,0:T(8,128)(2,1)S(1)}, bf16[1,128,768]{2,1,0:T(8,128)(2,1)}, u32[]{:S(2)}) copy-start(bf16[1,128,768]{2,1,0:T(8,128)(2,1)} %param.16) | copy-start | bytes 589828
  13.0 19.7 %copy-start.6 = (f32[3072]{0:T(1024)S(1)}, f32[3072]{0:T(1024)}, u32[]{:S(2)}) copy-start(f32[3072]{0:T(1024)} %param.24) | copy-start | bytes 36868
  13.0 19.7 %copy-start.7 = (f32[2,768]{1,0:T(2,128)S(1)}, f32[2,768]{1,0:T(2,128)}, u32[]{:S(2)}) copy-start(f32[2,768]{1,0:T(2,128)} %refs_14_.1) | copy-start | bytes 18436
  13.0 19.7 %copy-start.8 = (f32[2,768]{1,0:T(2,128)S(1)}, f32[2,768]{1,0:T(2,128)}, u32[]{:S(2)}) copy-start(f32[2,768]{1,0:T(2,128)} %gain_ref.1) | copy-start | bytes 18436
  15.3 16.8 %collective-permute-start.6 = (bf16[136,768]{1,0:T(8,128)(2,1)S(1)}, bf16[136,768]{1,0:T(8,128)(2,1)S(1)}, u32[]{:S(2)}, u32[]{:S(2)}) collective-permute-start(bf16[136,768]{1,0:T(8,128)(2,1)S(1)} %collective-permute-done.5.refs_6_), channel_id=1, source_target_pairs={{0,4},{4,0},{8,12},{12,8},{16,20},{20,16},{24,28},{28,24},{1,5},{5... | collective-permute-start | bytes 626696 | tf_op jit(solution)/shard_map/ppermute | solution.py:30
  19.3 12.9 %collective-permute-start.2 = (bf16[136,768]{1,0:T(8,128)(2,1)S(1)}, bf16[136,768]{1,0:T(8,128)(2,1)S(1)}, u32[]{:S(2)}, u32[]{:S(2)}) collective-permute-start(bf16[136,768]{1,0:T(8,128)(2,1)S(1)} %collective-permute-done.1.refs_2_), channel_id=1, source_target_pairs={{0,4},{4,0},{8,12},{12,8},{16,20},{20,16},{24,28},{28,24},{1,5},{5... | collective-permute-start | bytes 626696 | tf_op jit(solution)/shard_map/ppermute | solution.py:30
  26.5 6.2 %collective-permute-start.4 = (bf16[136,768]{1,0:T(8,128)(2,1)S(1)}, bf16[136,768]{1,0:T(8,128)(2,1)S(1)}, u32[]{:S(2)}, u32[]{:S(2)}) collective-permute-start(bf16[136,768]{1,0:T(8,128)(2,1)S(1)} %collective-permute-done.3.refs_4_), channel_id=1, source_target_pairs={{0,4},{4,0},{8,12},{12,8},{16,20},{20,16},{24,28},{28,24},{1,5},{5... | collective-permute-start | bytes 626696 | tf_op jit(solution)/shard_map/ppermute | solution.py:30
  50.9 13.7 %all-to-all-start = ((bf16[8,176,128]{2,1,0:T(8,128)(2,1)}), bf16[8,176,128]{2,1,0:T(8,128)(2,1)S(1)}, u32[]{:S(2)}, u32[]{:S(2)}) async-start(bf16[8,176,128]{2,1,0:T(8,128)(2,1)} %get-tuple-element.106), calls=%async_computation | async-start | bytes 720896 | tf_op jit(solution)/shard_map/all_to_all | solution.py:1034
  55.6 25.8 %collective-permute-start.13 = (bf16[128,2304]{1,0:T(8,128)(2,1)}, bf16[128,2304]{1,0:T(8,128)(2,1)S(1)}, u32[]{:S(2)}, u32[]{:S(2)}) collective-permute-start(bf16[128,2304]{1,0:T(8,128)(2,1)} %get-tuple-element.119.refs_0_), channel_id=1, source_target_pairs={{0,1},{1,0},{2,3},{3,2},{4,5},{5,4},{6,7},{7,6},{8,9},{9,8},{10,11... | collective-permute-start | bytes 1769480 | tf_op jit(solution)/shard_map/ppermute | solution.py:30
  55.6 31.1 %collective-permute-start.14 = (bf16[128,2304]{1,0:T(8,128)(2,1)}, bf16[128,2304]{1,0:T(8,128)(2,1)}, u32[]{:S(2)}, u32[]{:S(2)}) collective-permute-start(bf16[128,2304]{1,0:T(8,128)(2,1)} %get-tuple-element.120), channel_id=1, source_target_pairs={{0,2},{1,3},{2,0},{3,1},{4,6},{5,7},{6,4},{7,5},{8,10},{9,11},{10,... | collective-permute-start | bytes 1769480 | tf_op jit(solution)/shard_map/ppermute | solution.py:30
  57.1 35.1 %collective-permute-start.15 = (bf16[128,2304]{1,0:T(8,128)(2,1)}, bf16[128,2304]{1,0:T(8,128)(2,1)}, u32[]{:S(2)}, u32[]{:S(2)}) collective-permute-start(bf16[128,2304]{1,0:T(8,128)(2,1)} %get-tuple-element.121), channel_id=1, source_target_pairs={{0,4},{4,0},{8,12},{12,8},{16,20},{20,16},{24,28},{28,24},{1,5},{5... | collective-permute-start | bytes 1769480 | tf_op jit(solution)/shard_map/ppermute | solution.py:30
  59.1 33.1 %collective-permute-start.16 = (bf16[128,2304]{1,0:T(8,128)(2,1)}, bf16[128,2304]{1,0:T(8,128)(2,1)}, u32[]{:S(2)}, u32[]{:S(2)}) collective-permute-start(bf16[128,2304]{1,0:T(8,128)(2,1)} %get-tuple-element.122), channel_id=1, source_target_pairs={{0,6},{1,7},{2,4},{3,5},{4,2},{5,3},{6,0},{7,1},{8,14},{9,15},{10,... | collective-permute-start | bytes 1769480 | tf_op jit(solution)/shard_map/ppermute | solution.py:809
  76.8 33.9 %all-to-all-start.1 = ((bf16[8,384,128]{2,1,0:T(8,128)(2,1)}), bf16[8,384,128]{2,1,0:T(8,128)(2,1)S(1)}, u32[]{:S(2)}, u32[]{:S(2)}) async-start(bf16[8,384,128]{2,1,0:T(8,128)(2,1)} %get-tuple-element.108), calls=%async_computation.1 | async-start | bytes 1572864 | tf_op jit(solution)/shard_map/all_to_all | solution.py:1067
  81.4 5.3 %copy-start.10 = (bf16[128,2304]{1,0:T(8,128)(2,1)}, bf16[128,2304]{1,0:T(8,128)(2,1)S(1)}, u32[]{:S(2)}) copy-start(bf16[128,2304]{1,0:T(8,128)(2,1)S(1)} %collective-permute-done.13.refs_1_) | copy-start | bytes 1769476
  92.2 2.2 %collective-permute-start.17 = (bf16[128,2304]{1,0:T(8,128)(2,1)}, bf16[128,2304]{1,0:T(8,128)(2,1)S(1)}, u32[]{:S(2)}, u32[]{:S(2)}) collective-permute-start(bf16[128,2304]{1,0:T(8,128)(2,1)} %collective-permute-done.14.refs_2_), channel_id=1, source_target_pairs={{0,1},{1,0},{2,3},{3,2},{4,5},{5,4},{6,7},{7,6},{8,9},{9,8},{10,11... | collective-permute-start | bytes 1769480 | tf_op jit(solution)/shard_map/ppermute | solution.py:30
  92.2 3.3 %collective-permute-start.18 = (bf16[128,2304]{1,0:T(8,128)(2,1)}, bf16[128,2304]{1,0:T(8,128)(2,1)S(1)}, u32[]{:S(2)}, u32[]{:S(2)}) collective-permute-start(bf16[128,2304]{1,0:T(8,128)(2,1)} %collective-permute-done.15.refs_3_), channel_id=1, source_target_pairs={{0,1},{1,0},{2,3},{3,2},{4,5},{5,4},{6,7},{7,6},{8,9},{9,8},{10,11... | collective-permute-start | bytes 1769480 | tf_op jit(solution)/shard_map/ppermute | solution.py:30
  92.7 3.7 %collective-permute-start.19 = (bf16[128,2304]{1,0:T(8,128)(2,1)}, bf16[128,2304]{1,0:T(8,128)(2,1)S(1)}, u32[]{:S(2)}, u32[]{:S(2)}) collective-permute-start(bf16[128,2304]{1,0:T(8,128)(2,1)} %collective-permute-done.16.refs_4_), channel_id=1, source_target_pairs={{0,1},{1,0},{2,3},{3,2},{4,5},{5,4},{6,7},{7,6},{8,9},{9,8},{10,11... | collective-permute-start | bytes 1769480 | tf_op jit(solution)/shard_map/ppermute | solution.py:30
  92.8 16.6 %collective-permute-start.7 = (bf16[8,32,288]{2,1,0:T(8,128)(2,1)S(1)}, bf16[8,32,288]{2,1,0:T(8,128)(2,1)S(1)}, u32[]{:S(2)}, u32[]{:S(2)}) collective-permute-start(bf16[8,32,288]{2,1,0:T(8,128)(2,1)S(1)} %get-tuple-element.112), channel_id=1, source_target_pairs={{0,1},{1,0},{2,3},{3,2},{4,5},{5,4},{6,7},{7,6},{8,9},{9,8},{10,11... | collective-permute-start | bytes 442376 | tf_op jit(solution)/shard_map/ppermute | solution.py:30
  93.3 16.1 %collective-permute-start.8 = (bf16[8,32,288]{2,1,0:T(8,128)(2,1)S(1)}, bf16[8,32,288]{2,1,0:T(8,128)(2,1)S(1)}, u32[]{:S(2)}, u32[]{:S(2)}) collective-permute-start(bf16[8,32,288]{2,1,0:T(8,128)(2,1)S(1)} %get-tuple-element.113), channel_id=1, source_target_pairs={{0,2},{1,3},{2,0},{3,1},{4,6},{5,7},{6,4},{7,5},{8,10},{9,11},{10,... | collective-permute-start | bytes 442376 | tf_op jit(solution)/shard_map/ppermute | solution.py:30
  94.5 2.0 %copy-start.11 = (bf16[128,2304]{1,0:T(8,128)(2,1)}, bf16[128,2304]{1,0:T(8,128)(2,1)S(1)}, u32[]{:S(2)}) copy-start(bf16[128,2304]{1,0:T(8,128)(2,1)S(1)} %collective-permute-done.17.refs_5_) | copy-start | bytes 1769476
  94.5 16.2 %collective-permute-start.9 = (bf16[8,32,288]{2,1,0:T(8,128)(2,1)S(1)}, bf16[8,32,288]{2,1,0:T(8,128)(2,1)}, u32[]{:S(2)}, u32[]{:S(2)}) collective-permute-start(bf16[8,32,288]{2,1,0:T(8,128)(2,1)S(1)} %get-tuple-element.114), channel_id=1, source_target_pairs={{0,3},{1,2},{2,1},{3,0},{4,7},{5,6},{6,5},{7,4},{8,11},{9,10},{10,... | collective-permute-start | bytes 442376 | tf_op jit(solution)/shard_map/ppermute | solution.py:30
  95.6 0.9 copy-start.12
  96.4 0.8 copy-start.13
  106.2 18.5 %collective-permute-start.20 = (bf16[2,120,768]{2,1,0:T(8,128)(2,1)S(1)}, bf16[2,120,768]{2,1,0:T(8,128)(2,1)}, u32[]{:S(2)}, u32[]{:S(2)}) collective-permute-start(bf16[2,120,768]{2,1,0:T(8,128)(2,1)S(1)} %get-tuple-element.133), channel_id=1, source_target_pairs={{0,8},{4,12},{8,0},{12,4},{16,24},{20,28},{24,16},{28,20},{1,9},{5... | collective-permute-start | bytes 1105928 | tf_op jit(solution)/shard_map/ppermute | solution.py:30
  106.2 18.4 %collective-permute-start.21 = (bf16[2,96,768]{2,1,0:T(8,128)(2,1)S(1)}, bf16[2,96,768]{2,1,0:T(8,128)(2,1)}, u32[]{:S(2)}, u32[]{:S(2)}) collective-permute-start(bf16[2,96,768]{2,1,0:T(8,128)(2,1)S(1)} %get-tuple-element.134), channel_id=1, source_target_pairs={{0,16},{4,20},{8,24},{12,28},{16,0},{20,4},{24,8},{28,12},{1,17},{... | collective-permute-start | bytes 884744 | tf_op jit(solution)/shard_map/ppermute | solution.py:30
  109.3 0.7 copy-start.14
  110.0 0.7 copy-start.15
  115.7 12.5 %all-to-all-start.2 = ((bf16[8,32,288]{2,1,0:T(8,128)(2,1)}), bf16[8,32,288]{2,1,0:T(8,128)(2,1)S(1)}, u32[]{:S(2)}, u32[]{:S(2)}) async-start(bf16[8,32,288]{2,1,0:T(8,128)(2,1)} %get-tuple-element.116), calls=%async_computation.2 | async-start | bytes 393216 | tf_op jit(solution)/shard_map/all_to_all | solution.py:1086
  120.0 4.6 %collective-permute-start.23 = (f32[32,768]{1,0:T(8,128)S(1)}, f32[32,768]{1,0:T(8,128)S(1)}, u32[]{:S(2)}, u32[]{:S(2)}) collective-permute-start(f32[32,768]{1,0:T(8,128)S(1)} %get-tuple-element.135.refs_4_), channel_id=1, source_target_pairs={{0,2},{1,3},{2,0},{3,1},{4,6},{5,7},{6,4},{7,5},{8,10},{9,11},{10,... | collective-permute-start | bytes 294920 | tf_op jit(solution)/shard_map/ppermute | solution.py:30
  120.4 4.3 %collective-permute-start.22 = (f32[32,768]{1,0:T(8,128)S(1)}, f32[32,768]{1,0:T(8,128)S(1)}, u32[]{:S(2)}, u32[]{:S(2)}) collective-permute-start(f32[32,768]{1,0:T(8,128)S(1)} %get-tuple-element.135.refs_4_), channel_id=1, source_target_pairs={{0,1},{1,0},{2,3},{3,2},{4,5},{5,4},{6,7},{7,6},{8,9},{9,8},{10,11... | collective-permute-start | bytes 294920 | tf_op jit(solution)/shard_map/ppermute | solution.py:30
  124.6 1.3 collective-permute-start.24
  124.6 0.6 copy-start.2
  125.9 0.6 copy-start.4
  128.3 6.5 %collective-permute-start.11 = (bf16[8,32,288]{2,1,0:T(8,128)(2,1)S(1)}, bf16[8,32,288]{2,1,0:T(8,128)(2,1)S(1)}, u32[]{:S(2)}, u32[]{:S(2)}) collective-permute-start(bf16[8,32,288]{2,1,0:T(8,128)(2,1)S(1)} %all-to-all-done.2.a_ref), channel_id=1, source_target_pairs={{0,2},{1,3},{2,0},{3,1},{4,6},{5,7},{6,4},{7,5},{8,10},{9,11},{10,... | collective-permute-start | bytes 442376 | tf_op jit(solution)/shard_map/ppermute | solution.py:30
  128.5 10.1 %copy-start.3 = (f32[32,768]{1,0:T(8,128)S(1)}, f32[32,768]{1,0:T(8,128)}, u32[]{:S(2)}) copy-start(f32[32,768]{1,0:T(8,128)} %copy-done.2) | copy-start | bytes 294916
  128.5 10.1 %copy-start.5 = (f32[32,768]{1,0:T(8,128)S(1)}, f32[32,768]{1,0:T(8,128)}, u32[]{:S(2)}) copy-start(f32[32,768]{1,0:T(8,128)} %copy-done.4) | copy-start | bytes 294916
  130.2 11.0 %collective-permute-start.25 = (bf16[120,768]{1,0:T(8,128)(2,1)S(1)}, bf16[120,768]{1,0:T(8,128)(2,1)S(1)}, u32[]{:S(2)}, u32[]{:S(2)}) collective-permute-start(bf16[120,768]{1,0:T(8,128)(2,1)S(1)} %get-tuple-element.138), channel_id=1, source_target_pairs={{0,16},{4,20},{8,24},{12,28},{16,0},{20,4},{24,8},{28,12},{1,17},{... | collective-permute-start | bytes 552968 | tf_op jit(solution)/shard_map/ppermute | solution.py:30
  131.8 6.2 %copy-start.9 = (bf16[16,768]{1,0:T(8,128)(2,1)}, bf16[16,768]{1,0:T(8,128)(2,1)S(1)}, u32[]{:S(2)}) copy-start(bf16[16,768]{1,0:T(8,128)(2,1)S(1)} %pad_maximum_fusion.refs_0_) | copy-start | bytes 73732
  131.8 3.8 %collective-permute-start.28 = (bf16[16,768]{1,0:T(8,128)(2,1)S(1)}, bf16[16,768]{1,0:T(8,128)(2,1)S(1)}, u32[]{:S(2)}, u32[]{:S(2)}) collective-permute-start(bf16[16,768]{1,0:T(8,128)(2,1)S(1)} %pad_maximum_fusion.refs_0_), channel_id=1, source_target_pairs={{0,2},{1,3},{2,0},{3,1},{4,6},{5,7},{6,4},{7,5},{8,10},{9,11},{10,... | collective-permute-start | bytes 73736 | tf_op jit(solution)/shard_map/ppermute | solution.py:30
  133.5 7.6 %collective-permute-start.26 = (bf16[96,768]{1,0:T(8,128)(2,1)S(1)}, bf16[96,768]{1,0:T(8,128)(2,1)S(1)}, u32[]{:S(2)}, u32[]{:S(2)}) collective-permute-start(bf16[96,768]{1,0:T(8,128)(2,1)S(1)} %get-tuple-element.139), channel_id=1, source_target_pairs={{0,8},{4,12},{8,0},{12,4},{16,24},{20,28},{24,16},{28,20},{1,9},{5... | collective-permute-start | bytes 442376 | tf_op jit(solution)/shard_map/ppermute | solution.py:30
  134.7 6.5 %collective-permute-start.10 = (bf16[8,32,288]{2,1,0:T(8,128)(2,1)S(1)}, bf16[8,32,288]{2,1,0:T(8,128)(2,1)S(1)}, u32[]{:S(2)}, u32[]{:S(2)}) collective-permute-start(bf16[8,32,288]{2,1,0:T(8,128)(2,1)S(1)} %all-to-all-done.2.a_ref), channel_id=1, source_target_pairs={{0,1},{1,0},{2,3},{3,2},{4,5},{5,4},{6,7},{7,6},{8,9},{9,8},{10,11... | collective-permute-start | bytes 442376 | tf_op jit(solution)/shard_map/ppermute | solution.py:30
  134.8 6.3 %collective-permute-start.12 = (bf16[8,32,288]{2,1,0:T(8,128)(2,1)S(1)}, bf16[8,32,288]{2,1,0:T(8,128)(2,1)S(1)}, u32[]{:S(2)}, u32[]{:S(2)}) collective-permute-start(bf16[8,32,288]{2,1,0:T(8,128)(2,1)S(1)} %collective-permute-done.11.c_ref), channel_id=1, source_target_pairs={{0,1},{1,0},{2,3},{3,2},{4,5},{5,4},{6,7},{7,6},{8,9},{9,8},{10,11... | collective-permute-start | bytes 442376 | tf_op jit(solution)/shard_map/ppermute | solution.py:30
  135.7 2.4 %copy-start.16 = (bf16[16,768]{1,0:T(8,128)(2,1)}, bf16[16,768]{1,0:T(8,128)(2,1)S(1)}, u32[]{:S(2)}) copy-start(bf16[16,768]{1,0:T(8,128)(2,1)S(1)} %collective-permute-done.28.refs_2_) | copy-start | bytes 73732
  135.7 1.2 collective-permute-start.27
  136.9 1.2 copy-start.17
  136.9 1.2 collective-permute-start.29
  138.1 0.6 copy-start.18
  142.5 9.5 %collective-permute-start.31 = (bf16[216,768]{1,0:T(8,128)(2,1)S(1)}, bf16[216,768]{1,0:T(8,128)(2,1)S(1)}, u32[]{:S(2)}, u32[]{:S(2)}) collective-permute-start(bf16[216,768]{1,0:T(8,128)(2,1)S(1)} %combine_all.1.a_ref), channel_id=1, source_target_pairs={{0,2},{1,3},{2,0},{3,1},{4,6},{5,7},{6,4},{7,5},{8,10},{9,11},{10,... | collective-permute-start | bytes 995336 | tf_op jit(solution)/shard_map/ppermute | solution.py:30
  144.0 10.9 %collective-permute-start.30 = (bf16[216,768]{1,0:T(8,128)(2,1)S(1)}, bf16[216,768]{1,0:T(8,128)(2,1)S(1)}, u32[]{:S(2)}, u32[]{:S(2)}) collective-permute-start(bf16[216,768]{1,0:T(8,128)(2,1)S(1)} %combine_all.1.a_ref), channel_id=1, source_target_pairs={{0,1},{1,0},{2,3},{3,2},{4,5},{5,4},{6,7},{7,6},{8,9},{9,8},{10,11... | collective-permute-start | bytes 995336 | tf_op jit(solution)/shard_map/ppermute | solution.py:30
  151.9 3.0 %collective-permute-start.32 = (bf16[216,768]{1,0:T(8,128)(2,1)S(1)}, bf16[216,768]{1,0:T(8,128)(2,1)S(1)}, u32[]{:S(2)}, u32[]{:S(2)}) collective-permute-start(bf16[216,768]{1,0:T(8,128)(2,1)S(1)} %collective-permute-done.31.c_ref), channel_id=1, source_target_pairs={{0,1},{1,0},{2,3},{3,2},{4,5},{5,4},{6,7},{7,6},{8,9},{9,8},{10,11... | collective-permute-start | bytes 995336 | tf_op jit(solution)/shard_map/ppermute | solution.py:30

commit v2 on v1

--- a/solution.py
+++ b/solution.py
@@ -1120,22 +1120,33 @@
             4,
         )[0]
         known["all"] = merged
-        feed_all = spread_rows(gate("AGF", merged))
-        known["AGF"] = feed_all[1:]
+        merged = gate("AGF", merged)
+        across = swap(merged, "rows", 2)
+        feed_all = [merged, swap(merged, "rows", 1), across]
         grad_qkv_weight, grad_qv_bias = call(
             finish_heads_kernel, "finish_heads", gate("finh", heads_all),
             [((share, 3 * D), F32), ((1, 192), F32)],
         )
         known["finh"] = grad_qkv_weight
+        grad_qv_bias, grad_up_bias = grad_qv_bias[0], grad_up_bias[0]
+        grad_out_bias, grad_down_bias = bias_sums[0], bias_sums[1]
+        grad_norm_gain, grad_norm_bias = norm_sums[:2], norm_sums[2:]
+        others = (
+            grad_qkv_weight, grad_qv_bias, grad_up_bias, grad_out_bias, grad_down_bias,
+            grad_norm_gain, grad_norm_bias,
+        )
+        others, held = lax.optimization_barrier((others, across))
+        (
+            grad_qkv_weight, grad_qv_bias, grad_up_bias, grad_out_bias, grad_down_bias,
+            grad_norm_gain, grad_norm_bias,
+        ) = others
+        feed_all.append(swap(held, "rows", 1))
         grad_up_weight, grad_down_weight, grad_out_weight = call(
             finish_all_kernel, "finish_all", gate("finf", feed_all),
             [((share, FF), F32), ((FF // seqs, D), F32), ((share, D), F32)],
             [((4, 120, D), F32)],
         )
         known["finf"] = grad_out_weight
-        grad_qv_bias, grad_up_bias = grad_qv_bias[0], grad_up_bias[0]
-        grad_out_bias, grad_down_bias = bias_sums[0], bias_sums[1]
-        grad_norm_gain, grad_norm_bias = norm_sums[:2], norm_sums[2:]
     else:
         doc_grad = gather_rows(doc_grad[:DOCS], rank).reshape(ranks * DOCS, D)
         grad_time_weight = lax.dot_general(

time: 158 us -> 156 us (0.987)
    unnamed x38 -> x32, local copies, waits for them, and re-layouts: 4.1 us -> 2.85 us
  transfers between devices with their start and end apart: 36 -> 36, of which waited for: 18 -> 19; matrix products, arithmetic and copies ran while one was open for 3% -> 3% of each run, Pallas kernels for 29% -> 29%
where the time goes in v2:
time: 156 us
  Pallas kernels  66.9 us (43%)
  waiting for transfers between devices  42 us (27%)
  starting transfers between devices  36.4 us (23%)
  local copies, waits for them, and re-layouts  6.01 us (4%)
  other arithmetic  3.13 us (2%)
    pallas_call x13, Pallas kernels, call(): pl.pallas_call(kernel, out_shape=tuple(((pltpu.HBM if FAR in one else plt...  66.9 us
    ppermute x32, waiting for transfers between devices, swap(): lax.ppermute(block, axis, [(i, i ^ bit) for i in range(lax.axis_size(axis...  38.2 us
    ppermute x32, starting transfers between devices, swap(): lax.ppermute(block, axis, [(i, i ^ bit) for i in range(lax.axis_size(axis...  22.8 us
    all_to_all x1, starting transfers between devices, body(): arrived = lax.all_to_all(gate('DA', packed), 'seq', 0, 0, tiled=True)  4.71 us
    all_to_all x1, starting transfers between devices, body(): back = lax.all_to_all(gate('BACK', back), 'seq', 0, 0, tiled=True)  4.59 us
    all_to_all x1, starting transfers between devices, body(): spread = lax.all_to_all(gate('GA2A', mine[0]), 'seq', 0, 0, tiled=True)  4.24 us
  transfers between devices with their start and end apart: 36, of which 19 were waited for; matrix products, arithmetic and copies ran while one was open for 3% of the time, Pallas kernels for 29%

profile of v2, /device:TPU:0, one launch (start us, length us, event | category | flops | bytes accessed | tf_op | source)
XLA Modules:
  0.0 155.6 jit_solution(6846050543005143212)
XLA Ops:
  0.7 0.8 convert_element_type.16
  1.4 0.9 fusion.1.refs_0_
  2.4 3.0 %collective-permute-start = (bf16[136,768]{1,0:T(8,128)(2,1)S(1)}, bf16[136,768]{1,0:T(8,128)(2,1)S(1)}, u32[]{:S(2)}, u32[]{:S(2)}) collective-permute-start(bf16[136,768]{1,0:T(8,128)(2,1)S(1)} %fusion.1.refs_0_), channel_id=1, source_target_pairs={{0,4},{4,0},{8,12},{12,8},{16,20},{20,16},{24,28},{28,24},{1,5},{5... | collective-permute-start | bytes 626696 | tf_op jit(solution)/shard_map/ppermute | solution.py:30
  5.4 3.6 %collective-permute-start.5 = (bf16[136,768]{1,0:T(8,128)(2,1)S(1)}, bf16[136,768]{1,0:T(8,128)(2,1)S(1)}, u32[]{:S(2)}, u32[]{:S(2)}) collective-permute-start(bf16[136,768]{1,0:T(8,128)(2,1)S(1)} %fusion.1.refs_0_), channel_id=1, source_target_pairs={{0,24},{4,28},{8,16},{12,20},{16,8},{20,12},{24,0},{28,4},{1,25},{... | collective-permute-start | bytes 626696 | tf_op jit(solution)/shard_map/ppermute | solution.py:30
  9.0 0.8 collective-permute-start.3
  9.8 0.7 convert_bitcast_fusion
  10.5 0.7 reshape.49.refs_10_.bias_ref
  11.2 0.7 reshape.50.refs_12_
  11.8 0.7 reshape.52.refs_19_
  12.7 0.3 fusion.4.refs_8_
  13.0 2.2 %collective-permute-done.5.refs_6_ = bf16[136,768]{1,0:T(8,128)(2,1)S(1)} collective-permute-done((bf16[136,768]{1,0:T(8,128)(2,1)S(1)}, bf16[136,768]{1,0:T(8,128)(2,1)S(1)}, u32[]{:S(2)}, u32[]{:S(2)}) %collective-permute-start.5) | collective-permute-done | bytes 208928 | tf_op jit(solution)/shard_map/ppermute | solution.py:30
  15.5 3.8 %collective-permute-done.1.refs_2_ = bf16[136,768]{1,0:T(8,128)(2,1)S(1)} collective-permute-done((bf16[136,768]{1,0:T(8,128)(2,1)S(1)}, bf16[136,768]{1,0:T(8,128)(2,1)S(1)}, u32[]{:S(2)}, u32[]{:S(2)}) %collective-permute-start.1) | collective-permute-done | bytes 208928 | tf_op jit(solution)/shard_map/ppermute | solution.py:30
  19.3 0.6 collective-permute-start.2
  19.9 6.6 %collective-permute-done.3.refs_4_ = bf16[136,768]{1,0:T(8,128)(2,1)S(1)} collective-permute-done((bf16[136,768]{1,0:T(8,128)(2,1)S(1)}, bf16[136,768]{1,0:T(8,128)(2,1)S(1)}, u32[]{:S(2)}, u32[]{:S(2)}) %collective-permute-start.3) | collective-permute-done | bytes 208928 | tf_op jit(solution)/shard_map/ppermute | solution.py:30
  26.5 0.5 collective-permute-start.4
  27.0 5.1 %fetch.1 = (bf16[768,2304]{1,0:T(8,128)(2,1)S(1)}, bf16[768,768]{1,0:T(8,128)(2,1)S(1)}, bf16[768,3072]{1,0:T(8,128)(2,1)S(1)}, bf16[3072,768]{1,0:T(8,128)(2,1)S(1)}) custom-call(bf16[768,2304]{1,0:T(8,128)(2,1)} %qkv_in.3, bf16[768,768]{1,0:T(8,128)(2,1)} %refs_1_.1, bf16[768,3072]{1,0:T(8,128)(2,1)} %up_in.1, bf16[3072,768]{1,0:T(8,128)(2,1)} %refs_10_.1), custom_call_target="tpu_custom_call" | custom-call | flops 7000000000 | tf_op jit(solution)/shard_map/fetch/pallas_call | solution.py:67
  32.1 0.5 collective-permute-done.4.refs_5_
  32.7 12.3 %forward.1 = (bf16[1024,768]{1,0:T(8,128)(2,1)}, f32[128,128]{1,0:T(8,128)S(1)}, f32[128,768]{1,0:T(8,128)S(1)}, bf16[16,1024]{1,0:T(8,128)(2,1)S(1)}, f32[128,7...) custom-call(bf16[136,768]{1,0:T(8,128)(2,1)S(1)} %fusion.1.refs_0_, ...), custom_call_target="tpu_custom_call" | custom-call | flops 12000000000 | tf_op jit(solution)/shard_map/forward/pallas_call | solution.py:67
  44.9 5.9 %backward.1 = (bf16[8,176,128]{2,1,0:T(8,128)(2,1)}, f32[128,768]{1,0:T(8,128)}, f32[16,768]{1,0:T(8,128)}, bf16[16,1024]{1,0:T(8,128)(2,1)}, bf16[128,2304]{1,0...) custom-call(f32[128,768]{1,0:T(8,128)S(1)} %get-tuple-element.103.z1_ref, ...), custom_call_target="tpu_custom_call" | custom-call | flops 5000000000 | tf_op jit(solution)/shard_map/backward/pallas_call | solution.py:67
  50.8 4.7 %all-to-all-start = ((bf16[8,176,128]{2,1,0:T(8,128)(2,1)}), bf16[8,176,128]{2,1,0:T(8,128)(2,1)S(1)}, u32[]{:S(2)}, u32[]{:S(2)}) async-start(bf16[8,176,128]{2,1,0:T(8,128)(2,1)} %get-tuple-element.114), calls=%async_computation | async-start | bytes 720896 | tf_op jit(solution)/shard_map/all_to_all | solution.py:1034
  55.5 1.5 collective-permute-start.20
  57.1 2.0 %collective-permute-start.21 = (bf16[128,2304]{1,0:T(8,128)(2,1)}, bf16[128,2304]{1,0:T(8,128)(2,1)}, u32[]{:S(2)}, u32[]{:S(2)}) collective-permute-start(bf16[128,2304]{1,0:T(8,128)(2,1)} %get-tuple-element.133), channel_id=1, source_target_pairs={{0,4},{4,0},{8,12},{12,8},{16,20},{20,16},{24,28},{28,24},{1,5},{5... | collective-permute-start | bytes 1769480 | tf_op jit(solution)/shard_map/ppermute | solution.py:30
  59.1 4.1 %heads.1 = (bf16[1024,128]{1,0:T(8,128)(2,1)}, bf16[1024,128]{1,0:T(8,128)(2,1)}, bf16[1024,128]{1,0:T(8,128)(2,1)}, bf16[768,384]{1,0:T(8,128)(2,1)}) custom-call(bf16[1024,768]{1,0:T(8,128)(2,1)} %get-tuple-element.97.x_in.refs_6_, bf16[768,2304]{1,0:T(8,128)(2,1)} %qkv_in.3, f32[1,1536]{1,0:T(1,128)S(1)} %reshape.49.refs_10_.bias_ref), custom_call_target="tpu_custom_call" | custom-call | flops 3000000000 | tf_op jit(solution)/shard_map/heads/pallas_call | solution.py:67
  63.2 1.4 all-to-all-done.refs_7_
  64.6 12.2 %head_grad.1 = (bf16[8,384,128]{2,1,0:T(8,128)(2,1)}, f32[16,128]{1,0:T(8,128)S(1)}, bf16[8,32,288]{2,1,0:T(8,128)(2,1)S(1)}, bf16[8,32,288]{2,1,0:T(8,128)(2,1)...) custom-call(bf16[768,384]{1,0:T(8,128)(2,1)} %get-tuple-element.98.refs_0_, ...), custom_call_target="tpu_custom_call" | custom-call | flops 12000000000 | tf_op jit(solution)/shard_map/head_grad/pallas_call | solution.py:67
  76.7 4.6 %all-to-all-start.1 = ((bf16[8,384,128]{2,1,0:T(8,128)(2,1)}), bf16[8,384,128]{2,1,0:T(8,128)(2,1)S(1)}, u32[]{:S(2)}, u32[]{:S(2)}) async-start(bf16[8,384,128]{2,1,0:T(8,128)(2,1)} %get-tuple-element.116), calls=%async_computation.1 | async-start | bytes 1572864 | tf_op jit(solution)/shard_map/all_to_all | solution.py:1067
  81.3 5.2 %part_weights.1 = (bf16[768,768]{1,0:T(8,128)(2,1)}, f32[1,768]{1,0:T(1,128)S(1)}) custom-call(bf16[768,3072]{1,0:T(8,128)(2,1)} %up_in.1, f32[1,3072]{1,0:T(1,128)S(1)} %bitcast.16), custom_call_target="tpu_custom_call" | custom-call | flops 3000000000 | tf_op jit(solution)/shard_map/part_weights/pallas_call | solution.py:67
  86.6 5.6 %collective-permute-done.21.refs_3_ = bf16[128,2304]{1,0:T(8,128)(2,1)} collective-permute-done((bf16[128,2304]{1,0:T(8,128)(2,1)}, bf16[128,2304]{1,0:T(8,128)(2,1)}, u32[]{:S(2)}, u32[]{:S(2)}) %collective-permute-start.21) | collective-permute-done | bytes 589856 | tf_op jit(solution)/shard_map/ppermute | solution.py:30
  92.2 0.5 collective-permute-start.24
  92.7 0.5 collective-permute-start.7
  93.2 1.2 collective-permute-done.23.refs_5_
  94.6 1.0 collective-permute-done.24.refs_6_
  95.5 0.8 collective-permute-done.25.refs_7_
  96.4 0.8 copy-done.9
  97.2 8.9 %feed_grad.1 = (f32[2,120,768]{2,1,0:T(8,128)}, bf16[2,120,768]{2,1,0:T(8,128)(2,1)S(1)}, f32[2,96,768]{2,1,0:T(8,128)}, bf16[2,96,768]{2,1,0:T(8,128)(2,1)S(1)}) custom-call(bf16[128,2304]{1,0:T(8,128)(2,1)} %get-tuple-element.131.refs_0_, bf16[128,2304]{1,0:T(8,128)(2,1)} %copy-done.6, bf16[128,2304]{1,0:T(8,128)(2,1)} %collective-permute-done.20.refs_2_, ...), custom_call_target="tpu_custom_call" | custom-call | flops 8000000000 | tf_op jit(solution)/shard_map/feed_grad/pallas_call | solution.py:67
  106.2 3.1 %collective-permute-start.27 = (bf16[2,96,768]{2,1,0:T(8,128)(2,1)S(1)}, bf16[2,96,768]{2,1,0:T(8,128)(2,1)S(1)}, u32[]{:S(2)}, u32[]{:S(2)}) collective-permute-start(bf16[2,96,768]{2,1,0:T(8,128)(2,1)S(1)} %get-tuple-element.146), channel_id=1, source_target_pairs={{0,16},{4,20},{8,24},{12,28},{16,0},{20,4},{24,8},{28,12},{1,17},{... | collective-permute-start | bytes 884744 | tf_op jit(solution)/shard_map/ppermute | solution.py:30
  109.3 0.7 copy-done.11
  109.9 0.7 copy-done.12
  110.6 5.1 %input_grad.1 = (f32[128,768]{1,0:T(8,128)}, f32[32,768]{1,0:T(8,128)S(1)}, bf16[8,32,288]{2,1,0:T(8,128)(2,1)}) custom-call(bf16[8,384,128]{2,1,0:T(8,128)(2,1)S(1)} %all-to-all-done.1.back_ref, f32[128,768]{1,0:T(8,128)} %get-tuple-element.117.dr1_in, bf16[768,2304]{1,0:T(8,128)(2,1)} %qkv_in.3, f32[16,128]{1,0:T(8,128)S(1)} %get-tuple-element.118.sums_ref, ...), custom_call_target="tpu_custom_call" | custom-call | flops 5000000000 | tf_op jit(solution)/shard_map/input_grad/pallas_call | solution.py:67
  115.7 4.2 %all-to-all-start.2 = ((bf16[8,32,288]{2,1,0:T(8,128)(2,1)}), bf16[8,32,288]{2,1,0:T(8,128)(2,1)S(1)}, u32[]{:S(2)}, u32[]{:S(2)}) async-start(bf16[8,32,288]{2,1,0:T(8,128)(2,1)} %get-tuple-element.124), calls=%async_computation.2 | async-start | bytes 393216 | tf_op jit(solution)/shard_map/all_to_all | solution.py:1086
  119.9 0.4 collective-permute-start.17
  120.3 4.2 %collective-permute-done.17.refs_6_ = f32[32,768]{1,0:T(8,128)S(1)} collective-permute-done((f32[32,768]{1,0:T(8,128)S(1)}, f32[32,768]{1,0:T(8,128)S(1)}, u32[]{:S(2)}, u32[]{:S(2)}) %collective-permute-start.17) | collective-permute-done | bytes 98336 | tf_op jit(solution)/shard_map/ppermute | solution.py:30
  124.6 1.3 collective-permute-done.18.refs_7_
  125.8 2.4 %all-to-all-done.2.a_ref = bf16[8,32,288]{2,1,0:T(8,128)(2,1)S(1)} async-done(((bf16[8,32,288]{2,1,0:T(8,128)(2,1)}), bf16[8,32,288]{2,1,0:T(8,128)(2,1)S(1)}, u32[]{:S(2)}, u32[]{:S(2)}) %all-to-all-start.2) | async-done | bytes 147488 | tf_op jit(solution)/shard_map/all_to_all | solution.py:1086
  128.5 1.6 %combine_half.1 = (bf16[120,768]{1,0:T(8,128)(2,1)S(1)}, bf16[96,768]{1,0:T(8,128)(2,1)S(1)}) custom-call(f32[2,120,768]{2,1,0:T(8,128)} %get-tuple-element.141.up_in, f32[2,96,768]{2,1,0:T(8,128)} %get-tuple-element.142.down_in, bf16[2,120,768]{2,1,0:T(8,128)(2,1)} %collective-permute-done.26.up_got_in, bf16[2,96,768]{2,1,0:T(8,128)(2,1)} %copy-done.10), custom_call_target="tpu_custom_call" | custom-call | flops 1000000000 | tf_op jit(solution)/shard_map/combine_half/pallas_call | solution.py:67
  130.0 1.7 %collective-permute-start.28 = (bf16[120,768]{1,0:T(8,128)(2,1)S(1)}, bf16[120,768]{1,0:T(8,128)(2,1)S(1)}, u32[]{:S(2)}, u32[]{:S(2)}) collective-permute-start(bf16[120,768]{1,0:T(8,128)(2,1)S(1)} %get-tuple-element.149), channel_id=1, source_target_pairs={{0,16},{4,20},{8,24},{12,28},{16,0},{20,4},{24,8},{28,12},{1,17},{... | collective-permute-start | bytes 552968 | tf_op jit(solution)/shard_map/ppermute | solution.py:30
  131.7 1.6 %collective-permute-start.14 = (bf16[16,768]{1,0:T(8,128)(2,1)S(1)}, bf16[16,768]{1,0:T(8,128)(2,1)S(1)}, u32[]{:S(2)}, u32[]{:S(2)}) collective-permute-start(bf16[16,768]{1,0:T(8,128)(2,1)S(1)} %pad_maximum_fusion.refs_0_), channel_id=1, source_target_pairs={{0,2},{1,3},{2,0},{3,1},{4,6},{5,7},{6,4},{7,5},{8,10},{9,11},{10,... | collective-permute-start | bytes 73736 | tf_op jit(solution)/shard_map/ppermute | solution.py:30
  133.4 0.5 collective-permute-start.29
  133.9 0.9 collective-permute-done.11.c_ref
  134.8 0.8 collective-permute-done.14.refs_2_
  135.6 1.2 collective-permute-done.13.refs_1_
  136.9 1.0 collective-permute-done.15.refs_3_
  138.0 0.6 copy-done.15
  138.6 1.9 %time_grad.1 = (f32[96,768]{1,0:T(8,128)}, f32[4,96]{1,0:T(4,128)S(1)}, f32[2,96]{1,0:T(2,128)S(1)}, f32[1,384]{1,0:T(1,128)S(1)}) custom-call(bf16[16,768]{1,0:T(8,128)(2,1)} %copy-done.5, bf16[16,768]{1,0:T(8,128)(2,1)} %copy-done.14, bf16[16,768]{1,0:T(8,128)(2,1)} %copy-done.13, bf16[16,768]{1,0:T(8,128)(2,1)} %copy-done.15, ...), custom_call_target="tpu_custom_call" | custom-call | flops 1000000000 | tf_op jit(solution)/shard_map/time_grad/pallas_call | solution.py:67
  140.6 0.5 collective-permute-done.29.down_last_ref
  141.1 1.3 combine_all.1.a_ref
  142.4 1.5 collective-permute-start.30
  143.9 0.5 slice_bitcast_fusion
  144.4 0.6 reduce
  145.0 0.6 fusion.5
  145.6 1.3 finish_heads.1
  146.8 5.0 %collective-permute-done.30.c_ref = bf16[216,768]{1,0:T(8,128)(2,1)S(1)} collective-permute-done((bf16[216,768]{1,0:T(8,128)(2,1)S(1)}, bf16[216,768]{1,0:T(8,128)(2,1)S(1)}, u32[]{:S(2)}, u32[]{:S(2)}) %collective-permute-start.30) | collective-permute-done | bytes 331808 | tf_op jit(solution)/shard_map/ppermute | solution.py:30
  151.8 1.6 %collective-permute-done.32.d_ref = bf16[216,768]{1,0:T(8,128)(2,1)S(1)} collective-permute-done((bf16[216,768]{1,0:T(8,128)(2,1)S(1)}, bf16[216,768]{1,0:T(8,128)(2,1)S(1)}, u32[]{:S(2)}, u32[]{:S(2)}) %collective-permute-start.32) | collective-permute-done | bytes 331808 | tf_op jit(solution)/shard_map/ppermute | solution.py:30
  153.5 2.1 %finish_all.1 = (f32[96,3072]{1,0:T(8,128)}, f32[384,768]{1,0:T(8,128)}, f32[96,768]{1,0:T(8,128)}) custom-call(bf16[216,768]{1,0:T(8,128)(2,1)S(1)} %combine_all.1.a_ref, bf16[216,768]{1,0:T(8,128)(2,1)S(1)} %collective-permute-done.31.b_ref, bf16[216,768]{1,0:T(8,128)(2,1)S(1)} %collective-permute-done.30.c_ref, ...), custom_call_target="tpu_custom_call" | custom-call | flops 2000000000 | tf_op jit(solution)/shard_map/finish_all/pallas_call | solution.py:67
  (66 shorter events, 1.3 us)
Async XLA Ops:
  0.6 12.1 %copy-start = (bf16[768,768]{1,0:T(8,128)(2,1)S(1)}, bf16[768,768]{1,0:T(8,128)(2,1)}, u32[]{:S(2)}) copy-start(bf16[768,768]{1,0:T(8,128)(2,1)} %param.29) | copy-start | bytes 3538948
  2.4 10.7 %collective-permute-start = (bf16[136,768]{1,0:T(8,128)(2,1)S(1)}, bf16[136,768]{1,0:T(8,128)(2,1)S(1)}, u32[]{:S(2)}, u32[]{:S(2)}) collective-permute-start(bf16[136,768]{1,0:T(8,128)(2,1)S(1)} %fusion.1.refs_0_), channel_id=1, source_target_pairs={{0,4},{4,0},{8,12},{12,8},{16,20},{20,16},{24,28},{28,24},{1,5},{5... | collective-permute-start | bytes 626696 | tf_op jit(solution)/shard_map/ppermute | solution.py:30
  5.4 9.9 %collective-permute-start.5 = (bf16[136,768]{1,0:T(8,128)(2,1)S(1)}, bf16[136,768]{1,0:T(8,128)(2,1)S(1)}, u32[]{:S(2)}, u32[]{:S(2)}) collective-permute-start(bf16[136,768]{1,0:T(8,128)(2,1)S(1)} %fusion.1.refs_0_), channel_id=1, source_target_pairs={{0,24},{4,28},{8,16},{12,20},{16,8},{20,12},{24,0},{28,4},{1,25},{... | collective-permute-start | bytes 626696 | tf_op jit(solution)/shard_map/ppermute | solution.py:30
  9.0 10.3 %collective-permute-start.1 = (bf16[136,768]{1,0:T(8,128)(2,1)S(1)}, bf16[136,768]{1,0:T(8,128)(2,1)S(1)}, u32[]{:S(2)}, u32[]{:S(2)}) collective-permute-start(bf16[136,768]{1,0:T(8,128)(2,1)S(1)} %fusion.1.refs_0_), channel_id=1, source_target_pairs={{0,8},{4,12},{8,0},{12,4},{16,24},{20,28},{24,16},{28,20},{1,9},{5... | collective-permute-start | bytes 626696 | tf_op jit(solution)/shard_map/ppermute | solution.py:30
  9.0 17.5 %collective-permute-start.3 = (bf16[136,768]{1,0:T(8,128)(2,1)S(1)}, bf16[136,768]{1,0:T(8,128)(2,1)S(1)}, u32[]{:S(2)}, u32[]{:S(2)}) collective-permute-start(bf16[136,768]{1,0:T(8,128)(2,1)S(1)} %fusion.1.refs_0_), channel_id=1, source_target_pairs={{0,16},{4,20},{8,24},{12,28},{16,0},{20,4},{24,8},{28,12},{1,17},{... | collective-permute-start | bytes 626696 | tf_op jit(solution)/shard_map/ppermute | solution.py:30
  13.0 19.7 %copy-start.1 = (bf16[1,128,768]{2,1,0:T(8,128)(2,1)S(1)}, bf16[1,128,768]{2,1,0:T(8,128)(2,1)}, u32[]{:S(2)}) copy-start(bf16[1,128,768]{2,1,0:T(8,128)(2,1)} %param.16) | copy-start | bytes 589828
  13.0 19.7 %copy-start.2 = (f32[3072]{0:T(1024)S(1)}, f32[3072]{0:T(1024)}, u32[]{:S(2)}) copy-start(f32[3072]{0:T(1024)} %param.24) | copy-start | bytes 36868
  13.0 19.7 %copy-start.3 = (f32[2,768]{1,0:T(2,128)S(1)}, f32[2,768]{1,0:T(2,128)}, u32[]{:S(2)}) copy-start(f32[2,768]{1,0:T(2,128)} %refs_14_.1) | copy-start | bytes 18436
  13.0 19.7 %copy-start.4 = (f32[2,768]{1,0:T(2,128)S(1)}, f32[2,768]{1,0:T(2,128)}, u32[]{:S(2)}) copy-start(f32[2,768]{1,0:T(2,128)} %gain_ref.1) | copy-start | bytes 18436
  15.3 16.8 %collective-permute-start.6 = (bf16[136,768]{1,0:T(8,128)(2,1)S(1)}, bf16[136,768]{1,0:T(8,128)(2,1)S(1)}, u32[]{:S(2)}, u32[]{:S(2)}) collective-permute-start(bf16[136,768]{1,0:T(8,128)(2,1)S(1)} %collective-permute-done.5.refs_6_), channel_id=1, source_target_pairs={{0,4},{4,0},{8,12},{12,8},{16,20},{20,16},{24,28},{28,24},{1,5},{5... | collective-permute-start | bytes 626696 | tf_op jit(solution)/shard_map/ppermute | solution.py:30
  19.3 12.9 %collective-permute-start.2 = (bf16[136,768]{1,0:T(8,128)(2,1)S(1)}, bf16[136,768]{1,0:T(8,128)(2,1)S(1)}, u32[]{:S(2)}, u32[]{:S(2)}) collective-permute-start(bf16[136,768]{1,0:T(8,128)(2,1)S(1)} %collective-permute-done.1.refs_2_), channel_id=1, source_target_pairs={{0,4},{4,0},{8,12},{12,8},{16,20},{20,16},{24,28},{28,24},{1,5},{5... | collective-permute-start | bytes 626696 | tf_op jit(solution)/shard_map/ppermute | solution.py:30
  26.5 6.2 %collective-permute-start.4 = (bf16[136,768]{1,0:T(8,128)(2,1)S(1)}, bf16[136,768]{1,0:T(8,128)(2,1)S(1)}, u32[]{:S(2)}, u32[]{:S(2)}) collective-permute-start(bf16[136,768]{1,0:T(8,128)(2,1)S(1)} %collective-permute-done.3.refs_4_), channel_id=1, source_target_pairs={{0,4},{4,0},{8,12},{12,8},{16,20},{20,16},{24,28},{28,24},{1,5},{5... | collective-permute-start | bytes 626696 | tf_op jit(solution)/shard_map/ppermute | solution.py:30
  50.8 13.7 %all-to-all-start = ((bf16[8,176,128]{2,1,0:T(8,128)(2,1)}), bf16[8,176,128]{2,1,0:T(8,128)(2,1)S(1)}, u32[]{:S(2)}, u32[]{:S(2)}) async-start(bf16[8,176,128]{2,1,0:T(8,128)(2,1)} %get-tuple-element.114), calls=%async_computation | async-start | bytes 720896 | tf_op jit(solution)/shard_map/all_to_all | solution.py:1034
  55.5 25.8 %collective-permute-start.19 = (bf16[128,2304]{1,0:T(8,128)(2,1)}, bf16[128,2304]{1,0:T(8,128)(2,1)S(1)}, u32[]{:S(2)}, u32[]{:S(2)}) collective-permute-start(bf16[128,2304]{1,0:T(8,128)(2,1)} %get-tuple-element.131.refs_0_), channel_id=1, source_target_pairs={{0,1},{1,0},{2,3},{3,2},{4,5},{5,4},{6,7},{7,6},{8,9},{9,8},{10,11... | collective-permute-start | bytes 1769480 | tf_op jit(solution)/shard_map/ppermute | solution.py:30
  55.5 31.1 %collective-permute-start.20 = (bf16[128,2304]{1,0:T(8,128)(2,1)}, bf16[128,2304]{1,0:T(8,128)(2,1)}, u32[]{:S(2)}, u32[]{:S(2)}) collective-permute-start(bf16[128,2304]{1,0:T(8,128)(2,1)} %get-tuple-element.132), channel_id=1, source_target_pairs={{0,2},{1,3},{2,0},{3,1},{4,6},{5,7},{6,4},{7,5},{8,10},{9,11},{10,... | collective-permute-start | bytes 1769480 | tf_op jit(solution)/shard_map/ppermute | solution.py:30
  57.1 35.1 %collective-permute-start.21 = (bf16[128,2304]{1,0:T(8,128)(2,1)}, bf16[128,2304]{1,0:T(8,128)(2,1)}, u32[]{:S(2)}, u32[]{:S(2)}) collective-permute-start(bf16[128,2304]{1,0:T(8,128)(2,1)} %get-tuple-element.133), channel_id=1, source_target_pairs={{0,4},{4,0},{8,12},{12,8},{16,20},{20,16},{24,28},{28,24},{1,5},{5... | collective-permute-start | bytes 1769480 | tf_op jit(solution)/shard_map/ppermute | solution.py:30
  59.0 33.1 %collective-permute-start.22 = (bf16[128,2304]{1,0:T(8,128)(2,1)}, bf16[128,2304]{1,0:T(8,128)(2,1)}, u32[]{:S(2)}, u32[]{:S(2)}) collective-permute-start(bf16[128,2304]{1,0:T(8,128)(2,1)} %get-tuple-element.134), channel_id=1, source_target_pairs={{0,6},{1,7},{2,4},{3,5},{4,2},{5,3},{6,0},{7,1},{8,14},{9,15},{10,... | collective-permute-start | bytes 1769480 | tf_op jit(solution)/shard_map/ppermute | solution.py:809
  76.7 33.9 %all-to-all-start.1 = ((bf16[8,384,128]{2,1,0:T(8,128)(2,1)}), bf16[8,384,128]{2,1,0:T(8,128)(2,1)S(1)}, u32[]{:S(2)}, u32[]{:S(2)}) async-start(bf16[8,384,128]{2,1,0:T(8,128)(2,1)} %get-tuple-element.116), calls=%async_computation.1 | async-start | bytes 1572864 | tf_op jit(solution)/shard_map/all_to_all | solution.py:1067
  81.3 5.3 %copy-start.6 = (bf16[128,2304]{1,0:T(8,128)(2,1)}, bf16[128,2304]{1,0:T(8,128)(2,1)S(1)}, u32[]{:S(2)}) copy-start(bf16[128,2304]{1,0:T(8,128)(2,1)S(1)} %collective-permute-done.19.refs_1_) | copy-start | bytes 1769476
  92.2 2.2 %collective-permute-start.23 = (bf16[128,2304]{1,0:T(8,128)(2,1)}, bf16[128,2304]{1,0:T(8,128)(2,1)S(1)}, u32[]{:S(2)}, u32[]{:S(2)}) collective-permute-start(bf16[128,2304]{1,0:T(8,128)(2,1)} %collective-permute-done.20.refs_2_), channel_id=1, source_target_pairs={{0,1},{1,0},{2,3},{3,2},{4,5},{5,4},{6,7},{7,6},{8,9},{9,8},{10,11... | collective-permute-start | bytes 1769480 | tf_op jit(solution)/shard_map/ppermute | solution.py:30
  92.2 3.3 %collective-permute-start.24 = (bf16[128,2304]{1,0:T(8,128)(2,1)}, bf16[128,2304]{1,0:T(8,128)(2,1)S(1)}, u32[]{:S(2)}, u32[]{:S(2)}) collective-permute-start(bf16[128,2304]{1,0:T(8,128)(2,1)} %collective-permute-done.21.refs_3_), channel_id=1, source_target_pairs={{0,1},{1,0},{2,3},{3,2},{4,5},{5,4},{6,7},{7,6},{8,9},{9,8},{10,11... | collective-permute-start | bytes 1769480 | tf_op jit(solution)/shard_map/ppermute | solution.py:30
  92.7 3.7 %collective-permute-start.25 = (bf16[128,2304]{1,0:T(8,128)(2,1)}, bf16[128,2304]{1,0:T(8,128)(2,1)S(1)}, u32[]{:S(2)}, u32[]{:S(2)}) collective-permute-start(bf16[128,2304]{1,0:T(8,128)(2,1)} %collective-permute-done.22.refs_4_), channel_id=1, source_target_pairs={{0,1},{1,0},{2,3},{3,2},{4,5},{5,4},{6,7},{7,6},{8,9},{9,8},{10,11... | collective-permute-start | bytes 1769480 | tf_op jit(solution)/shard_map/ppermute | solution.py:30
  92.7 16.6 %collective-permute-start.7 = (bf16[8,32,288]{2,1,0:T(8,128)(2,1)S(1)}, bf16[8,32,288]{2,1,0:T(8,128)(2,1)S(1)}, u32[]{:S(2)}, u32[]{:S(2)}) collective-permute-start(bf16[8,32,288]{2,1,0:T(8,128)(2,1)S(1)} %get-tuple-element.120), channel_id=1, source_target_pairs={{0,1},{1,0},{2,3},{3,2},{4,5},{5,4},{6,7},{7,6},{8,9},{9,8},{10,11... | collective-permute-start | bytes 442376 | tf_op jit(solution)/shard_map/ppermute | solution.py:30
  93.2 16.1 %collective-permute-start.8 = (bf16[8,32,288]{2,1,0:T(8,128)(2,1)S(1)}, bf16[8,32,288]{2,1,0:T(8,128)(2,1)S(1)}, u32[]{:S(2)}, u32[]{:S(2)}) collective-permute-start(bf16[8,32,288]{2,1,0:T(8,128)(2,1)S(1)} %get-tuple-element.121), channel_id=1, source_target_pairs={{0,2},{1,3},{2,0},{3,1},{4,6},{5,7},{6,4},{7,5},{8,10},{9,11},{10,... | collective-permute-start | bytes 442376 | tf_op jit(solution)/shard_map/ppermute | solution.py:30
  94.4 2.0 %copy-start.7 = (bf16[128,2304]{1,0:T(8,128)(2,1)}, bf16[128,2304]{1,0:T(8,128)(2,1)S(1)}, u32[]{:S(2)}) copy-start(bf16[128,2304]{1,0:T(8,128)(2,1)S(1)} %collective-permute-done.23.refs_5_) | copy-start | bytes 1769476
  94.4 16.2 %collective-permute-start.9 = (bf16[8,32,288]{2,1,0:T(8,128)(2,1)S(1)}, bf16[8,32,288]{2,1,0:T(8,128)(2,1)}, u32[]{:S(2)}, u32[]{:S(2)}) collective-permute-start(bf16[8,32,288]{2,1,0:T(8,128)(2,1)S(1)} %get-tuple-element.122), channel_id=1, source_target_pairs={{0,3},{1,2},{2,1},{3,0},{4,7},{5,6},{6,5},{7,4},{8,11},{9,10},{10,... | collective-permute-start | bytes 442376 | tf_op jit(solution)/shard_map/ppermute | solution.py:30
  95.5 0.9 copy-start.8
  96.4 0.8 copy-start.9
  106.1 18.5 %collective-permute-start.26 = (bf16[2,120,768]{2,1,0:T(8,128)(2,1)S(1)}, bf16[2,120,768]{2,1,0:T(8,128)(2,1)}, u32[]{:S(2)}, u32[]{:S(2)}) collective-permute-start(bf16[2,120,768]{2,1,0:T(8,128)(2,1)S(1)} %get-tuple-element.145), channel_id=1, source_target_pairs={{0,8},{4,12},{8,0},{12,4},{16,24},{20,28},{24,16},{28,20},{1,9},{5... | collective-permute-start | bytes 1105928 | tf_op jit(solution)/shard_map/ppermute | solution.py:30
  106.2 18.4 %collective-permute-start.27 = (bf16[2,96,768]{2,1,0:T(8,128)(2,1)S(1)}, bf16[2,96,768]{2,1,0:T(8,128)(2,1)S(1)}, u32[]{:S(2)}, u32[]{:S(2)}) collective-permute-start(bf16[2,96,768]{2,1,0:T(8,128)(2,1)S(1)} %get-tuple-element.146), channel_id=1, source_target_pairs={{0,16},{4,20},{8,24},{12,28},{16,0},{20,4},{24,8},{28,12},{1,17},{... | collective-permute-start | bytes 884744 | tf_op jit(solution)/shard_map/ppermute | solution.py:30
  109.3 0.7 copy-start.11
  109.9 0.7 copy-start.12
  115.7 12.5 %all-to-all-start.2 = ((bf16[8,32,288]{2,1,0:T(8,128)(2,1)}), bf16[8,32,288]{2,1,0:T(8,128)(2,1)S(1)}, u32[]{:S(2)}, u32[]{:S(2)}) async-start(bf16[8,32,288]{2,1,0:T(8,128)(2,1)} %get-tuple-element.124), calls=%async_computation.2 | async-start | bytes 393216 | tf_op jit(solution)/shard_map/all_to_all | solution.py:1086
  119.9 4.6 %collective-permute-start.17 = (f32[32,768]{1,0:T(8,128)S(1)}, f32[32,768]{1,0:T(8,128)S(1)}, u32[]{:S(2)}, u32[]{:S(2)}) collective-permute-start(f32[32,768]{1,0:T(8,128)S(1)} %get-tuple-element.127.refs_4_), channel_id=1, source_target_pairs={{0,2},{1,3},{2,0},{3,1},{4,6},{5,7},{6,4},{7,5},{8,10},{9,11},{10,... | collective-permute-start | bytes 294920 | tf_op jit(solution)/shard_map/ppermute | solution.py:30
  120.3 4.3 %collective-permute-start.16 = (f32[32,768]{1,0:T(8,128)S(1)}, f32[32,768]{1,0:T(8,128)S(1)}, u32[]{:S(2)}, u32[]{:S(2)}) collective-permute-start(f32[32,768]{1,0:T(8,128)S(1)} %get-tuple-element.127.refs_4_), channel_id=1, source_target_pairs={{0,1},{1,0},{2,3},{3,2},{4,5},{5,4},{6,7},{7,6},{8,9},{9,8},{10,11... | collective-permute-start | bytes 294920 | tf_op jit(solution)/shard_map/ppermute | solution.py:30
  124.5 1.3 collective-permute-start.18
  124.6 3.9 %copy-start.10 = (bf16[2,96,768]{2,1,0:T(8,128)(2,1)}, bf16[2,96,768]{2,1,0:T(8,128)(2,1)S(1)}, u32[]{:S(2)}) copy-start(bf16[2,96,768]{2,1,0:T(8,128)(2,1)S(1)} %collective-permute-done.27.down_got_in) | copy-start | bytes 884740
  128.2 6.5 %collective-permute-start.11 = (bf16[8,32,288]{2,1,0:T(8,128)(2,1)S(1)}, bf16[8,32,288]{2,1,0:T(8,128)(2,1)S(1)}, u32[]{:S(2)}, u32[]{:S(2)}) collective-permute-start(bf16[8,32,288]{2,1,0:T(8,128)(2,1)S(1)} %all-to-all-done.2.a_ref), channel_id=1, source_target_pairs={{0,2},{1,3},{2,0},{3,1},{4,6},{5,7},{6,4},{7,5},{8,10},{9,11},{10,... | collective-permute-start | bytes 442376 | tf_op jit(solution)/shard_map/ppermute | solution.py:30
  130.0 11.0 %collective-permute-start.28 = (bf16[120,768]{1,0:T(8,128)(2,1)S(1)}, bf16[120,768]{1,0:T(8,128)(2,1)S(1)}, u32[]{:S(2)}, u32[]{:S(2)}) collective-permute-start(bf16[120,768]{1,0:T(8,128)(2,1)S(1)} %get-tuple-element.149), channel_id=1, source_target_pairs={{0,16},{4,20},{8,24},{12,28},{16,0},{20,4},{24,8},{28,12},{1,17},{... | collective-permute-start | bytes 552968 | tf_op jit(solution)/shard_map/ppermute | solution.py:30
  131.7 6.2 %copy-start.5 = (bf16[16,768]{1,0:T(8,128)(2,1)}, bf16[16,768]{1,0:T(8,128)(2,1)S(1)}, u32[]{:S(2)}) copy-start(bf16[16,768]{1,0:T(8,128)(2,1)S(1)} %pad_maximum_fusion.refs_0_) | copy-start | bytes 73732
  131.7 3.8 %collective-permute-start.14 = (bf16[16,768]{1,0:T(8,128)(2,1)S(1)}, bf16[16,768]{1,0:T(8,128)(2,1)S(1)}, u32[]{:S(2)}, u32[]{:S(2)}) collective-permute-start(bf16[16,768]{1,0:T(8,128)(2,1)S(1)} %pad_maximum_fusion.refs_0_), channel_id=1, source_target_pairs={{0,2},{1,3},{2,0},{3,1},{4,6},{5,7},{6,4},{7,5},{8,10},{9,11},{10,... | collective-permute-start | bytes 73736 | tf_op jit(solution)/shard_map/ppermute | solution.py:30
  133.4 7.7 %collective-permute-start.29 = (bf16[96,768]{1,0:T(8,128)(2,1)S(1)}, bf16[96,768]{1,0:T(8,128)(2,1)S(1)}, u32[]{:S(2)}, u32[]{:S(2)}) collective-permute-start(bf16[96,768]{1,0:T(8,128)(2,1)S(1)} %get-tuple-element.150), channel_id=1, source_target_pairs={{0,8},{4,12},{8,0},{12,4},{16,24},{20,28},{24,16},{28,20},{1,9},{5... | collective-permute-start | bytes 442376 | tf_op jit(solution)/shard_map/ppermute | solution.py:30
  133.9 7.1 %collective-permute-start.10 = (bf16[8,32,288]{2,1,0:T(8,128)(2,1)S(1)}, bf16[8,32,288]{2,1,0:T(8,128)(2,1)S(1)}, u32[]{:S(2)}, u32[]{:S(2)}) collective-permute-start(bf16[8,32,288]{2,1,0:T(8,128)(2,1)S(1)} %all-to-all-done.2.a_ref), channel_id=1, source_target_pairs={{0,1},{1,0},{2,3},{3,2},{4,5},{5,4},{6,7},{7,6},{8,9},{9,8},{10,11... | collective-permute-start | bytes 442376 | tf_op jit(solution)/shard_map/ppermute | solution.py:30
  134.8 6.3 %collective-permute-start.12 = (bf16[8,32,288]{2,1,0:T(8,128)(2,1)S(1)}, bf16[8,32,288]{2,1,0:T(8,128)(2,1)S(1)}, u32[]{:S(2)}, u32[]{:S(2)}) collective-permute-start(bf16[8,32,288]{2,1,0:T(8,128)(2,1)S(1)} %collective-permute-done.11.c_ref), channel_id=1, source_target_pairs={{0,1},{1,0},{2,3},{3,2},{4,5},{5,4},{6,7},{7,6},{8,9},{9,8},{10,11... | collective-permute-start | bytes 442376 | tf_op jit(solution)/shard_map/ppermute | solution.py:30
  135.6 2.4 %copy-start.13 = (bf16[16,768]{1,0:T(8,128)(2,1)}, bf16[16,768]{1,0:T(8,128)(2,1)S(1)}, u32[]{:S(2)}) copy-start(bf16[16,768]{1,0:T(8,128)(2,1)S(1)} %collective-permute-done.14.refs_2_) | copy-start | bytes 73732
  135.6 1.2 collective-permute-start.13
  136.8 1.2 copy-start.14
  136.8 1.2 collective-permute-start.15
  138.0 0.6 copy-start.15
  142.4 9.5 %collective-permute-start.30 = (bf16[216,768]{1,0:T(8,128)(2,1)S(1)}, bf16[216,768]{1,0:T(8,128)(2,1)S(1)}, u32[]{:S(2)}, u32[]{:S(2)}) collective-permute-start(bf16[216,768]{1,0:T(8,128)(2,1)S(1)} %combine_all.1.a_ref), channel_id=1, source_target_pairs={{0,2},{1,3},{2,0},{3,1},{4,6},{5,7},{6,4},{7,5},{8,10},{9,11},{10,... | collective-permute-start | bytes 995336 | tf_op jit(solution)/shard_map/ppermute | solution.py:30
  145.6 6.3 %collective-permute-start.31 = (bf16[216,768]{1,0:T(8,128)(2,1)S(1)}, bf16[216,768]{1,0:T(8,128)(2,1)S(1)}, u32[]{:S(2)}, u32[]{:S(2)}) collective-permute-start(bf16[216,768]{1,0:T(8,128)(2,1)S(1)} %combine_all.1.a_ref), channel_id=1, source_target_pairs={{0,1},{1,0},{2,3},{3,2},{4,5},{5,4},{6,7},{7,6},{8,9},{9,8},{10,11... | collective-permute-start | bytes 995336 | tf_op jit(solution)/shard_map/ppermute | solution.py:30
  151.8 1.6 %collective-permute-start.32 = (bf16[216,768]{1,0:T(8,128)(2,1)S(1)}, bf16[216,768]{1,0:T(8,128)(2,1)S(1)}, u32[]{:S(2)}, u32[]{:S(2)}) collective-permute-start(bf16[216,768]{1,0:T(8,128)(2,1)S(1)} %collective-permute-done.30.c_ref), channel_id=1, source_target_pairs={{0,1},{1,0},{2,3},{3,2},{4,5},{5,4},{6,7},{7,6},{8,9},{9,8},{10,11... | collective-permute-start | bytes 995336 | tf_op jit(solution)/shard_map/ppermute | solution.py:30

commit v3 on v2

--- a/solution.py
+++ b/solution.py
@@ -144,14 +144,13 @@
 ORDER = {
     "Etwin": ("part", ),
     "RS1": ("feed", "part", ),
-    "all": ("AGG", "time", ),
+    "all": ("time", ),
     "backward": ("Y3", "forward", ),
     "fetch": ("Y0", ),
     "finf": ("finh", ),
     "forward": ("Y3", ),
     "half": ("DOCS", "in", ),
-    "head": ("heads", ),
-    "part": ("E0", "head", ),
+    "part": ("head", ),
 }
 COSTS = {
     "fetch": 7, "forward": 12, "backward": 5, "heads": 3, "part_weights": 3, "feed_grad": 8,

time: 156 us -> 155 us (level)
  waiting for transfers between devices: 42 us -> 39 us
  starting transfers between devices: 36.4 us -> 38 us
    all_to_all x1, waiting for transfers between devices: 2.37 us -> 0.01 us  [body(): spread = lax.all_to_all(gate('GA2A', mine[0]), 'seq', 0, 0, tiled=True)]
    ppermute x32, starting transfers between devices: 22.8 us -> 24.7 us  [swap(): lax.ppermute(block, axis, [(i, i ^ bit) for i in range(lax.axis_size(axis...]
  transfers between devices with their start and end apart: 36 -> 36, of which waited for: 19 -> 17; matrix products, arithmetic and copies ran while one was open for 3% -> 3% of each run, Pallas kernels for 29% -> 30%
where the time goes in v3:
time: 155 us
  Pallas kernels  66.7 us (43%)
  waiting for transfers between devices  39 us (25%)
  starting transfers between devices  38 us (25%)
  local copies, waits for them, and re-layouts  6.68 us (4%)
  other arithmetic  3.13 us (2%)
    pallas_call x13, Pallas kernels, call(): pl.pallas_call(kernel, out_shape=tuple(((pltpu.HBM if FAR in one else plt...  66.7 us
    ppermute x32, waiting for transfers between devices, swap(): lax.ppermute(block, axis, [(i, i ^ bit) for i in range(lax.axis_size(axis...  37.5 us
    ppermute x32, starting transfers between devices, swap(): lax.ppermute(block, axis, [(i, i ^ bit) for i in range(lax.axis_size(axis...  24.7 us
    all_to_all x1, starting transfers between devices, body(): arrived = lax.all_to_all(gate('DA', packed), 'seq', 0, 0, tiled=True)  4.71 us
    all_to_all x1, starting transfers between devices, body(): back = lax.all_to_all(gate('BACK', back), 'seq', 0, 0, tiled=True)  4.57 us
    all_to_all x1, starting transfers between devices, body(): spread = lax.all_to_all(gate('GA2A', mine[0]), 'seq', 0, 0, tiled=True)  4.03 us
    unnamed x32, local copies, waits for them, and re-layouts  3.52 us
  transfers between devices with their start and end apart: 36, of which 17 were waited for; matrix products, arithmetic and copies ran while one was open for 3% of the time, Pallas kernels for 30%

profile of v3, /device:TPU:0, one launch (start us, length us, event | category | flops | bytes accessed | tf_op | source)
XLA Modules:
  0.0 154.7 jit_solution(6768014121540193759)
XLA Ops:
  0.7 0.8 convert_element_type.16
  1.4 0.9 fusion.1.refs_0_
  2.4 3.0 %collective-permute-start = (bf16[136,768]{1,0:T(8,128)(2,1)S(1)}, bf16[136,768]{1,0:T(8,128)(2,1)S(1)}, u32[]{:S(2)}, u32[]{:S(2)}) collective-permute-start(bf16[136,768]{1,0:T(8,128)(2,1)S(1)} %fusion.1.refs_0_), channel_id=1, source_target_pairs={{0,4},{4,0},{8,12},{12,8},{16,20},{20,16},{24,28},{28,24},{1,5},{5... | collective-permute-start | bytes 626696 | tf_op jit(solution)/shard_map/ppermute | solution.py:30
  5.4 3.6 %collective-permute-start.5 = (bf16[136,768]{1,0:T(8,128)(2,1)S(1)}, bf16[136,768]{1,0:T(8,128)(2,1)S(1)}, u32[]{:S(2)}, u32[]{:S(2)}) collective-permute-start(bf16[136,768]{1,0:T(8,128)(2,1)S(1)} %fusion.1.refs_0_), channel_id=1, source_target_pairs={{0,24},{4,28},{8,16},{12,20},{16,8},{20,12},{24,0},{28,4},{1,25},{... | collective-permute-start | bytes 626696 | tf_op jit(solution)/shard_map/ppermute | solution.py:30
  9.0 0.8 collective-permute-start.3
  9.8 0.7 convert_bitcast_fusion
  10.5 0.7 reshape.49.refs_10_.bias_ref
  11.2 0.7 reshape.50.refs_12_
  11.8 0.7 reshape.52.refs_19_
  13.0 2.2 %collective-permute-done.5.refs_6_ = bf16[136,768]{1,0:T(8,128)(2,1)S(1)} collective-permute-done((bf16[136,768]{1,0:T(8,128)(2,1)S(1)}, bf16[136,768]{1,0:T(8,128)(2,1)S(1)}, u32[]{:S(2)}, u32[]{:S(2)}) %collective-permute-start.5) | collective-permute-done | bytes 208928 | tf_op jit(solution)/shard_map/ppermute | solution.py:30
  15.5 3.8 %collective-permute-done.1.refs_2_ = bf16[136,768]{1,0:T(8,128)(2,1)S(1)} collective-permute-done((bf16[136,768]{1,0:T(8,128)(2,1)S(1)}, bf16[136,768]{1,0:T(8,128)(2,1)S(1)}, u32[]{:S(2)}, u32[]{:S(2)}) %collective-permute-start.1) | collective-permute-done | bytes 208928 | tf_op jit(solution)/shard_map/ppermute | solution.py:30
  19.3 0.6 collective-permute-start.2
  19.9 6.6 %collective-permute-done.3.refs_4_ = bf16[136,768]{1,0:T(8,128)(2,1)S(1)} collective-permute-done((bf16[136,768]{1,0:T(8,128)(2,1)S(1)}, bf16[136,768]{1,0:T(8,128)(2,1)S(1)}, u32[]{:S(2)}, u32[]{:S(2)}) %collective-permute-start.3) | collective-permute-done | bytes 208928 | tf_op jit(solution)/shard_map/ppermute | solution.py:30
  26.5 0.5 collective-permute-start.4
  27.0 5.1 %fetch.1 = (bf16[768,2304]{1,0:T(8,128)(2,1)S(1)}, bf16[768,768]{1,0:T(8,128)(2,1)S(1)}, bf16[768,3072]{1,0:T(8,128)(2,1)S(1)}, bf16[3072,768]{1,0:T(8,128)(2,1)S(1)}) custom-call(bf16[768,2304]{1,0:T(8,128)(2,1)} %qkv_in.3, bf16[768,768]{1,0:T(8,128)(2,1)} %refs_1_.1, bf16[768,3072]{1,0:T(8,128)(2,1)} %up_in.1, bf16[3072,768]{1,0:T(8,128)(2,1)} %refs_10_.1), custom_call_target="tpu_custom_call" | custom-call | flops 7000000000 | tf_op jit(solution)/shard_map/fetch/pallas_call | solution.py:67
  32.1 0.5 collective-permute-done.4.refs_5_
  32.7 12.3 %forward.1 = (bf16[1024,768]{1,0:T(8,128)(2,1)}, f32[128,128]{1,0:T(8,128)S(1)}, f32[128,768]{1,0:T(8,128)S(1)}, bf16[16,1024]{1,0:T(8,128)(2,1)S(1)}, f32[128,7...) custom-call(bf16[136,768]{1,0:T(8,128)(2,1)S(1)} %fusion.1.refs_0_, ...), custom_call_target="tpu_custom_call" | custom-call | flops 12000000000 | tf_op jit(solution)/shard_map/forward/pallas_call | solution.py:67
  44.9 5.9 %backward.1 = (bf16[8,176,128]{2,1,0:T(8,128)(2,1)}, f32[128,768]{1,0:T(8,128)}, f32[16,768]{1,0:T(8,128)}, bf16[16,1024]{1,0:T(8,128)(2,1)}, bf16[128,2304]{1,0...) custom-call(f32[128,768]{1,0:T(8,128)S(1)} %get-tuple-element.102.z1_ref, ...), custom_call_target="tpu_custom_call" | custom-call | flops 5000000000 | tf_op jit(solution)/shard_map/backward/pallas_call | solution.py:67
  50.8 4.7 %all-to-all-start = ((bf16[8,176,128]{2,1,0:T(8,128)(2,1)}), bf16[8,176,128]{2,1,0:T(8,128)(2,1)S(1)}, u32[]{:S(2)}, u32[]{:S(2)}) async-start(bf16[8,176,128]{2,1,0:T(8,128)(2,1)} %get-tuple-element.113), calls=%async_computation | async-start | bytes 720896 | tf_op jit(solution)/shard_map/all_to_all | solution.py:1033
  55.5 1.5 collective-permute-start.20
  57.0 2.0 %collective-permute-start.21 = (bf16[128,2304]{1,0:T(8,128)(2,1)}, bf16[128,2304]{1,0:T(8,128)(2,1)}, u32[]{:S(2)}, u32[]{:S(2)}) collective-permute-start(bf16[128,2304]{1,0:T(8,128)(2,1)} %get-tuple-element.131), channel_id=1, source_target_pairs={{0,4},{4,0},{8,12},{12,8},{16,20},{20,16},{24,28},{28,24},{1,5},{5... | collective-permute-start | bytes 1769480 | tf_op jit(solution)/shard_map/ppermute | solution.py:30
  59.0 4.1 %heads.1 = (bf16[1024,128]{1,0:T(8,128)(2,1)}, bf16[1024,128]{1,0:T(8,128)(2,1)}, bf16[1024,128]{1,0:T(8,128)(2,1)}, bf16[768,384]{1,0:T(8,128)(2,1)}) custom-call(bf16[1024,768]{1,0:T(8,128)(2,1)} %get-tuple-element.96.x_in.refs_6_, bf16[768,2304]{1,0:T(8,128)(2,1)} %qkv_in.3, f32[1,1536]{1,0:T(1,128)S(1)} %reshape.49.refs_10_.bias_ref), custom_call_target="tpu_custom_call" | custom-call | flops 3000000000 | tf_op jit(solution)/shard_map/heads/pallas_call | solution.py:67
  63.1 1.4 all-to-all-done.refs_7_
  64.6 12.2 %head_grad.1 = (bf16[8,384,128]{2,1,0:T(8,128)(2,1)}, f32[16,128]{1,0:T(8,128)S(1)}, bf16[8,32,288]{2,1,0:T(8,128)(2,1)S(1)}, bf16[8,32,288]{2,1,0:T(8,128)(2,1)...) custom-call(bf16[768,384]{1,0:T(8,128)(2,1)} %get-tuple-element.97.refs_0_, ...), custom_call_target="tpu_custom_call" | custom-call | flops 12000000000 | tf_op jit(solution)/shard_map/head_grad/pallas_call | solution.py:67
  76.7 4.6 %all-to-all-start.1 = ((bf16[8,384,128]{2,1,0:T(8,128)(2,1)}), bf16[8,384,128]{2,1,0:T(8,128)(2,1)S(1)}, u32[]{:S(2)}, u32[]{:S(2)}) async-start(bf16[8,384,128]{2,1,0:T(8,128)(2,1)} %get-tuple-element.114), calls=%async_computation.1 | async-start | bytes 1572864 | tf_op jit(solution)/shard_map/all_to_all | solution.py:1066
  81.3 5.0 %part_weights.1 = (bf16[768,768]{1,0:T(8,128)(2,1)}, f32[1,768]{1,0:T(1,128)S(1)}) custom-call(bf16[768,3072]{1,0:T(8,128)(2,1)} %up_in.1, f32[1,3072]{1,0:T(1,128)S(1)} %bitcast.16), custom_call_target="tpu_custom_call" | custom-call | flops 3000000000 | tf_op jit(solution)/shard_map/part_weights/pallas_call | solution.py:67
  86.3 3.3 %collective-permute-done.21.refs_3_ = bf16[128,2304]{1,0:T(8,128)(2,1)} collective-permute-done((bf16[128,2304]{1,0:T(8,128)(2,1)}, bf16[128,2304]{1,0:T(8,128)(2,1)}, u32[]{:S(2)}, u32[]{:S(2)}) %collective-permute-start.21) | collective-permute-done | bytes 589856 | tf_op jit(solution)/shard_map/ppermute | solution.py:30
  89.6 0.5 collective-permute-start.24
  90.1 0.5 collective-permute-start.7
  90.6 1.8 %collective-permute-done.23.refs_5_ = bf16[128,2304]{1,0:T(8,128)(2,1)S(1)} collective-permute-done((bf16[128,2304]{1,0:T(8,128)(2,1)S(1)}, bf16[128,2304]{1,0:T(8,128)(2,1)S(1)}, u32[]{:S(2)}, u32[]{:S(2)}) %collective-permute-start.23) | collective-permute-done | bytes 589856 | tf_op jit(solution)/shard_map/ppermute | solution.py:30
  92.7 1.1 collective-permute-done.25.refs_7_
  93.8 0.8 copy-done.9
  94.6 8.9 %feed_grad.1 = (f32[2,120,768]{2,1,0:T(8,128)}, bf16[2,120,768]{2,1,0:T(8,128)(2,1)S(1)}, f32[2,96,768]{2,1,0:T(8,128)}, bf16[2,96,768]{2,1,0:T(8,128)(2,1)S(1)}) custom-call(bf16[128,2304]{1,0:T(8,128)(2,1)} %get-tuple-element.129.refs_0_, bf16[128,2304]{1,0:T(8,128)(2,1)} %collective-permute-done.19.refs_1_, bf16[128,2304]{1,0:T(8,128)(2,1)} %copy-done.6, ...), custom_call_target="tpu_custom_call" | custom-call | flops 8000000000 | tf_op jit(solution)/shard_map/feed_grad/pallas_call | solution.py:67
  103.5 1.4 collective-permute-start.26
  104.9 2.4 %collective-permute-start.27 = (bf16[2,96,768]{2,1,0:T(8,128)(2,1)S(1)}, bf16[2,96,768]{2,1,0:T(8,128)(2,1)S(1)}, u32[]{:S(2)}, u32[]{:S(2)}) collective-permute-start(bf16[2,96,768]{2,1,0:T(8,128)(2,1)S(1)} %get-tuple-element.144), channel_id=1, source_target_pairs={{0,16},{4,20},{8,24},{12,28},{16,0},{20,4},{24,8},{28,12},{1,17},{... | collective-permute-start | bytes 884744 | tf_op jit(solution)/shard_map/ppermute | solution.py:30
  107.3 0.7 copy-done.11
  108.0 0.7 copy-done.12
  108.7 5.1 %input_grad.1 = (f32[128,768]{1,0:T(8,128)}, f32[32,768]{1,0:T(8,128)S(1)}, bf16[8,32,288]{2,1,0:T(8,128)(2,1)}) custom-call(bf16[8,384,128]{2,1,0:T(8,128)(2,1)S(1)} %all-to-all-done.1.back_ref, f32[128,768]{1,0:T(8,128)} %get-tuple-element.115.dr1_in, bf16[768,2304]{1,0:T(8,128)(2,1)} %qkv_in.3, f32[16,128]{1,0:T(8,128)S(1)} %get-tuple-element.116.sums_ref, ...), custom_call_target="tpu_custom_call" | custom-call | flops 5000000000 | tf_op jit(solution)/shard_map/input_grad/pallas_call | solution.py:67
  113.7 0.7 collective-permute-start.17
  114.4 4.0 %collective-permute-done.17.refs_6_ = f32[32,768]{1,0:T(8,128)S(1)} collective-permute-done((f32[32,768]{1,0:T(8,128)S(1)}, f32[32,768]{1,0:T(8,128)S(1)}, u32[]{:S(2)}, u32[]{:S(2)}) %collective-permute-start.17) | collective-permute-done | bytes 98336 | tf_op jit(solution)/shard_map/ppermute | solution.py:30
  118.4 4.0 %all-to-all-start.2 = ((bf16[8,32,288]{2,1,0:T(8,128)(2,1)}), bf16[8,32,288]{2,1,0:T(8,128)(2,1)S(1)}, u32[]{:S(2)}, u32[]{:S(2)}) async-start(bf16[8,32,288]{2,1,0:T(8,128)(2,1)} %get-tuple-element.122), calls=%async_computation.2 | async-start | bytes 393216 | tf_op jit(solution)/shard_map/all_to_all | solution.py:1085
  122.5 0.7 copy-done.10
  123.2 1.6 %combine_half.1 = (bf16[120,768]{1,0:T(8,128)(2,1)S(1)}, bf16[96,768]{1,0:T(8,128)(2,1)S(1)}) custom-call(f32[2,120,768]{2,1,0:T(8,128)} %get-tuple-element.139.up_in, f32[2,96,768]{2,1,0:T(8,128)} %get-tuple-element.140.down_in, bf16[2,120,768]{2,1,0:T(8,128)(2,1)} %collective-permute-done.26.up_got_in, bf16[2,96,768]{2,1,0:T(8,128)(2,1)} %copy-done.10), custom_call_target="tpu_custom_call" | custom-call | flops 1000000000 | tf_op jit(solution)/shard_map/combine_half/pallas_call | solution.py:67
  124.7 3.0 %collective-permute-start.28 = (bf16[120,768]{1,0:T(8,128)(2,1)S(1)}, bf16[120,768]{1,0:T(8,128)(2,1)S(1)}, u32[]{:S(2)}, u32[]{:S(2)}) collective-permute-start(bf16[120,768]{1,0:T(8,128)(2,1)S(1)} %get-tuple-element.147), channel_id=1, source_target_pairs={{0,16},{4,20},{8,24},{12,28},{16,0},{20,4},{24,8},{28,12},{1,17},{... | collective-permute-start | bytes 552968 | tf_op jit(solution)/shard_map/ppermute | solution.py:30
  127.7 1.5 collective-permute-start.29
  129.2 0.6 collective-permute-start.14
  129.8 3.2 %collective-permute-done.14.refs_2_ = bf16[16,768]{1,0:T(8,128)(2,1)S(1)} collective-permute-done((bf16[16,768]{1,0:T(8,128)(2,1)S(1)}, bf16[16,768]{1,0:T(8,128)(2,1)S(1)}, u32[]{:S(2)}, u32[]{:S(2)}) %collective-permute-start.14) | collective-permute-done | bytes 24608 | tf_op jit(solution)/shard_map/ppermute | solution.py:30
  133.0 1.2 collective-permute-done.15.refs_3_
  134.2 0.6 copy-done.15
  134.9 1.9 %time_grad.1 = (f32[96,768]{1,0:T(8,128)}, f32[4,96]{1,0:T(4,128)S(1)}, f32[2,96]{1,0:T(2,128)S(1)}, f32[1,384]{1,0:T(1,128)S(1)}) custom-call(bf16[16,768]{1,0:T(8,128)(2,1)} %copy-done.5, bf16[16,768]{1,0:T(8,128)(2,1)} %copy-done.14, bf16[16,768]{1,0:T(8,128)(2,1)} %copy-done.13, bf16[16,768]{1,0:T(8,128)(2,1)} %copy-done.15, ...), custom_call_target="tpu_custom_call" | custom-call | flops 1000000000 | tf_op jit(solution)/shard_map/time_grad/pallas_call | solution.py:67
  136.8 0.7 collective-permute-start.11
  137.5 1.0 collective-permute-done.28.up_last_ref
  138.5 1.3 combine_all.1.a_ref
  139.8 0.7 collective-permute-start.30
  140.5 0.6 fusion.5
  141.1 0.6 reduce
  141.7 3.0 %collective-permute-done.11.c_ref = bf16[8,32,288]{2,1,0:T(8,128)(2,1)S(1)} collective-permute-done((bf16[8,32,288]{2,1,0:T(8,128)(2,1)S(1)}, bf16[8,32,288]{2,1,0:T(8,128)(2,1)S(1)}, u32[]{:S(2)}, u32[]{:S(2)}) %collective-permute-start.11) | collective-permute-done | bytes 147488 | tf_op jit(solution)/shard_map/ppermute | solution.py:30
  144.6 0.5 slice_bitcast_fusion
  145.1 0.5 collective-permute-start.31
  145.7 0.4 collective-permute-done.12.d_ref
  146.1 1.3 finish_heads.1
  147.3 3.6 %collective-permute-done.30.c_ref = bf16[216,768]{1,0:T(8,128)(2,1)S(1)} collective-permute-done((bf16[216,768]{1,0:T(8,128)(2,1)S(1)}, bf16[216,768]{1,0:T(8,128)(2,1)S(1)}, u32[]{:S(2)}, u32[]{:S(2)}) %collective-permute-start.30) | collective-permute-done | bytes 331808 | tf_op jit(solution)/shard_map/ppermute | solution.py:30
  151.0 1.6 %collective-permute-done.32.d_ref = bf16[216,768]{1,0:T(8,128)(2,1)S(1)} collective-permute-done((bf16[216,768]{1,0:T(8,128)(2,1)S(1)}, bf16[216,768]{1,0:T(8,128)(2,1)S(1)}, u32[]{:S(2)}, u32[]{:S(2)}) %collective-permute-start.32) | collective-permute-done | bytes 331808 | tf_op jit(solution)/shard_map/ppermute | solution.py:30
  152.6 2.1 %finish_all.1 = (f32[96,3072]{1,0:T(8,128)}, f32[384,768]{1,0:T(8,128)}, f32[96,768]{1,0:T(8,128)}) custom-call(bf16[216,768]{1,0:T(8,128)(2,1)S(1)} %combine_all.1.a_ref, bf16[216,768]{1,0:T(8,128)(2,1)S(1)} %collective-permute-done.31.b_ref, bf16[216,768]{1,0:T(8,128)(2,1)S(1)} %collective-permute-done.30.c_ref, ...), custom_call_target="tpu_custom_call" | custom-call | flops 2000000000 | tf_op jit(solution)/shard_map/finish_all/pallas_call | solution.py:67
  (66 shorter events, 1.1 us)
Async XLA Ops:
  0.6 12.1 %copy-start = (bf16[768,768]{1,0:T(8,128)(2,1)S(1)}, bf16[768,768]{1,0:T(8,128)(2,1)}, u32[]{:S(2)}) copy-start(bf16[768,768]{1,0:T(8,128)(2,1)} %param.29) | copy-start | bytes 3538948
  2.4 10.7 %collective-permute-start = (bf16[136,768]{1,0:T(8,128)(2,1)S(1)}, bf16[136,768]{1,0:T(8,128)(2,1)S(1)}, u32[]{:S(2)}, u32[]{:S(2)}) collective-permute-start(bf16[136,768]{1,0:T(8,128)(2,1)S(1)} %fusion.1.refs_0_), channel_id=1, source_target_pairs={{0,4},{4,0},{8,12},{12,8},{16,20},{20,16},{24,28},{28,24},{1,5},{5... | collective-permute-start | bytes 626696 | tf_op jit(solution)/shard_map/ppermute | solution.py:30
  5.4 9.9 %collective-permute-start.5 = (bf16[136,768]{1,0:T(8,128)(2,1)S(1)}, bf16[136,768]{1,0:T(8,128)(2,1)S(1)}, u32[]{:S(2)}, u32[]{:S(2)}) collective-permute-start(bf16[136,768]{1,0:T(8,128)(2,1)S(1)} %fusion.1.refs_0_), channel_id=1, source_target_pairs={{0,24},{4,28},{8,16},{12,20},{16,8},{20,12},{24,0},{28,4},{1,25},{... | collective-permute-start | bytes 626696 | tf_op jit(solution)/shard_map/ppermute | solution.py:30
  9.0 10.3 %collective-permute-start.1 = (bf16[136,768]{1,0:T(8,128)(2,1)S(1)}, bf16[136,768]{1,0:T(8,128)(2,1)S(1)}, u32[]{:S(2)}, u32[]{:S(2)}) collective-permute-start(bf16[136,768]{1,0:T(8,128)(2,1)S(1)} %fusion.1.refs_0_), channel_id=1, source_target_pairs={{0,8},{4,12},{8,0},{12,4},{16,24},{20,28},{24,16},{28,20},{1,9},{5... | collective-permute-start | bytes 626696 | tf_op jit(solution)/shard_map/ppermute | solution.py:30
  9.0 17.5 %collective-permute-start.3 = (bf16[136,768]{1,0:T(8,128)(2,1)S(1)}, bf16[136,768]{1,0:T(8,128)(2,1)S(1)}, u32[]{:S(2)}, u32[]{:S(2)}) collective-permute-start(bf16[136,768]{1,0:T(8,128)(2,1)S(1)} %fusion.1.refs_0_), channel_id=1, source_target_pairs={{0,16},{4,20},{8,24},{12,28},{16,0},{20,4},{24,8},{28,12},{1,17},{... | collective-permute-start | bytes 626696 | tf_op jit(solution)/shard_map/ppermute | solution.py:30
  13.0 19.7 %copy-start.1 = (bf16[1,128,768]{2,1,0:T(8,128)(2,1)S(1)}, bf16[1,128,768]{2,1,0:T(8,128)(2,1)}, u32[]{:S(2)}) copy-start(bf16[1,128,768]{2,1,0:T(8,128)(2,1)} %param.16) | copy-start | bytes 589828
  13.0 19.7 %copy-start.2 = (f32[3072]{0:T(1024)S(1)}, f32[3072]{0:T(1024)}, u32[]{:S(2)}) copy-start(f32[3072]{0:T(1024)} %param.24) | copy-start | bytes 36868
  13.0 19.7 %copy-start.3 = (f32[2,768]{1,0:T(2,128)S(1)}, f32[2,768]{1,0:T(2,128)}, u32[]{:S(2)}) copy-start(f32[2,768]{1,0:T(2,128)} %refs_14_.1) | copy-start | bytes 18436
  13.0 19.7 %copy-start.4 = (f32[2,768]{1,0:T(2,128)S(1)}, f32[2,768]{1,0:T(2,128)}, u32[]{:S(2)}) copy-start(f32[2,768]{1,0:T(2,128)} %gain_ref.1) | copy-start | bytes 18436
  15.3 16.8 %collective-permute-start.6 = (bf16[136,768]{1,0:T(8,128)(2,1)S(1)}, bf16[136,768]{1,0:T(8,128)(2,1)S(1)}, u32[]{:S(2)}, u32[]{:S(2)}) collective-permute-start(bf16[136,768]{1,0:T(8,128)(2,1)S(1)} %collective-permute-done.5.refs_6_), channel_id=1, source_target_pairs={{0,4},{4,0},{8,12},{12,8},{16,20},{20,16},{24,28},{28,24},{1,5},{5... | collective-permute-start | bytes 626696 | tf_op jit(solution)/shard_map/ppermute | solution.py:30
  19.3 12.9 %collective-permute-start.2 = (bf16[136,768]{1,0:T(8,128)(2,1)S(1)}, bf16[136,768]{1,0:T(8,128)(2,1)S(1)}, u32[]{:S(2)}, u32[]{:S(2)}) collective-permute-start(bf16[136,768]{1,0:T(8,128)(2,1)S(1)} %collective-permute-done.1.refs_2_), channel_id=1, source_target_pairs={{0,4},{4,0},{8,12},{12,8},{16,20},{20,16},{24,28},{28,24},{1,5},{5... | collective-permute-start | bytes 626696 | tf_op jit(solution)/shard_map/ppermute | solution.py:30
  26.5 6.2 %collective-permute-start.4 = (bf16[136,768]{1,0:T(8,128)(2,1)S(1)}, bf16[136,768]{1,0:T(8,128)(2,1)S(1)}, u32[]{:S(2)}, u32[]{:S(2)}) collective-permute-start(bf16[136,768]{1,0:T(8,128)(2,1)S(1)} %collective-permute-done.3.refs_4_), channel_id=1, source_target_pairs={{0,4},{4,0},{8,12},{12,8},{16,20},{20,16},{24,28},{28,24},{1,5},{5... | collective-permute-start | bytes 626696 | tf_op jit(solution)/shard_map/ppermute | solution.py:30
  50.8 13.7 %all-to-all-start = ((bf16[8,176,128]{2,1,0:T(8,128)(2,1)}), bf16[8,176,128]{2,1,0:T(8,128)(2,1)S(1)}, u32[]{:S(2)}, u32[]{:S(2)}) async-start(bf16[8,176,128]{2,1,0:T(8,128)(2,1)} %get-tuple-element.113), calls=%async_computation | async-start | bytes 720896 | tf_op jit(solution)/shard_map/all_to_all | solution.py:1033
  55.5 30.8 %collective-permute-start.20 = (bf16[128,2304]{1,0:T(8,128)(2,1)}, bf16[128,2304]{1,0:T(8,128)(2,1)S(1)}, u32[]{:S(2)}, u32[]{:S(2)}) collective-permute-start(bf16[128,2304]{1,0:T(8,128)(2,1)} %get-tuple-element.130), channel_id=1, source_target_pairs={{0,2},{1,3},{2,0},{3,1},{4,6},{5,7},{6,4},{7,5},{8,10},{9,11},{10,... | collective-permute-start | bytes 1769480 | tf_op jit(solution)/shard_map/ppermute | solution.py:30
  57.0 32.6 %collective-permute-start.21 = (bf16[128,2304]{1,0:T(8,128)(2,1)}, bf16[128,2304]{1,0:T(8,128)(2,1)}, u32[]{:S(2)}, u32[]{:S(2)}) collective-permute-start(bf16[128,2304]{1,0:T(8,128)(2,1)} %get-tuple-element.131), channel_id=1, source_target_pairs={{0,4},{4,0},{8,12},{12,8},{16,20},{20,16},{24,28},{28,24},{1,5},{5... | collective-permute-start | bytes 1769480 | tf_op jit(solution)/shard_map/ppermute | solution.py:30
  59.0 30.6 %collective-permute-start.22 = (bf16[128,2304]{1,0:T(8,128)(2,1)}, bf16[128,2304]{1,0:T(8,128)(2,1)}, u32[]{:S(2)}, u32[]{:S(2)}) collective-permute-start(bf16[128,2304]{1,0:T(8,128)(2,1)} %get-tuple-element.132), channel_id=1, source_target_pairs={{0,6},{1,7},{2,4},{3,5},{4,2},{5,3},{6,0},{7,1},{8,14},{9,15},{10,... | collective-permute-start | bytes 1769480 | tf_op jit(solution)/shard_map/ppermute | solution.py:808
  59.0 31.6 %collective-permute-start.19 = (bf16[128,2304]{1,0:T(8,128)(2,1)}, bf16[128,2304]{1,0:T(8,128)(2,1)}, u32[]{:S(2)}, u32[]{:S(2)}) collective-permute-start(bf16[128,2304]{1,0:T(8,128)(2,1)} %get-tuple-element.129.refs_0_), channel_id=1, source_target_pairs={{0,1},{1,0},{2,3},{3,2},{4,5},{5,4},{6,7},{7,6},{8,9},{9,8},{10,11... | collective-permute-start | bytes 1769480 | tf_op jit(solution)/shard_map/ppermute | solution.py:30
  76.7 31.9 %all-to-all-start.1 = ((bf16[8,384,128]{2,1,0:T(8,128)(2,1)}), bf16[8,384,128]{2,1,0:T(8,128)(2,1)S(1)}, u32[]{:S(2)}, u32[]{:S(2)}) async-start(bf16[8,384,128]{2,1,0:T(8,128)(2,1)} %get-tuple-element.114), calls=%async_computation.1 | async-start | bytes 1572864 | tf_op jit(solution)/shard_map/all_to_all | solution.py:1066
  86.3 7.5 %copy-start.6 = (bf16[128,2304]{1,0:T(8,128)(2,1)}, bf16[128,2304]{1,0:T(8,128)(2,1)S(1)}, u32[]{:S(2)}) copy-start(bf16[128,2304]{1,0:T(8,128)(2,1)S(1)} %collective-permute-done.20.refs_2_) | copy-start | bytes 1769476
  89.6 2.8 %collective-permute-start.23 = (bf16[128,2304]{1,0:T(8,128)(2,1)S(1)}, bf16[128,2304]{1,0:T(8,128)(2,1)S(1)}, u32[]{:S(2)}, u32[]{:S(2)}) collective-permute-start(bf16[128,2304]{1,0:T(8,128)(2,1)S(1)} %collective-permute-done.20.refs_2_), channel_id=1, source_target_pairs={{0,1},{1,0},{2,3},{3,2},{4,5},{5,4},{6,7},{7,6},{8,9},{9,8},{10,11... | collective-permute-start | bytes 1769480 | tf_op jit(solution)/shard_map/ppermute | solution.py:30
  89.6 3.1 %collective-permute-start.24 = (bf16[128,2304]{1,0:T(8,128)(2,1)}, bf16[128,2304]{1,0:T(8,128)(2,1)S(1)}, u32[]{:S(2)}, u32[]{:S(2)}) collective-permute-start(bf16[128,2304]{1,0:T(8,128)(2,1)} %collective-permute-done.21.refs_3_), channel_id=1, source_target_pairs={{0,1},{1,0},{2,3},{3,2},{4,5},{5,4},{6,7},{7,6},{8,9},{9,8},{10,11... | collective-permute-start | bytes 1769480 | tf_op jit(solution)/shard_map/ppermute | solution.py:30
  90.1 3.7 %collective-permute-start.25 = (bf16[128,2304]{1,0:T(8,128)(2,1)}, bf16[128,2304]{1,0:T(8,128)(2,1)S(1)}, u32[]{:S(2)}, u32[]{:S(2)}) collective-permute-start(bf16[128,2304]{1,0:T(8,128)(2,1)} %collective-permute-done.22.refs_4_), channel_id=1, source_target_pairs={{0,1},{1,0},{2,3},{3,2},{4,5},{5,4},{6,7},{7,6},{8,9},{9,8},{10,11... | collective-permute-start | bytes 1769480 | tf_op jit(solution)/shard_map/ppermute | solution.py:30
  90.1 17.2 %collective-permute-start.7 = (bf16[8,32,288]{2,1,0:T(8,128)(2,1)S(1)}, bf16[8,32,288]{2,1,0:T(8,128)(2,1)S(1)}, u32[]{:S(2)}, u32[]{:S(2)}) collective-permute-start(bf16[8,32,288]{2,1,0:T(8,128)(2,1)S(1)} %get-tuple-element.118), channel_id=1, source_target_pairs={{0,1},{1,0},{2,3},{3,2},{4,5},{5,4},{6,7},{7,6},{8,9},{9,8},{10,11... | collective-permute-start | bytes 442376 | tf_op jit(solution)/shard_map/ppermute | solution.py:30
  90.6 16.7 %collective-permute-start.8 = (bf16[8,32,288]{2,1,0:T(8,128)(2,1)S(1)}, bf16[8,32,288]{2,1,0:T(8,128)(2,1)S(1)}, u32[]{:S(2)}, u32[]{:S(2)}) collective-permute-start(bf16[8,32,288]{2,1,0:T(8,128)(2,1)S(1)} %get-tuple-element.119), channel_id=1, source_target_pairs={{0,2},{1,3},{2,0},{3,1},{4,6},{5,7},{6,4},{7,5},{8,10},{9,11},{10,... | collective-permute-start | bytes 442376 | tf_op jit(solution)/shard_map/ppermute | solution.py:30
  92.4 1.4 copy-start.7
  92.4 16.2 %collective-permute-start.9 = (bf16[8,32,288]{2,1,0:T(8,128)(2,1)S(1)}, bf16[8,32,288]{2,1,0:T(8,128)(2,1)}, u32[]{:S(2)}, u32[]{:S(2)}) collective-permute-start(bf16[8,32,288]{2,1,0:T(8,128)(2,1)S(1)} %get-tuple-element.120), channel_id=1, source_target_pairs={{0,3},{1,2},{2,1},{3,0},{4,7},{5,6},{6,5},{7,4},{8,11},{9,10},{10,... | collective-permute-start | bytes 442376 | tf_op jit(solution)/shard_map/ppermute | solution.py:30
  92.7 1.1 copy-start.8
  93.8 0.8 copy-start.9
  103.5 18.9 %collective-permute-start.26 = (bf16[2,120,768]{2,1,0:T(8,128)(2,1)S(1)}, bf16[2,120,768]{2,1,0:T(8,128)(2,1)}, u32[]{:S(2)}, u32[]{:S(2)}) collective-permute-start(bf16[2,120,768]{2,1,0:T(8,128)(2,1)S(1)} %get-tuple-element.143), channel_id=1, source_target_pairs={{0,8},{4,12},{8,0},{12,4},{16,24},{20,28},{24,16},{28,20},{1,9},{5... | collective-permute-start | bytes 1105928 | tf_op jit(solution)/shard_map/ppermute | solution.py:30
  104.9 17.5 %collective-permute-start.27 = (bf16[2,96,768]{2,1,0:T(8,128)(2,1)S(1)}, bf16[2,96,768]{2,1,0:T(8,128)(2,1)S(1)}, u32[]{:S(2)}, u32[]{:S(2)}) collective-permute-start(bf16[2,96,768]{2,1,0:T(8,128)(2,1)S(1)} %get-tuple-element.144), channel_id=1, source_target_pairs={{0,16},{4,20},{8,24},{12,28},{16,0},{20,4},{24,8},{28,12},{1,17},{... | collective-permute-start | bytes 884744 | tf_op jit(solution)/shard_map/ppermute | solution.py:30
  107.3 0.7 copy-start.11
  108.0 0.7 copy-start.12
  113.7 4.7 %collective-permute-start.17 = (f32[32,768]{1,0:T(8,128)S(1)}, f32[32,768]{1,0:T(8,128)S(1)}, u32[]{:S(2)}, u32[]{:S(2)}) collective-permute-start(f32[32,768]{1,0:T(8,128)S(1)} %get-tuple-element.125.refs_4_), channel_id=1, source_target_pairs={{0,2},{1,3},{2,0},{3,1},{4,6},{5,7},{6,4},{7,5},{8,10},{9,11},{10,... | collective-permute-start | bytes 294920 | tf_op jit(solution)/shard_map/ppermute | solution.py:30
  114.4 8.1 %collective-permute-start.16 = (f32[32,768]{1,0:T(8,128)S(1)}, f32[32,768]{1,0:T(8,128)S(1)}, u32[]{:S(2)}, u32[]{:S(2)}) collective-permute-start(f32[32,768]{1,0:T(8,128)S(1)} %get-tuple-element.125.refs_4_), channel_id=1, source_target_pairs={{0,1},{1,0},{2,3},{3,2},{4,5},{5,4},{6,7},{7,6},{8,9},{9,8},{10,11... | collective-permute-start | bytes 294920 | tf_op jit(solution)/shard_map/ppermute | solution.py:30
  118.4 4.1 %collective-permute-start.18 = (f32[32,768]{1,0:T(8,128)S(1)}, f32[32,768]{1,0:T(8,128)S(1)}, u32[]{:S(2)}, u32[]{:S(2)}) collective-permute-start(f32[32,768]{1,0:T(8,128)S(1)} %collective-permute-done.17.refs_6_), channel_id=1, source_target_pairs={{0,1},{1,0},{2,3},{3,2},{4,5},{5,4},{6,7},{7,6},{8,9},{9,8},{10,11... | collective-permute-start | bytes 294920 | tf_op jit(solution)/shard_map/ppermute | solution.py:30
  118.4 18.4 %all-to-all-start.2 = ((bf16[8,32,288]{2,1,0:T(8,128)(2,1)}), bf16[8,32,288]{2,1,0:T(8,128)(2,1)S(1)}, u32[]{:S(2)}, u32[]{:S(2)}) async-start(bf16[8,32,288]{2,1,0:T(8,128)(2,1)} %get-tuple-element.122), calls=%async_computation.2 | async-start | bytes 393216 | tf_op jit(solution)/shard_map/all_to_all | solution.py:1085
  122.5 0.7 copy-start.10
  124.7 13.7 %collective-permute-start.28 = (bf16[120,768]{1,0:T(8,128)(2,1)S(1)}, bf16[120,768]{1,0:T(8,128)(2,1)S(1)}, u32[]{:S(2)}, u32[]{:S(2)}) collective-permute-start(bf16[120,768]{1,0:T(8,128)(2,1)S(1)} %get-tuple-element.147), channel_id=1, source_target_pairs={{0,16},{4,20},{8,24},{12,28},{16,0},{20,4},{24,8},{28,12},{1,17},{... | collective-permute-start | bytes 552968 | tf_op jit(solution)/shard_map/ppermute | solution.py:30
  127.7 9.8 %collective-permute-start.29 = (bf16[96,768]{1,0:T(8,128)(2,1)S(1)}, bf16[96,768]{1,0:T(8,128)(2,1)S(1)}, u32[]{:S(2)}, u32[]{:S(2)}) collective-permute-start(bf16[96,768]{1,0:T(8,128)(2,1)S(1)} %get-tuple-element.148), channel_id=1, source_target_pairs={{0,8},{4,12},{8,0},{12,4},{16,24},{20,28},{24,16},{28,20},{1,9},{5... | collective-permute-start | bytes 442376 | tf_op jit(solution)/shard_map/ppermute | solution.py:30
  129.2 5.0 %copy-start.5 = (bf16[16,768]{1,0:T(8,128)(2,1)}, bf16[16,768]{1,0:T(8,128)(2,1)S(1)}, u32[]{:S(2)}) copy-start(bf16[16,768]{1,0:T(8,128)(2,1)S(1)} %pad_maximum_fusion.refs_0_) | copy-start | bytes 73732
  129.2 3.8 %collective-permute-start.14 = (bf16[16,768]{1,0:T(8,128)(2,1)S(1)}, bf16[16,768]{1,0:T(8,128)(2,1)S(1)}, u32[]{:S(2)}, u32[]{:S(2)}) collective-permute-start(bf16[16,768]{1,0:T(8,128)(2,1)S(1)} %pad_maximum_fusion.refs_0_), channel_id=1, source_target_pairs={{0,2},{1,3},{2,0},{3,1},{4,6},{5,7},{6,4},{7,5},{8,10},{9,11},{10,... | collective-permute-start | bytes 73736 | tf_op jit(solution)/shard_map/ppermute | solution.py:30
  129.8 3.2 %collective-permute-start.13 = (bf16[16,768]{1,0:T(8,128)(2,1)S(1)}, bf16[16,768]{1,0:T(8,128)(2,1)S(1)}, u32[]{:S(2)}, u32[]{:S(2)}) collective-permute-start(bf16[16,768]{1,0:T(8,128)(2,1)S(1)} %pad_maximum_fusion.refs_0_), channel_id=1, source_target_pairs={{0,1},{1,0},{2,3},{3,2},{4,5},{5,4},{6,7},{7,6},{8,9},{9,8},{10,11... | collective-permute-start | bytes 73736 | tf_op jit(solution)/shard_map/ppermute | solution.py:30
  133.0 1.2 copy-start.13
  133.0 1.2 collective-permute-start.15
  133.0 1.2 copy-start.14
  134.2 0.6 copy-start.15
  136.8 7.8 %collective-permute-start.11 = (bf16[8,32,288]{2,1,0:T(8,128)(2,1)S(1)}, bf16[8,32,288]{2,1,0:T(8,128)(2,1)S(1)}, u32[]{:S(2)}, u32[]{:S(2)}) collective-permute-start(bf16[8,32,288]{2,1,0:T(8,128)(2,1)S(1)} %all-to-all-done.2.a_ref), channel_id=1, source_target_pairs={{0,2},{1,3},{2,0},{3,1},{4,6},{5,7},{6,4},{7,5},{8,10},{9,11},{10,... | collective-permute-start | bytes 442376 | tf_op jit(solution)/shard_map/ppermute | solution.py:30
  139.8 11.2 %collective-permute-start.30 = (bf16[216,768]{1,0:T(8,128)(2,1)S(1)}, bf16[216,768]{1,0:T(8,128)(2,1)S(1)}, u32[]{:S(2)}, u32[]{:S(2)}) collective-permute-start(bf16[216,768]{1,0:T(8,128)(2,1)S(1)} %combine_all.1.a_ref), channel_id=1, source_target_pairs={{0,2},{1,3},{2,0},{3,1},{4,6},{5,7},{6,4},{7,5},{8,10},{9,11},{10,... | collective-permute-start | bytes 995336 | tf_op jit(solution)/shard_map/ppermute | solution.py:30
  141.7 4.0 %collective-permute-start.10 = (bf16[8,32,288]{2,1,0:T(8,128)(2,1)S(1)}, bf16[8,32,288]{2,1,0:T(8,128)(2,1)S(1)}, u32[]{:S(2)}, u32[]{:S(2)}) collective-permute-start(bf16[8,32,288]{2,1,0:T(8,128)(2,1)S(1)} %all-to-all-done.2.a_ref), channel_id=1, source_target_pairs={{0,1},{1,0},{2,3},{3,2},{4,5},{5,4},{6,7},{7,6},{8,9},{9,8},{10,11... | collective-permute-start | bytes 442376 | tf_op jit(solution)/shard_map/ppermute | solution.py:30
  144.6 1.4 collective-permute-start.12
  145.1 5.8 %collective-permute-start.31 = (bf16[216,768]{1,0:T(8,128)(2,1)S(1)}, bf16[216,768]{1,0:T(8,128)(2,1)S(1)}, u32[]{:S(2)}, u32[]{:S(2)}) collective-permute-start(bf16[216,768]{1,0:T(8,128)(2,1)S(1)} %combine_all.1.a_ref), channel_id=1, source_target_pairs={{0,1},{1,0},{2,3},{3,2},{4,5},{5,4},{6,7},{7,6},{8,9},{9,8},{10,11... | collective-permute-start | bytes 995336 | tf_op jit(solution)/shard_map/ppermute | solution.py:30
  151.0 1.6 %collective-permute-start.32 = (bf16[216,768]{1,0:T(8,128)(2,1)S(1)}, bf16[216,768]{1,0:T(8,128)(2,1)S(1)}, u32[]{:S(2)}, u32[]{:S(2)}) collective-permute-start(bf16[216,768]{1,0:T(8,128)(2,1)S(1)} %collective-permute-done.30.c_ref), channel_id=1, source_target_pairs={{0,1},{1,0},{2,3},{3,2},{4,5},{5,4},{6,7},{7,6},{8,9},{9,8},{10,11... | collective-permute-start | bytes 995336 | tf_op jit(solution)/shard_map/ppermute | solution.py:30

commit v4 on v3

--- a/solution.py
+++ b/solution.py
@@ -259,7 +259,7 @@
             top = jnp.max(scores, axis=-1, keepdims=True)
             weights = jnp.exp(scores - top)
             summed = jnp.sum(weights, axis=-1, keepdims=True)
-            halves.append(nn(weights.astype(BF), v_ref[:, cols]) / summed)
+            halves.append(nn(weights.astype(BF), v_ref[:, cols]) * (1.0 / summed))
             lse = jnp.where(lane == 2 * pair + half, top + jnp.log(summed), lse)
         attn_ref[:, cols] = jnp.where(first, halves[0], halves[1])
     lse_ref[...] = lse

time: 155 us -> 155 us (level)
  no operation moved by 1% of the time
where the time goes in v4:
time: 155 us
  Pallas kernels  66.7 us (43%)
  waiting for transfers between devices  39 us (25%)
  starting transfers between devices  38 us (25%)
  local copies, waits for them, and re-layouts  6.68 us (4%)
  other arithmetic  3.13 us (2%)
    pallas_call x13, Pallas kernels, call(): pl.pallas_call(kernel, out_shape=tuple(((pltpu.HBM if FAR in one else plt...  66.7 us
    ppermute x32, waiting for transfers between devices, swap(): lax.ppermute(block, axis, [(i, i ^ bit) for i in range(lax.axis_size(axis...  37.5 us
    ppermute x32, starting transfers between devices, swap(): lax.ppermute(block, axis, [(i, i ^ bit) for i in range(lax.axis_size(axis...  24.7 us
    all_to_all x1, starting transfers between devices, body(): arrived = lax.all_to_all(gate('DA', packed), 'seq', 0, 0, tiled=True)  4.71 us
    all_to_all x1, starting transfers between devices, body(): back = lax.all_to_all(gate('BACK', back), 'seq', 0, 0, tiled=True)  4.57 us
    all_to_all x1, starting transfers between devices, body(): spread = lax.all_to_all(gate('GA2A', mine[0]), 'seq', 0, 0, tiled=True)  4.03 us
    unnamed x32, local copies, waits for them, and re-layouts  3.52 us
  transfers between devices with their start and end apart: 36, of which 17 were waited for; matrix products, arithmetic and copies ran while one was open for 3% of the time, Pallas kernels for 30%

profile of v4, /device:TPU:0, one launch (start us, length us, event | category | flops | bytes accessed | tf_op | source)
XLA Modules:
  0.0 154.7 jit_solution(6768014121540193759)
XLA Ops:
  0.7 0.8 convert_element_type.16
  1.4 0.9 fusion.1.refs_0_
  2.4 3.0 %collective-permute-start = (bf16[136,768]{1,0:T(8,128)(2,1)S(1)}, bf16[136,768]{1,0:T(8,128)(2,1)S(1)}, u32[]{:S(2)}, u32[]{:S(2)}) collective-permute-start(bf16[136,768]{1,0:T(8,128)(2,1)S(1)} %fusion.1.refs_0_), channel_id=1, source_target_pairs={{0,4},{4,0},{8,12},{12,8},{16,20},{20,16},{24,28},{28,24},{1,5},{5... | collective-permute-start | bytes 626696 | tf_op jit(solution)/shard_map/ppermute | solution.py:30
  5.4 3.6 %collective-permute-start.5 = (bf16[136,768]{1,0:T(8,128)(2,1)S(1)}, bf16[136,768]{1,0:T(8,128)(2,1)S(1)}, u32[]{:S(2)}, u32[]{:S(2)}) collective-permute-start(bf16[136,768]{1,0:T(8,128)(2,1)S(1)} %fusion.1.refs_0_), channel_id=1, source_target_pairs={{0,24},{4,28},{8,16},{12,20},{16,8},{20,12},{24,0},{28,4},{1,25},{... | collective-permute-start | bytes 626696 | tf_op jit(solution)/shard_map/ppermute | solution.py:30
  9.0 0.8 collective-permute-start.3
  9.8 0.7 convert_bitcast_fusion
  10.5 0.7 reshape.49.refs_10_.bias_ref
  11.2 0.7 reshape.50.refs_12_
  11.8 0.7 reshape.52.refs_19_
  13.0 2.2 %collective-permute-done.5.refs_6_ = bf16[136,768]{1,0:T(8,128)(2,1)S(1)} collective-permute-done((bf16[136,768]{1,0:T(8,128)(2,1)S(1)}, bf16[136,768]{1,0:T(8,128)(2,1)S(1)}, u32[]{:S(2)}, u32[]{:S(2)}) %collective-permute-start.5) | collective-permute-done | bytes 208928 | tf_op jit(solution)/shard_map/ppermute | solution.py:30
  15.5 3.8 %collective-permute-done.1.refs_2_ = bf16[136,768]{1,0:T(8,128)(2,1)S(1)} collective-permute-done((bf16[136,768]{1,0:T(8,128)(2,1)S(1)}, bf16[136,768]{1,0:T(8,128)(2,1)S(1)}, u32[]{:S(2)}, u32[]{:S(2)}) %collective-permute-start.1) | collective-permute-done | bytes 208928 | tf_op jit(solution)/shard_map/ppermute | solution.py:30
  19.3 0.6 collective-permute-start.2
  19.9 6.6 %collective-permute-done.3.refs_4_ = bf16[136,768]{1,0:T(8,128)(2,1)S(1)} collective-permute-done((bf16[136,768]{1,0:T(8,128)(2,1)S(1)}, bf16[136,768]{1,0:T(8,128)(2,1)S(1)}, u32[]{:S(2)}, u32[]{:S(2)}) %collective-permute-start.3) | collective-permute-done | bytes 208928 | tf_op jit(solution)/shard_map/ppermute | solution.py:30
  26.5 0.5 collective-permute-start.4
  27.0 5.1 %fetch.1 = (bf16[768,2304]{1,0:T(8,128)(2,1)S(1)}, bf16[768,768]{1,0:T(8,128)(2,1)S(1)}, bf16[768,3072]{1,0:T(8,128)(2,1)S(1)}, bf16[3072,768]{1,0:T(8,128)(2,1)S(1)}) custom-call(bf16[768,2304]{1,0:T(8,128)(2,1)} %qkv_in.3, bf16[768,768]{1,0:T(8,128)(2,1)} %refs_1_.1, bf16[768,3072]{1,0:T(8,128)(2,1)} %up_in.1, bf16[3072,768]{1,0:T(8,128)(2,1)} %refs_10_.1), custom_call_target="tpu_custom_call" | custom-call | flops 7000000000 | tf_op jit(solution)/shard_map/fetch/pallas_call | solution.py:67
  32.1 0.5 collective-permute-done.4.refs_5_
  32.7 12.3 %forward.1 = (bf16[1024,768]{1,0:T(8,128)(2,1)}, f32[128,128]{1,0:T(8,128)S(1)}, f32[128,768]{1,0:T(8,128)S(1)}, bf16[16,1024]{1,0:T(8,128)(2,1)S(1)}, f32[128,7...) custom-call(bf16[136,768]{1,0:T(8,128)(2,1)S(1)} %fusion.1.refs_0_, ...), custom_call_target="tpu_custom_call" | custom-call | flops 12000000000 | tf_op jit(solution)/shard_map/forward/pallas_call | solution.py:67
  44.9 5.9 %backward.1 = (bf16[8,176,128]{2,1,0:T(8,128)(2,1)}, f32[128,768]{1,0:T(8,128)}, f32[16,768]{1,0:T(8,128)}, bf16[16,1024]{1,0:T(8,128)(2,1)}, bf16[128,2304]{1,0...) custom-call(f32[128,768]{1,0:T(8,128)S(1)} %get-tuple-element.102.z1_ref, ...), custom_call_target="tpu_custom_call" | custom-call | flops 5000000000 | tf_op jit(solution)/shard_map/backward/pallas_call | solution.py:67
  50.8 4.7 %all-to-all-start = ((bf16[8,176,128]{2,1,0:T(8,128)(2,1)}), bf16[8,176,128]{2,1,0:T(8,128)(2,1)S(1)}, u32[]{:S(2)}, u32[]{:S(2)}) async-start(bf16[8,176,128]{2,1,0:T(8,128)(2,1)} %get-tuple-element.113), calls=%async_computation | async-start | bytes 720896 | tf_op jit(solution)/shard_map/all_to_all | solution.py:1033
  55.5 1.5 collective-permute-start.20
  57.0 2.0 %collective-permute-start.21 = (bf16[128,2304]{1,0:T(8,128)(2,1)}, bf16[128,2304]{1,0:T(8,128)(2,1)}, u32[]{:S(2)}, u32[]{:S(2)}) collective-permute-start(bf16[128,2304]{1,0:T(8,128)(2,1)} %get-tuple-element.131), channel_id=1, source_target_pairs={{0,4},{4,0},{8,12},{12,8},{16,20},{20,16},{24,28},{28,24},{1,5},{5... | collective-permute-start | bytes 1769480 | tf_op jit(solution)/shard_map/ppermute | solution.py:30
  59.0 4.1 %heads.1 = (bf16[1024,128]{1,0:T(8,128)(2,1)}, bf16[1024,128]{1,0:T(8,128)(2,1)}, bf16[1024,128]{1,0:T(8,128)(2,1)}, bf16[768,384]{1,0:T(8,128)(2,1)}) custom-call(bf16[1024,768]{1,0:T(8,128)(2,1)} %get-tuple-element.96.x_in.refs_6_, bf16[768,2304]{1,0:T(8,128)(2,1)} %qkv_in.3, f32[1,1536]{1,0:T(1,128)S(1)} %reshape.49.refs_10_.bias_ref), custom_call_target="tpu_custom_call" | custom-call | flops 3000000000 | tf_op jit(solution)/shard_map/heads/pallas_call | solution.py:67
  63.1 1.4 all-to-all-done.refs_7_
  64.6 12.2 %head_grad.1 = (bf16[8,384,128]{2,1,0:T(8,128)(2,1)}, f32[16,128]{1,0:T(8,128)S(1)}, bf16[8,32,288]{2,1,0:T(8,128)(2,1)S(1)}, bf16[8,32,288]{2,1,0:T(8,128)(2,1)...) custom-call(bf16[768,384]{1,0:T(8,128)(2,1)} %get-tuple-element.97.refs_0_, ...), custom_call_target="tpu_custom_call" | custom-call | flops 12000000000 | tf_op jit(solution)/shard_map/head_grad/pallas_call | solution.py:67
  76.7 4.6 %all-to-all-start.1 = ((bf16[8,384,128]{2,1,0:T(8,128)(2,1)}), bf16[8,384,128]{2,1,0:T(8,128)(2,1)S(1)}, u32[]{:S(2)}, u32[]{:S(2)}) async-start(bf16[8,384,128]{2,1,0:T(8,128)(2,1)} %get-tuple-element.114), calls=%async_computation.1 | async-start | bytes 1572864 | tf_op jit(solution)/shard_map/all_to_all | solution.py:1066
  81.3 5.0 %part_weights.1 = (bf16[768,768]{1,0:T(8,128)(2,1)}, f32[1,768]{1,0:T(1,128)S(1)}) custom-call(bf16[768,3072]{1,0:T(8,128)(2,1)} %up_in.1, f32[1,3072]{1,0:T(1,128)S(1)} %bitcast.16), custom_call_target="tpu_custom_call" | custom-call | flops 3000000000 | tf_op jit(solution)/shard_map/part_weights/pallas_call | solution.py:67
  86.3 3.3 %collective-permute-done.21.refs_3_ = bf16[128,2304]{1,0:T(8,128)(2,1)} collective-permute-done((bf16[128,2304]{1,0:T(8,128)(2,1)}, bf16[128,2304]{1,0:T(8,128)(2,1)}, u32[]{:S(2)}, u32[]{:S(2)}) %collective-permute-start.21) | collective-permute-done | bytes 589856 | tf_op jit(solution)/shard_map/ppermute | solution.py:30
  89.6 0.5 collective-permute-start.24
  90.1 0.5 collective-permute-start.7
  90.6 1.8 %collective-permute-done.23.refs_5_ = bf16[128,2304]{1,0:T(8,128)(2,1)S(1)} collective-permute-done((bf16[128,2304]{1,0:T(8,128)(2,1)S(1)}, bf16[128,2304]{1,0:T(8,128)(2,1)S(1)}, u32[]{:S(2)}, u32[]{:S(2)}) %collective-permute-start.23) | collective-permute-done | bytes 589856 | tf_op jit(solution)/shard_map/ppermute | solution.py:30
  92.7 1.1 collective-permute-done.25.refs_7_
  93.8 0.8 copy-done.9
  94.6 8.9 %feed_grad.1 = (f32[2,120,768]{2,1,0:T(8,128)}, bf16[2,120,768]{2,1,0:T(8,128)(2,1)S(1)}, f32[2,96,768]{2,1,0:T(8,128)}, bf16[2,96,768]{2,1,0:T(8,128)(2,1)S(1)}) custom-call(bf16[128,2304]{1,0:T(8,128)(2,1)} %get-tuple-element.129.refs_0_, bf16[128,2304]{1,0:T(8,128)(2,1)} %collective-permute-done.19.refs_1_, bf16[128,2304]{1,0:T(8,128)(2,1)} %copy-done.6, ...), custom_call_target="tpu_custom_call" | custom-call | flops 8000000000 | tf_op jit(solution)/shard_map/feed_grad/pallas_call | solution.py:67
  103.5 1.4 collective-permute-start.26
  104.9 2.4 %collective-permute-start.27 = (bf16[2,96,768]{2,1,0:T(8,128)(2,1)S(1)}, bf16[2,96,768]{2,1,0:T(8,128)(2,1)S(1)}, u32[]{:S(2)}, u32[]{:S(2)}) collective-permute-start(bf16[2,96,768]{2,1,0:T(8,128)(2,1)S(1)} %get-tuple-element.144), channel_id=1, source_target_pairs={{0,16},{4,20},{8,24},{12,28},{16,0},{20,4},{24,8},{28,12},{1,17},{... | collective-permute-start | bytes 884744 | tf_op jit(solution)/shard_map/ppermute | solution.py:30
  107.3 0.7 copy-done.11
  108.0 0.7 copy-done.12
  108.7 5.1 %input_grad.1 = (f32[128,768]{1,0:T(8,128)}, f32[32,768]{1,0:T(8,128)S(1)}, bf16[8,32,288]{2,1,0:T(8,128)(2,1)}) custom-call(bf16[8,384,128]{2,1,0:T(8,128)(2,1)S(1)} %all-to-all-done.1.back_ref, f32[128,768]{1,0:T(8,128)} %get-tuple-element.115.dr1_in, bf16[768,2304]{1,0:T(8,128)(2,1)} %qkv_in.3, f32[16,128]{1,0:T(8,128)S(1)} %get-tuple-element.116.sums_ref, ...), custom_call_target="tpu_custom_call" | custom-call | flops 5000000000 | tf_op jit(solution)/shard_map/input_grad/pallas_call | solution.py:67
  113.7 0.7 collective-permute-start.17
  114.4 4.0 %collective-permute-done.17.refs_6_ = f32[32,768]{1,0:T(8,128)S(1)} collective-permute-done((f32[32,768]{1,0:T(8,128)S(1)}, f32[32,768]{1,0:T(8,128)S(1)}, u32[]{:S(2)}, u32[]{:S(2)}) %collective-permute-start.17) | collective-permute-done | bytes 98336 | tf_op jit(solution)/shard_map/ppermute | solution.py:30
  118.4 4.0 %all-to-all-start.2 = ((bf16[8,32,288]{2,1,0:T(8,128)(2,1)}), bf16[8,32,288]{2,1,0:T(8,128)(2,1)S(1)}, u32[]{:S(2)}, u32[]{:S(2)}) async-start(bf16[8,32,288]{2,1,0:T(8,128)(2,1)} %get-tuple-element.122), calls=%async_computation.2 | async-start | bytes 393216 | tf_op jit(solution)/shard_map/all_to_all | solution.py:1085
  122.5 0.7 copy-done.10
  123.2 1.6 %combine_half.1 = (bf16[120,768]{1,0:T(8,128)(2,1)S(1)}, bf16[96,768]{1,0:T(8,128)(2,1)S(1)}) custom-call(f32[2,120,768]{2,1,0:T(8,128)} %get-tuple-element.139.up_in, f32[2,96,768]{2,1,0:T(8,128)} %get-tuple-element.140.down_in, bf16[2,120,768]{2,1,0:T(8,128)(2,1)} %collective-permute-done.26.up_got_in, bf16[2,96,768]{2,1,0:T(8,128)(2,1)} %copy-done.10), custom_call_target="tpu_custom_call" | custom-call | flops 1000000000 | tf_op jit(solution)/shard_map/combine_half/pallas_call | solution.py:67
  124.7 3.0 %collective-permute-start.28 = (bf16[120,768]{1,0:T(8,128)(2,1)S(1)}, bf16[120,768]{1,0:T(8,128)(2,1)S(1)}, u32[]{:S(2)}, u32[]{:S(2)}) collective-permute-start(bf16[120,768]{1,0:T(8,128)(2,1)S(1)} %get-tuple-element.147), channel_id=1, source_target_pairs={{0,16},{4,20},{8,24},{12,28},{16,0},{20,4},{24,8},{28,12},{1,17},{... | collective-permute-start | bytes 552968 | tf_op jit(solution)/shard_map/ppermute | solution.py:30
  127.7 1.5 collective-permute-start.29
  129.2 0.6 collective-permute-start.14
  129.8 3.2 %collective-permute-done.14.refs_2_ = bf16[16,768]{1,0:T(8,128)(2,1)S(1)} collective-permute-done((bf16[16,768]{1,0:T(8,128)(2,1)S(1)}, bf16[16,768]{1,0:T(8,128)(2,1)S(1)}, u32[]{:S(2)}, u32[]{:S(2)}) %collective-permute-start.14) | collective-permute-done | bytes 24608 | tf_op jit(solution)/shard_map/ppermute | solution.py:30
  133.0 1.2 collective-permute-done.15.refs_3_
  134.2 0.6 copy-done.15
  134.9 1.9 %time_grad.1 = (f32[96,768]{1,0:T(8,128)}, f32[4,96]{1,0:T(4,128)S(1)}, f32[2,96]{1,0:T(2,128)S(1)}, f32[1,384]{1,0:T(1,128)S(1)}) custom-call(bf16[16,768]{1,0:T(8,128)(2,1)} %copy-done.5, bf16[16,768]{1,0:T(8,128)(2,1)} %copy-done.14, bf16[16,768]{1,0:T(8,128)(2,1)} %copy-done.13, bf16[16,768]{1,0:T(8,128)(2,1)} %copy-done.15, ...), custom_call_target="tpu_custom_call" | custom-call | flops 1000000000 | tf_op jit(solution)/shard_map/time_grad/pallas_call | solution.py:67
  136.8 0.7 collective-permute-start.11
  137.5 1.0 collective-permute-done.28.up_last_ref
  138.5 1.3 combine_all.1.a_ref
  139.8 0.7 collective-permute-start.30
  140.5 0.6 fusion.5
  141.1 0.6 reduce
  141.7 3.0 %collective-permute-done.11.c_ref = bf16[8,32,288]{2,1,0:T(8,128)(2,1)S(1)} collective-permute-done((bf16[8,32,288]{2,1,0:T(8,128)(2,1)S(1)}, bf16[8,32,288]{2,1,0:T(8,128)(2,1)S(1)}, u32[]{:S(2)}, u32[]{:S(2)}) %collective-permute-start.11) | collective-permute-done | bytes 147488 | tf_op jit(solution)/shard_map/ppermute | solution.py:30
  144.6 0.5 slice_bitcast_fusion
  145.1 0.5 collective-permute-start.31
  145.7 0.4 collective-permute-done.12.d_ref
  146.1 1.3 finish_heads.1
  147.3 3.6 %collective-permute-done.30.c_ref = bf16[216,768]{1,0:T(8,128)(2,1)S(1)} collective-permute-done((bf16[216,768]{1,0:T(8,128)(2,1)S(1)}, bf16[216,768]{1,0:T(8,128)(2,1)S(1)}, u32[]{:S(2)}, u32[]{:S(2)}) %collective-permute-start.30) | collective-permute-done | bytes 331808 | tf_op jit(solution)/shard_map/ppermute | solution.py:30
  151.0 1.6 %collective-permute-done.32.d_ref = bf16[216,768]{1,0:T(8,128)(2,1)S(1)} collective-permute-done((bf16[216,768]{1,0:T(8,128)(2,1)S(1)}, bf16[216,768]{1,0:T(8,128)(2,1)S(1)}, u32[]{:S(2)}, u32[]{:S(2)}) %collective-permute-start.32) | collective-permute-done | bytes 331808 | tf_op jit(solution)/shard_map/ppermute | solution.py:30
  152.6 2.1 %finish_all.1 = (f32[96,3072]{1,0:T(8,128)}, f32[384,768]{1,0:T(8,128)}, f32[96,768]{1,0:T(8,128)}) custom-call(bf16[216,768]{1,0:T(8,128)(2,1)S(1)} %combine_all.1.a_ref, bf16[216,768]{1,0:T(8,128)(2,1)S(1)} %collective-permute-done.31.b_ref, bf16[216,768]{1,0:T(8,128)(2,1)S(1)} %collective-permute-done.30.c_ref, ...), custom_call_target="tpu_custom_call" | custom-call | flops 2000000000 | tf_op jit(solution)/shard_map/finish_all/pallas_call | solution.py:67
  (66 shorter events, 1.1 us)
Async XLA Ops:
  0.6 12.1 %copy-start = (bf16[768,768]{1,0:T(8,128)(2,1)S(1)}, bf16[768,768]{1,0:T(8,128)(2,1)}, u32[]{:S(2)}) copy-start(bf16[768,768]{1,0:T(8,128)(2,1)} %param.29) | copy-start | bytes 3538948
  2.4 10.7 %collective-permute-start = (bf16[136,768]{1,0:T(8,128)(2,1)S(1)}, bf16[136,768]{1,0:T(8,128)(2,1)S(1)}, u32[]{:S(2)}, u32[]{:S(2)}) collective-permute-start(bf16[136,768]{1,0:T(8,128)(2,1)S(1)} %fusion.1.refs_0_), channel_id=1, source_target_pairs={{0,4},{4,0},{8,12},{12,8},{16,20},{20,16},{24,28},{28,24},{1,5},{5... | collective-permute-start | bytes 626696 | tf_op jit(solution)/shard_map/ppermute | solution.py:30
  5.4 9.9 %collective-permute-start.5 = (bf16[136,768]{1,0:T(8,128)(2,1)S(1)}, bf16[136,768]{1,0:T(8,128)(2,1)S(1)}, u32[]{:S(2)}, u32[]{:S(2)}) collective-permute-start(bf16[136,768]{1,0:T(8,128)(2,1)S(1)} %fusion.1.refs_0_), channel_id=1, source_target_pairs={{0,24},{4,28},{8,16},{12,20},{16,8},{20,12},{24,0},{28,4},{1,25},{... | collective-permute-start | bytes 626696 | tf_op jit(solution)/shard_map/ppermute | solution.py:30
  9.0 10.3 %collective-permute-start.1 = (bf16[136,768]{1,0:T(8,128)(2,1)S(1)}, bf16[136,768]{1,0:T(8,128)(2,1)S(1)}, u32[]{:S(2)}, u32[]{:S(2)}) collective-permute-start(bf16[136,768]{1,0:T(8,128)(2,1)S(1)} %fusion.1.refs_0_), channel_id=1, source_target_pairs={{0,8},{4,12},{8,0},{12,4},{16,24},{20,28},{24,16},{28,20},{1,9},{5... | collective-permute-start | bytes 626696 | tf_op jit(solution)/shard_map/ppermute | solution.py:30
  9.0 17.5 %collective-permute-start.3 = (bf16[136,768]{1,0:T(8,128)(2,1)S(1)}, bf16[136,768]{1,0:T(8,128)(2,1)S(1)}, u32[]{:S(2)}, u32[]{:S(2)}) collective-permute-start(bf16[136,768]{1,0:T(8,128)(2,1)S(1)} %fusion.1.refs_0_), channel_id=1, source_target_pairs={{0,16},{4,20},{8,24},{12,28},{16,0},{20,4},{24,8},{28,12},{1,17},{... | collective-permute-start | bytes 626696 | tf_op jit(solution)/shard_map/ppermute | solution.py:30
  13.0 19.7 %copy-start.1 = (bf16[1,128,768]{2,1,0:T(8,128)(2,1)S(1)}, bf16[1,128,768]{2,1,0:T(8,128)(2,1)}, u32[]{:S(2)}) copy-start(bf16[1,128,768]{2,1,0:T(8,128)(2,1)} %param.16) | copy-start | bytes 589828
  13.0 19.7 %copy-start.2 = (f32[3072]{0:T(1024)S(1)}, f32[3072]{0:T(1024)}, u32[]{:S(2)}) copy-start(f32[3072]{0:T(1024)} %param.24) | copy-start | bytes 36868
  13.0 19.7 %copy-start.3 = (f32[2,768]{1,0:T(2,128)S(1)}, f32[2,768]{1,0:T(2,128)}, u32[]{:S(2)}) copy-start(f32[2,768]{1,0:T(2,128)} %refs_14_.1) | copy-start | bytes 18436
  13.0 19.7 %copy-start.4 = (f32[2,768]{1,0:T(2,128)S(1)}, f32[2,768]{1,0:T(2,128)}, u32[]{:S(2)}) copy-start(f32[2,768]{1,0:T(2,128)} %gain_ref.1) | copy-start | bytes 18436
  15.3 16.8 %collective-permute-start.6 = (bf16[136,768]{1,0:T(8,128)(2,1)S(1)}, bf16[136,768]{1,0:T(8,128)(2,1)S(1)}, u32[]{:S(2)}, u32[]{:S(2)}) collective-permute-start(bf16[136,768]{1,0:T(8,128)(2,1)S(1)} %collective-permute-done.5.refs_6_), channel_id=1, source_target_pairs={{0,4},{4,0},{8,12},{12,8},{16,20},{20,16},{24,28},{28,24},{1,5},{5... | collective-permute-start | bytes 626696 | tf_op jit(solution)/shard_map/ppermute | solution.py:30
  19.3 12.9 %collective-permute-start.2 = (bf16[136,768]{1,0:T(8,128)(2,1)S(1)}, bf16[136,768]{1,0:T(8,128)(2,1)S(1)}, u32[]{:S(2)}, u32[]{:S(2)}) collective-permute-start(bf16[136,768]{1,0:T(8,128)(2,1)S(1)} %collective-permute-done.1.refs_2_), channel_id=1, source_target_pairs={{0,4},{4,0},{8,12},{12,8},{16,20},{20,16},{24,28},{28,24},{1,5},{5... | collective-permute-start | bytes 626696 | tf_op jit(solution)/shard_map/ppermute | solution.py:30
  26.5 6.2 %collective-permute-start.4 = (bf16[136,768]{1,0:T(8,128)(2,1)S(1)}, bf16[136,768]{1,0:T(8,128)(2,1)S(1)}, u32[]{:S(2)}, u32[]{:S(2)}) collective-permute-start(bf16[136,768]{1,0:T(8,128)(2,1)S(1)} %collective-permute-done.3.refs_4_), channel_id=1, source_target_pairs={{0,4},{4,0},{8,12},{12,8},{16,20},{20,16},{24,28},{28,24},{1,5},{5... | collective-permute-start | bytes 626696 | tf_op jit(solution)/shard_map/ppermute | solution.py:30
  50.8 13.7 %all-to-all-start = ((bf16[8,176,128]{2,1,0:T(8,128)(2,1)}), bf16[8,176,128]{2,1,0:T(8,128)(2,1)S(1)}, u32[]{:S(2)}, u32[]{:S(2)}) async-start(bf16[8,176,128]{2,1,0:T(8,128)(2,1)} %get-tuple-element.113), calls=%async_computation | async-start | bytes 720896 | tf_op jit(solution)/shard_map/all_to_all | solution.py:1033
  55.5 30.8 %collective-permute-start.20 = (bf16[128,2304]{1,0:T(8,128)(2,1)}, bf16[128,2304]{1,0:T(8,128)(2,1)S(1)}, u32[]{:S(2)}, u32[]{:S(2)}) collective-permute-start(bf16[128,2304]{1,0:T(8,128)(2,1)} %get-tuple-element.130), channel_id=1, source_target_pairs={{0,2},{1,3},{2,0},{3,1},{4,6},{5,7},{6,4},{7,5},{8,10},{9,11},{10,... | collective-permute-start | bytes 1769480 | tf_op jit(solution)/shard_map/ppermute | solution.py:30
  57.0 32.6 %collective-permute-start.21 = (bf16[128,2304]{1,0:T(8,128)(2,1)}, bf16[128,2304]{1,0:T(8,128)(2,1)}, u32[]{:S(2)}, u32[]{:S(2)}) collective-permute-start(bf16[128,2304]{1,0:T(8,128)(2,1)} %get-tuple-element.131), channel_id=1, source_target_pairs={{0,4},{4,0},{8,12},{12,8},{16,20},{20,16},{24,28},{28,24},{1,5},{5... | collective-permute-start | bytes 1769480 | tf_op jit(solution)/shard_map/ppermute | solution.py:30
  59.0 30.6 %collective-permute-start.22 = (bf16[128,2304]{1,0:T(8,128)(2,1)}, bf16[128,2304]{1,0:T(8,128)(2,1)}, u32[]{:S(2)}, u32[]{:S(2)}) collective-permute-start(bf16[128,2304]{1,0:T(8,128)(2,1)} %get-tuple-element.132), channel_id=1, source_target_pairs={{0,6},{1,7},{2,4},{3,5},{4,2},{5,3},{6,0},{7,1},{8,14},{9,15},{10,... | collective-permute-start | bytes 1769480 | tf_op jit(solution)/shard_map/ppermute | solution.py:808
  59.0 31.6 %collective-permute-start.19 = (bf16[128,2304]{1,0:T(8,128)(2,1)}, bf16[128,2304]{1,0:T(8,128)(2,1)}, u32[]{:S(2)}, u32[]{:S(2)}) collective-permute-start(bf16[128,2304]{1,0:T(8,128)(2,1)} %get-tuple-element.129.refs_0_), channel_id=1, source_target_pairs={{0,1},{1,0},{2,3},{3,2},{4,5},{5,4},{6,7},{7,6},{8,9},{9,8},{10,11... | collective-permute-start | bytes 1769480 | tf_op jit(solution)/shard_map/ppermute | solution.py:30
  76.7 31.9 %all-to-all-start.1 = ((bf16[8,384,128]{2,1,0:T(8,128)(2,1)}), bf16[8,384,128]{2,1,0:T(8,128)(2,1)S(1)}, u32[]{:S(2)}, u32[]{:S(2)}) async-start(bf16[8,384,128]{2,1,0:T(8,128)(2,1)} %get-tuple-element.114), calls=%async_computation.1 | async-start | bytes 1572864 | tf_op jit(solution)/shard_map/all_to_all | solution.py:1066
  86.3 7.5 %copy-start.6 = (bf16[128,2304]{1,0:T(8,128)(2,1)}, bf16[128,2304]{1,0:T(8,128)(2,1)S(1)}, u32[]{:S(2)}) copy-start(bf16[128,2304]{1,0:T(8,128)(2,1)S(1)} %collective-permute-done.20.refs_2_) | copy-start | bytes 1769476
  89.6 2.8 %collective-permute-start.23 = (bf16[128,2304]{1,0:T(8,128)(2,1)S(1)}, bf16[128,2304]{1,0:T(8,128)(2,1)S(1)}, u32[]{:S(2)}, u32[]{:S(2)}) collective-permute-start(bf16[128,2304]{1,0:T(8,128)(2,1)S(1)} %collective-permute-done.20.refs_2_), channel_id=1, source_target_pairs={{0,1},{1,0},{2,3},{3,2},{4,5},{5,4},{6,7},{7,6},{8,9},{9,8},{10,11... | collective-permute-start | bytes 1769480 | tf_op jit(solution)/shard_map/ppermute | solution.py:30
  89.6 3.1 %collective-permute-start.24 = (bf16[128,2304]{1,0:T(8,128)(2,1)}, bf16[128,2304]{1,0:T(8,128)(2,1)S(1)}, u32[]{:S(2)}, u32[]{:S(2)}) collective-permute-start(bf16[128,2304]{1,0:T(8,128)(2,1)} %collective-permute-done.21.refs_3_), channel_id=1, source_target_pairs={{0,1},{1,0},{2,3},{3,2},{4,5},{5,4},{6,7},{7,6},{8,9},{9,8},{10,11... | collective-permute-start | bytes 1769480 | tf_op jit(solution)/shard_map/ppermute | solution.py:30
  90.1 3.7 %collective-permute-start.25 = (bf16[128,2304]{1,0:T(8,128)(2,1)}, bf16[128,2304]{1,0:T(8,128)(2,1)S(1)}, u32[]{:S(2)}, u32[]{:S(2)}) collective-permute-start(bf16[128,2304]{1,0:T(8,128)(2,1)} %collective-permute-done.22.refs_4_), channel_id=1, source_target_pairs={{0,1},{1,0},{2,3},{3,2},{4,5},{5,4},{6,7},{7,6},{8,9},{9,8},{10,11... | collective-permute-start | bytes 1769480 | tf_op jit(solution)/shard_map/ppermute | solution.py:30
  90.1 17.2 %collective-permute-start.7 = (bf16[8,32,288]{2,1,0:T(8,128)(2,1)S(1)}, bf16[8,32,288]{2,1,0:T(8,128)(2,1)S(1)}, u32[]{:S(2)}, u32[]{:S(2)}) collective-permute-start(bf16[8,32,288]{2,1,0:T(8,128)(2,1)S(1)} %get-tuple-element.118), channel_id=1, source_target_pairs={{0,1},{1,0},{2,3},{3,2},{4,5},{5,4},{6,7},{7,6},{8,9},{9,8},{10,11... | collective-permute-start | bytes 442376 | tf_op jit(solution)/shard_map/ppermute | solution.py:30
  90.6 16.7 %collective-permute-start.8 = (bf16[8,32,288]{2,1,0:T(8,128)(2,1)S(1)}, bf16[8,32,288]{2,1,0:T(8,128)(2,1)S(1)}, u32[]{:S(2)}, u32[]{:S(2)}) collective-permute-start(bf16[8,32,288]{2,1,0:T(8,128)(2,1)S(1)} %get-tuple-element.119), channel_id=1, source_target_pairs={{0,2},{1,3},{2,0},{3,1},{4,6},{5,7},{6,4},{7,5},{8,10},{9,11},{10,... | collective-permute-start | bytes 442376 | tf_op jit(solution)/shard_map/ppermute | solution.py:30
  92.4 1.4 copy-start.7
  92.4 16.2 %collective-permute-start.9 = (bf16[8,32,288]{2,1,0:T(8,128)(2,1)S(1)}, bf16[8,32,288]{2,1,0:T(8,128)(2,1)}, u32[]{:S(2)}, u32[]{:S(2)}) collective-permute-start(bf16[8,32,288]{2,1,0:T(8,128)(2,1)S(1)} %get-tuple-element.120), channel_id=1, source_target_pairs={{0,3},{1,2},{2,1},{3,0},{4,7},{5,6},{6,5},{7,4},{8,11},{9,10},{10,... | collective-permute-start | bytes 442376 | tf_op jit(solution)/shard_map/ppermute | solution.py:30
  92.7 1.1 copy-start.8
  93.8 0.8 copy-start.9
  103.5 18.9 %collective-permute-start.26 = (bf16[2,120,768]{2,1,0:T(8,128)(2,1)S(1)}, bf16[2,120,768]{2,1,0:T(8,128)(2,1)}, u32[]{:S(2)}, u32[]{:S(2)}) collective-permute-start(bf16[2,120,768]{2,1,0:T(8,128)(2,1)S(1)} %get-tuple-element.143), channel_id=1, source_target_pairs={{0,8},{4,12},{8,0},{12,4},{16,24},{20,28},{24,16},{28,20},{1,9},{5... | collective-permute-start | bytes 1105928 | tf_op jit(solution)/shard_map/ppermute | solution.py:30
  104.9 17.5 %collective-permute-start.27 = (bf16[2,96,768]{2,1,0:T(8,128)(2,1)S(1)}, bf16[2,96,768]{2,1,0:T(8,128)(2,1)S(1)}, u32[]{:S(2)}, u32[]{:S(2)}) collective-permute-start(bf16[2,96,768]{2,1,0:T(8,128)(2,1)S(1)} %get-tuple-element.144), channel_id=1, source_target_pairs={{0,16},{4,20},{8,24},{12,28},{16,0},{20,4},{24,8},{28,12},{1,17},{... | collective-permute-start | bytes 884744 | tf_op jit(solution)/shard_map/ppermute | solution.py:30
  107.3 0.7 copy-start.11
  108.0 0.7 copy-start.12
  113.7 4.7 %collective-permute-start.17 = (f32[32,768]{1,0:T(8,128)S(1)}, f32[32,768]{1,0:T(8,128)S(1)}, u32[]{:S(2)}, u32[]{:S(2)}) collective-permute-start(f32[32,768]{1,0:T(8,128)S(1)} %get-tuple-element.125.refs_4_), channel_id=1, source_target_pairs={{0,2},{1,3},{2,0},{3,1},{4,6},{5,7},{6,4},{7,5},{8,10},{9,11},{10,... | collective-permute-start | bytes 294920 | tf_op jit(solution)/shard_map/ppermute | solution.py:30
  114.4 8.1 %collective-permute-start.16 = (f32[32,768]{1,0:T(8,128)S(1)}, f32[32,768]{1,0:T(8,128)S(1)}, u32[]{:S(2)}, u32[]{:S(2)}) collective-permute-start(f32[32,768]{1,0:T(8,128)S(1)} %get-tuple-element.125.refs_4_), channel_id=1, source_target_pairs={{0,1},{1,0},{2,3},{3,2},{4,5},{5,4},{6,7},{7,6},{8,9},{9,8},{10,11... | collective-permute-start | bytes 294920 | tf_op jit(solution)/shard_map/ppermute | solution.py:30
  118.4 4.1 %collective-permute-start.18 = (f32[32,768]{1,0:T(8,128)S(1)}, f32[32,768]{1,0:T(8,128)S(1)}, u32[]{:S(2)}, u32[]{:S(2)}) collective-permute-start(f32[32,768]{1,0:T(8,128)S(1)} %collective-permute-done.17.refs_6_), channel_id=1, source_target_pairs={{0,1},{1,0},{2,3},{3,2},{4,5},{5,4},{6,7},{7,6},{8,9},{9,8},{10,11... | collective-permute-start | bytes 294920 | tf_op jit(solution)/shard_map/ppermute | solution.py:30
  118.4 18.4 %all-to-all-start.2 = ((bf16[8,32,288]{2,1,0:T(8,128)(2,1)}), bf16[8,32,288]{2,1,0:T(8,128)(2,1)S(1)}, u32[]{:S(2)}, u32[]{:S(2)}) async-start(bf16[8,32,288]{2,1,0:T(8,128)(2,1)} %get-tuple-element.122), calls=%async_computation.2 | async-start | bytes 393216 | tf_op jit(solution)/shard_map/all_to_all | solution.py:1085
  122.5 0.7 copy-start.10
  124.7 13.7 %collective-permute-start.28 = (bf16[120,768]{1,0:T(8,128)(2,1)S(1)}, bf16[120,768]{1,0:T(8,128)(2,1)S(1)}, u32[]{:S(2)}, u32[]{:S(2)}) collective-permute-start(bf16[120,768]{1,0:T(8,128)(2,1)S(1)} %get-tuple-element.147), channel_id=1, source_target_pairs={{0,16},{4,20},{8,24},{12,28},{16,0},{20,4},{24,8},{28,12},{1,17},{... | collective-permute-start | bytes 552968 | tf_op jit(solution)/shard_map/ppermute | solution.py:30
  127.7 9.8 %collective-permute-start.29 = (bf16[96,768]{1,0:T(8,128)(2,1)S(1)}, bf16[96,768]{1,0:T(8,128)(2,1)S(1)}, u32[]{:S(2)}, u32[]{:S(2)}) collective-permute-start(bf16[96,768]{1,0:T(8,128)(2,1)S(1)} %get-tuple-element.148), channel_id=1, source_target_pairs={{0,8},{4,12},{8,0},{12,4},{16,24},{20,28},{24,16},{28,20},{1,9},{5... | collective-permute-start | bytes 442376 | tf_op jit(solution)/shard_map/ppermute | solution.py:30
  129.2 5.0 %copy-start.5 = (bf16[16,768]{1,0:T(8,128)(2,1)}, bf16[16,768]{1,0:T(8,128)(2,1)S(1)}, u32[]{:S(2)}) copy-start(bf16[16,768]{1,0:T(8,128)(2,1)S(1)} %pad_maximum_fusion.refs_0_) | copy-start | bytes 73732
  129.2 3.8 %collective-permute-start.14 = (bf16[16,768]{1,0:T(8,128)(2,1)S(1)}, bf16[16,768]{1,0:T(8,128)(2,1)S(1)}, u32[]{:S(2)}, u32[]{:S(2)}) collective-permute-start(bf16[16,768]{1,0:T(8,128)(2,1)S(1)} %pad_maximum_fusion.refs_0_), channel_id=1, source_target_pairs={{0,2},{1,3},{2,0},{3,1},{4,6},{5,7},{6,4},{7,5},{8,10},{9,11},{10,... | collective-permute-start | bytes 73736 | tf_op jit(solution)/shard_map/ppermute | solution.py:30
  129.8 3.2 %collective-permute-start.13 = (bf16[16,768]{1,0:T(8,128)(2,1)S(1)}, bf16[16,768]{1,0:T(8,128)(2,1)S(1)}, u32[]{:S(2)}, u32[]{:S(2)}) collective-permute-start(bf16[16,768]{1,0:T(8,128)(2,1)S(1)} %pad_maximum_fusion.refs_0_), channel_id=1, source_target_pairs={{0,1},{1,0},{2,3},{3,2},{4,5},{5,4},{6,7},{7,6},{8,9},{9,8},{10,11... | collective-permute-start | bytes 73736 | tf_op jit(solution)/shard_map/ppermute | solution.py:30
  133.0 1.2 copy-start.13
  133.0 1.2 collective-permute-start.15
  133.0 1.2 copy-start.14
  134.2 0.6 copy-start.15
  136.8 7.8 %collective-permute-start.11 = (bf16[8,32,288]{2,1,0:T(8,128)(2,1)S(1)}, bf16[8,32,288]{2,1,0:T(8,128)(2,1)S(1)}, u32[]{:S(2)}, u32[]{:S(2)}) collective-permute-start(bf16[8,32,288]{2,1,0:T(8,128)(2,1)S(1)} %all-to-all-done.2.a_ref), channel_id=1, source_target_pairs={{0,2},{1,3},{2,0},{3,1},{4,6},{5,7},{6,4},{7,5},{8,10},{9,11},{10,... | collective-permute-start | bytes 442376 | tf_op jit(solution)/shard_map/ppermute | solution.py:30
  139.8 11.2 %collective-permute-start.30 = (bf16[216,768]{1,0:T(8,128)(2,1)S(1)}, bf16[216,768]{1,0:T(8,128)(2,1)S(1)}, u32[]{:S(2)}, u32[]{:S(2)}) collective-permute-start(bf16[216,768]{1,0:T(8,128)(2,1)S(1)} %combine_all.1.a_ref), channel_id=1, source_target_pairs={{0,2},{1,3},{2,0},{3,1},{4,6},{5,7},{6,4},{7,5},{8,10},{9,11},{10,... | collective-permute-start | bytes 995336 | tf_op jit(solution)/shard_map/ppermute | solution.py:30
  141.7 4.0 %collective-permute-start.10 = (bf16[8,32,288]{2,1,0:T(8,128)(2,1)S(1)}, bf16[8,32,288]{2,1,0:T(8,128)(2,1)S(1)}, u32[]{:S(2)}, u32[]{:S(2)}) collective-permute-start(bf16[8,32,288]{2,1,0:T(8,128)(2,1)S(1)} %all-to-all-done.2.a_ref), channel_id=1, source_target_pairs={{0,1},{1,0},{2,3},{3,2},{4,5},{5,4},{6,7},{7,6},{8,9},{9,8},{10,11... | collective-permute-start | bytes 442376 | tf_op jit(solution)/shard_map/ppermute | solution.py:30
  144.6 1.4 collective-permute-start.12
  145.1 5.8 %collective-permute-start.31 = (bf16[216,768]{1,0:T(8,128)(2,1)S(1)}, bf16[216,768]{1,0:T(8,128)(2,1)S(1)}, u32[]{:S(2)}, u32[]{:S(2)}) collective-permute-start(bf16[216,768]{1,0:T(8,128)(2,1)S(1)} %combine_all.1.a_ref), channel_id=1, source_target_pairs={{0,1},{1,0},{2,3},{3,2},{4,5},{5,4},{6,7},{7,6},{8,9},{9,8},{10,11... | collective-permute-start | bytes 995336 | tf_op jit(solution)/shard_map/ppermute | solution.py:30
  151.0 1.6 %collective-permute-start.32 = (bf16[216,768]{1,0:T(8,128)(2,1)S(1)}, bf16[216,768]{1,0:T(8,128)(2,1)S(1)}, u32[]{:S(2)}, u32[]{:S(2)}) collective-permute-start(bf16[216,768]{1,0:T(8,128)(2,1)S(1)} %collective-permute-done.30.c_ref), channel_id=1, source_target_pairs={{0,1},{1,0},{2,3},{3,2},{4,5},{5,4},{6,7},{7,6},{8,9},{9,8},{10,11... | collective-permute-start | bytes 995336 | tf_op jit(solution)/shard_map/ppermute | solution.py:30
